TPU v7x, 32 devices: a whole 2x2x4 slice. The times are simulated.
32 devices in a mesh: row: 4 (over z), col: 8 (over y, x, core).
Axes of the slice: x: 2, y: 2, z: 4, core: 2. Of those that a mesh axis runs over, the one named last changes fastest.
Arguments:
- picture: float32 [3, 256, 1024], P(None, 'row', 'col'), may hold values from -6 to 6
- membrane: float32 [32, 128, 1024], P('row', 'col'), may hold values from -3 to 3
- dictionary: bfloat16 [1024, 3072], replicated, may hold values from -4 to 4
- momentum: float32 [1024, 3072], P(('row', 'col')), may hold values from -5 to 5
Outputs:
- final_codes: float32 [32, 128, 1024], P('row', 'col')
- new_dictionary: float32 [1024, 3072], P(('row', 'col'))
- new_momentum: float32 [1024, 3072], P(('row', 'col'))
All inputs are finite; a program needn't handle non-finite values.
Results may differ from a plain program's by a relative error of at most 0.0032.
Values may be sent and summed in bfloat16 or wider, within the bound.
No kernel may reach another device: no remote copies, remote signals or barrier semaphores. Data moves between devices by JAX's collectives and lax.ppermute only.
A program may use at most 64 MiB of HBM per device.

v0:
```python
import functools

import jax
import jax.numpy as jnp
from jax import lax
from jax.experimental import pallas as pl
from jax.experimental.pallas import tpu as pltpu
from jax.sharding import Mesh
from jax.sharding import PartitionSpec as P


PATCH_SIDE = 32
STRIDE = 8
SWEEPS = 2
SPAN = PATCH_SIDE // STRIDE
MARGIN = SPAN - 1

THRESHOLD = 0.25
RELAXATION = 0.1
DECAY = 0.9
LEARNING = 0.25
EPSILON = 1e-05


F32 = jnp.float32
BF16 = jnp.bfloat16
VMEM = pl.BlockSpec(memory_space=pltpu.VMEM)
SMEM = pl.BlockSpec(memory_space=pltpu.SMEM)
HBM = pl.BlockSpec(memory_space=pltpu.HBM)
PARAMS = pltpu.CompilerParams(vmem_limit_bytes=24 * 1024 * 1024)


def up_to(value, step):
    return -(-value // step) * step


def shrink(potential):
    return potential - jnp.clip(potential, -THRESHOLD, THRESHOLD)


class Sizes:
    def __init__(self, site_rows, site_cols, atoms, patch_len):
        self.rows, self.cols, self.atoms, self.patch = site_rows, site_cols, atoms, patch_len
        self.cell = patch_len // (SPAN * SPAN)
        self.band = SPAN * self.cell
        self.sites = site_rows * site_cols
        self.tall = site_rows + MARGIN
        self.wide = site_cols + MARGIN
        self.wide_pad = up_to(self.wide, 8)
        self.tall_pad = up_to(self.tall, 16)
        self.lanes = up_to(self.cell, 128)
        self.rim = up_to(MARGIN * self.wide, 16)
        self.packed = up_to(self.tall * self.cols + MARGIN * self.tall_pad, 32)
        self.scale = patch_len ** (-0.5)


class Place:
    def __init__(self, where, rows_n, cols_n):
        self.row, self.col = where[0], where[1]
        self.rows_n, self.cols_n = rows_n, cols_n
        self.owner = self.row * cols_n + self.col

    def pairs(self, axis):
        at, n = (self.row, self.rows_n) if axis == 0 else (self.col, self.cols_n)
        before, after = at > 0, at < n - 1
        odd = at % 2
        return [
            (odd == 0, ((True, after), (False, before))),
            (odd == 1, ((False, before), (True, after))),
        ]


def partners(n):
    even, odd = {}, {}
    for i in range(n):
        even[i] = i ^ 1 if i ^ 1 < n else i
        other = ((i + 1) ^ 1) - 1
        odd[i] = other if 0 <= other < n else (n - 1 if i == 0 and n % 2 == 0 else i)
    if n % 2 == 0:
        odd[n - 1] = 0
    return [sorted(even.items()), sorted(odd.items())]


def reconstruct(z, place, coding, dic, pixels, tall_sum, own, ready=None):
    tall_sum[z.sites :, :] = jnp.zeros((z.tall * z.cols - z.sites, z.band), F32)
    for i in range(SPAN):
        if ready is not None:
            ready(i)
        placed = jnp.dot(
            coding, dic[:, i * z.band : (i + 1) * z.band], preferred_element_type=F32
        )
        start = i * z.cols
        if i == 0:
            tall_sum[0 : z.sites, :] = placed
        else:
            tall_sum[start : start + z.sites, :] += placed
    own[...] = jnp.zeros((z.tall, z.wide_pad, z.lanes), F32)
    own[0 : z.rows, 0 : z.cols, 0 : z.cell] = pixels[...].reshape(z.rows, z.cols, z.cell)
    for j in range(SPAN):
        part = tall_sum[:, j * z.cell : (j + 1) * z.cell].reshape(z.tall, z.cols, z.cell)
        own[:, j : j + z.cols, 0 : z.cell] -= part * z.scale

    @pl.when(place.row == place.rows_n - 1)
    def _():
        own[z.rows :] = jnp.zeros((MARGIN, z.wide_pad, z.lanes), F32)

    @pl.when(place.col == place.cols_n - 1)
    def _():
        own[:, z.cols :] = jnp.zeros((z.tall, z.wide_pad - z.cols, z.lanes), F32)


def send_sides(z, place, own, sends):
    for mine, halves in place.pairs(1):

        @pl.when(mine)
        def _(halves=halves):
            for send, (onward, _) in zip(sends, halves):
                first = z.cols if onward else 0
                for c in range(MARGIN):
                    send[c, 0 : z.tall, :] = own[:, first + c, :].astype(BF16)


def add_sides(z, place, whole, received):
    for mine, halves in place.pairs(1):
        for rim, (onward, there) in zip(received, halves):

            @pl.when(mine & there)
            def _(rim=rim, first=z.cols if onward else 0):
                for c in range(MARGIN):
                    whole[:, first + c, :] += rim[c].astype(F32)[0 : z.tall]


def is_equal(a, b):
    return (a == b).astype(F32).astype(BF16)


def cells_of(z, picture, pixels, spread):
    channels, height, width = picture.shape
    turned = picture[...].reshape(channels * height, width).T
    high = turned.astype(BF16)
    rest = turned - high.astype(F32)
    middle = rest.astype(BF16)
    spread[0:width, :] = high
    spread[width : 2 * width, :] = middle
    spread[2 * width :, :] = (rest - middle.astype(F32)).astype(BF16)

    def iota(shape, dim):
        return lax.broadcasted_iota(jnp.int32, shape, dim)

    shape = (channels * height, z.cell)
    line, entry = iota(shape, 0), iota(shape, 1)
    channel, image_row = line // height, line % height
    away = (
        (channel * STRIDE + image_row % STRIDE) * STRIDE
        + image_row // STRIDE * z.cell
        - entry // STRIDE * STRIDE
    )
    shape = (width, z.cell)
    mine = (iota(shape, 0) % STRIDE == iota(shape, 1) % STRIDE).astype(F32)
    for i in range(z.rows):
        moved = jnp.dot(
            spread[...], is_equal(away, i * z.cell), preferred_element_type=F32
        )
        whole = (moved[0:width] + moved[width : 2 * width]) + moved[2 * width :]
        whole = (whole * mine).reshape(z.cols, STRIDE, z.cell)
        pixels[i * z.cols : (i + 1) * z.cols, :] = jnp.sum(whole, axis=1)


def first_kernel(
    z, grid, where, membrane, picture, source, own, *rest
):
    (*sends, pixels, dic, potential, atoms, tall_sum, spread, drawing, sems) = rest
    place = Place(where, *grid)
    early = [
        pltpu.make_async_copy(picture, drawing, sems.at[SPAN]),
        pltpu.make_async_copy(membrane, potential, sems.at[SPAN + 1]),
    ]
    copies = [
        pltpu.make_async_copy(
            source.at[:, i * z.band : (i + 1) * z.band],
            dic.at[:, i * z.band : (i + 1) * z.band],
            sems.at[i],
        )
        for i in range(SPAN)
    ]
    for copy in early + copies:
        copy.start()
    early[0].wait()
    cells_of(z, drawing, pixels, spread)
    early[1].wait()
    coding = shrink(potential[...]).astype(BF16)
    reconstruct(z, place, coding, dic, pixels, tall_sum, own, lambda i: copies[i].wait())
    send_sides(z, place, own, sends)
    owned = atoms.shape[0]
    atoms[...] = dic[pl.ds(pl.multiple_of(place.owner * owned, owned), owned), :]


def side_kernel(z, grid, where, own, from_even, from_odd, joined, even, odd, rim):
    place = Place(where, *grid)
    joined[...] = own[...]
    add_sides(z, place, joined, (from_even, from_odd))
    rim[MARGIN * z.wide :, :] = jnp.zeros((z.rim - MARGIN * z.wide, z.lanes), F32)
    for mine, halves in place.pairs(0):

        @pl.when(mine)
        def _(halves=halves):
            for send, (onward, _) in zip((even, odd), halves):
                first = z.rows if onward else 0
                for r in range(MARGIN):
                    start = MARGIN * z.cols + r * MARGIN
                    rim[r * z.cols : (r + 1) * z.cols, :] = joined[first + r, 0 : z.cols, :]
                    rim[start : start + MARGIN, :] = joined[first + r, z.cols : z.wide, :]
                send[...] = rim[...].astype(BF16)


def add_ends(z, place, whole, received, rim):
    for mine, halves in place.pairs(0):
        for block, (onward, there) in zip(received, halves):

            @pl.when(mine & there)
            def _(block=block, first=z.rows if onward else 0):
                rim[...] = block[...].astype(F32)
                for r in range(MARGIN):
                    start = MARGIN * z.cols + r * MARGIN
                    whole[first + r, 0 : z.cols, :] += rim[r * z.cols : (r + 1) * z.cols, :]
                    whole[first + r, z.cols : z.wide, :] += rim[start : start + MARGIN, :]


def windows_of(z, whole, wide_part, first_row, row_stride):
    for j in range(SPAN):
        part = whole[:, j : j + z.cols, 0 : z.cell].astype(BF16)
        for p in range(z.tall):
            wide_part[
                pl.ds(p * row_stride + first_row, z.cols), j * z.cell : (j + 1) * z.cell
            ] = part[p]


def sweep_kernel(
    z, grid, last, where, potential, joined, from_even, from_odd, pixels, dic, *rest
):
    if last:
        new_potential, own, *sends, codes, tall_sum, whole, wide_part, rim = rest
    else:
        new_potential, own, *sends, tall_sum, whole, wide_part, rim = rest
    place = Place(where, *grid)
    whole[...] = joined[...]
    add_ends(z, place, whole, (from_even, from_odd), rim)
    windows_of(z, whole, wide_part, 0, z.cols)
    drive = None
    for i in range(SPAN):
        term = lax.dot_general(
            wide_part[i * z.cols : i * z.cols + z.sites, :],
            dic[:, i * z.band : (i + 1) * z.band],
            (((1,), (1,)), ((), ())),
            preferred_element_type=F32,
        )
        drive = term if drive is None else drive + term
    old = potential[...]
    updated = old + RELAXATION * (drive * z.scale + shrink(old) - old)
    active = shrink(updated)
    coding = active.astype(BF16)
    if last:
        new_potential[...] = active
        codes[...] = coding
    else:
        new_potential[...] = updated
    reconstruct(z, place, coding, dic, pixels, tall_sum, own)
    send_sides(z, place, own, sends)


def sort_kernel(z, groups, where, codes, _, shared):
    rows_n, cores_n, owned = groups
    span = z.atoms // rows_n
    src = lax.broadcasted_iota(jnp.int32, (span, span), 0)
    dst = lax.broadcasted_iota(jnp.int32, (span, span), 1)
    per_core = span // cores_n
    core, rem = dst // per_core, dst % per_core
    wanted = (rem // owned) * (owned * cores_n) + core * owned + rem % owned
    order = is_equal(src, wanted)
    for r in range(rows_n):
        line = jnp.dot(codes[:, r * span : (r + 1) * span], order, preferred_element_type=F32)
        for k in range(cores_n):
            shared[r * cores_n + k] = line[:, k * per_core : (k + 1) * per_core].astype(BF16)


def pack_kernel(z, grid, where, own, from_even, from_odd, packed, joined, flat):
    joined[...] = own[...]
    add_sides(z, Place(where, *grid), joined, (from_even, from_odd))
    base = z.tall * z.cols
    flat[base:, :] = jnp.zeros((z.packed - base, z.lanes), F32)
    for p in range(z.tall):
        flat[p * z.cols : (p + 1) * z.cols, :] = joined[p, 0 : z.cols, :]
    for c in range(MARGIN):
        start = base + c * z.tall_pad
        flat[start : start + z.tall, :] = joined[:, z.cols + c, :]
    half = z.packed // 2
    packed[0 : z.packed, :] = flat[:, 0:128].astype(BF16)
    tail = z.cell - 128
    ends = jnp.concatenate([flat[0:half, 128 : z.cell], flat[half:, 128 : z.cell]], axis=1)
    packed[z.packed :, 0 : 2 * tail] = ends.astype(BF16)


def offset(at, step, n):
    return at ^ step if n & (n - 1) == 0 else (at + step) % n


def learn_half(z, grid, where, across, wide_part, stride, bands, outs, partial):
    count = z.rows * stride
    for n, i in enumerate(bands):
        term = jnp.dot(
            across, wide_part[i * stride : i * stride + count, :], preferred_element_type=F32
        )
        partial[:, n * z.band : (n + 1) * z.band] = (term * z.scale).astype(BF16)
    owned = outs[0].shape[0]
    place = Place(where, *grid)
    for step, out in enumerate(outs):
        at = offset(place.col // 2, step, len(outs))
        out[...] = partial[pl.ds(pl.multiple_of(at * owned, owned), owned), :]


def learn_kernel(z, grid, groups, yx_n, where, shared, *rest):
    rows_n, cores_n, _ = groups
    members = rows_n * cores_n
    near, far, outs = rest[:rows_n], rest[rows_n : 2 * rows_n], rest[2 * rows_n :]
    outs, (across, wide_part, partial, flat, whole, codes) = outs[:yx_n], outs[yx_n:]
    stride = members * z.cols
    base = z.tall * z.cols
    half = z.packed // 2
    tail = z.cell - 128
    place = Place(where, *grid)
    mine = place.col % 2

    for x in range(rows_n):
        d = offset(place.row, x, rows_n)
        for k, block in ((mine, near[x]), (1 - mine, far[x])):
            flat[k, d, :, 0:128] = block[0 : z.packed, :].astype(F32)
            ends = block[z.packed :, :].astype(F32)
            flat[k, d, 0:half, 128 : z.cell] = ends[:, 0:tail]
            flat[k, d, half:, 128 : z.cell] = ends[:, tail : 2 * tail]
    for k in range(cores_n):
        for r in range(rows_n):
            d = r * cores_n + k
            for source, low, high, at in (
                (r, 0, z.tall, 0),
                (r - 1, z.rows, z.tall, 0),
                (r + 1, 0, MARGIN, z.rows),
            ):
                if not 0 <= source < rows_n:
                    continue
                n = high - low
                main = flat[k, source, low * z.cols : high * z.cols, :]
                main = main.reshape(n, z.cols, z.lanes)
                side = [
                    flat[k, source, base + c * z.tall_pad + low : base + c * z.tall_pad + high, :]
                    for c in range(MARGIN)
                ]
                if source == r:
                    whole[at : at + n, 0 : z.cols, :] = main
                    for c in range(MARGIN):
                        whole[at : at + n, z.cols + c, :] = side[c]
                else:
                    whole[at : at + n, 0 : z.cols, :] += main
                    for c in range(MARGIN):
                        whole[at : at + n, z.cols + c, :] += side[c]
            windows_of(z, whole, wide_part, d * z.cols, stride)
            for i in range(z.rows):
                codes[i * stride + d * z.cols : i * stride + (d + 1) * z.cols, :] = shared[
                    d, i * z.cols : (i + 1) * z.cols, :
                ]
    across[...] = codes[...].astype(F32).T.astype(BF16)
    learn_half(
        z, grid, where, across[...], wide_part, stride, range(SPAN // 2), outs, partial
    )


def rest_kernel(z, grid, stride, where, across, wide_part, *rest):
    *outs, partial = rest
    learn_half(
        z, grid, where, across[...], wide_part, stride, range(SPAN // 2, SPAN), outs, partial
    )


def finish_kernel(z, yx_n, where, momentum, atoms, *rest):
    *parts, new_dictionary, new_momentum, weights, updated, sems = rest
    width = z.patch // 2
    power = 0.0
    copies = []
    for h in range(2):
        lanes = pl.ds(h * width, width)
        learning = parts[h * yx_n][...].astype(F32)
        for part in parts[h * yx_n + 1 : (h + 1) * yx_n]:
            learning = learning + part[...].astype(F32)
        momentum_out = DECAY * momentum[:, lanes] + learning
        updated[:, lanes] = momentum_out
        copies.append(
            pltpu.make_async_copy(updated.at[:, lanes], new_momentum.at[:, lanes], sems.at[h])
        )
        copies[-1].start()
        weight = atoms[:, lanes].astype(F32) + LEARNING * momentum_out
        weights[:, lanes] = weight
        power = power + jnp.sum(weight * weight, axis=1, keepdims=True)
    norm = lax.rsqrt(power * (1.0 / z.patch) + EPSILON)
    for h in range(2):
        lanes = pl.ds(h * width, width)
        weights[:, lanes] = weights[:, lanes] * norm
        copies.append(
            pltpu.make_async_copy(
                weights.at[:, lanes], new_dictionary.at[:, lanes], sems.at[2 + h]
            )
        )
        copies[-1].start()
    for copy in copies:
        copy.wait()


def kept(x, space=pltpu.VMEM):
    return pltpu.with_memory_space_constraint(x, space)


def call(kernel, outs, inputs, scratch, far=0, leave=VMEM):
    specs = [SMEM] + [HBM] * far + [VMEM] * (len(inputs) - 1 - far)
    where, *others = inputs
    placed = [kept(x, pltpu.HBM) for x in others[:far]] + [kept(x) for x in others[far:]]
    return pl.pallas_call(
        kernel,
        out_shape=outs,
        in_specs=specs,
        out_specs=[leave] * len(outs),
        scratch_shapes=scratch,
        compiler_params=PARAMS,
    )(where, *placed)


def shards(picture, membrane, dictionary, momentum):
    site_rows, site_cols, atom_count = membrane.shape
    z = Sizes(site_rows, site_cols, atom_count, dictionary.shape[1])
    rows_n, yx_n, cores_n = (lax.axis_size(a) for a in ("row", "yx", "core"))
    cols_n = yx_n * cores_n
    owned = momentum.shape[0]
    groups = (rows_n, cores_n, owned)
    members = rows_n * cores_n
    grid = (rows_n, cols_n)
    where = jnp.stack([lax.axis_index("row"), lax.axis_index(("yx", "core"))]).astype(jnp.int32)

    def swapped(axis, n, blocks):
        return [lax.ppermute(b, axis, route) for b, route in zip(blocks, partners(n))]

    def sideways(blocks):
        even, odd = partners(cols_n)
        near_rim = lax.ppermute(blocks[0], ("yx", "core"), even)
        far_rim = lax.ppermute(blocks[1], ("yx", "core"), odd)
        return [near_rim, far_rim]

    own_v = pltpu.VMEM((z.tall, z.wide_pad, z.lanes), F32)
    side_v = pltpu.VMEM((MARGIN, z.tall_pad, z.lanes), BF16)
    end_v = pltpu.VMEM((z.rim, z.lanes), BF16)
    rim_v = pltpu.VMEM((z.rim, z.lanes), F32)
    tall_v = pltpu.VMEM((z.tall * z.cols, z.band), F32)
    wide_v = pltpu.VMEM((z.tall * z.cols, z.band), BF16)
    flat_v = pltpu.VMEM((z.packed, z.lanes), F32)
    site_v = pltpu.VMEM((z.sites, atom_count), F32)
    outs = [own_v, side_v, side_v]

    own, *sides, pixels, dic, potential, atoms = call(
        functools.partial(first_kernel, z, grid),
        outs
        + [
            pltpu.VMEM((z.sites, z.cell), F32),
            pltpu.VMEM(dictionary.shape, BF16),
            site_v,
            pltpu.VMEM(momentum.shape, BF16),
        ],
        (where, membrane.reshape(z.sites, atom_count), picture, dictionary),
        [
            tall_v,
            pltpu.VMEM((3 * picture.shape[2], z.cell), BF16),
            pltpu.VMEM(picture.shape, F32),
            pltpu.SemaphoreType.DMA((SPAN + 2,)),
        ],
        far=3,
    )
    for repeat in range(SWEEPS):
        last = repeat == SWEEPS - 1
        joined, *ends = call(
            functools.partial(side_kernel, z, grid),
            [own_v, end_v, end_v],
            (where, own, *sideways(sides)),
            [rim_v],
        )
        ends = swapped("row", rows_n, ends)
        final = [
            site_v,
            *outs,
            pltpu.VMEM((z.sites, atom_count), BF16),
        ]
        potential, own, *rest = call(
            functools.partial(sweep_kernel, z, grid, last),
            final if last else [site_v] + outs,
            (where, potential, joined, *ends, pixels, dic),
            [tall_v, own_v, wide_v, rim_v],
        )
        sides = rest[:2]
    final_codes = potential.reshape(membrane.shape)
    sides = sideways(sides)
    (shared,) = call(
        functools.partial(sort_kernel, z, groups),
        [pltpu.VMEM((members, z.sites, atom_count // members), BF16)],
        (where, rest[2], sides[0]),
        [],
    )
    shared = lax.all_to_all(shared, ("row", "core"), 0, 0, tiled=True)
    (packed,) = call(
        functools.partial(pack_kernel, z, grid),
        [pltpu.VMEM((z.packed * 3 // 2, 128), BF16)],
        (where, own, *sides),
        [own_v, flat_v],
    )

    def met(block, axis, n, step):
        return lax.ppermute(block, axis, [(i, offset(i, step, n)) for i in range(n)])

    power = rows_n & (rows_n - 1) == 0
    near = [packed] + [
        met(packed, "row", rows_n, x if power else rows_n - x) for x in range(1, rows_n)
    ]
    far = [met(block, "core", 2, 1) for block in near]
    stride = members * z.cols
    group_atoms = atom_count // members
    half_v = pltpu.VMEM((owned, z.patch // 2), BF16)
    partial_v = pltpu.VMEM((group_atoms, z.patch // 2), BF16)
    *first_half, across, wide_part = call(
        functools.partial(learn_kernel, z, grid, groups, yx_n),
        [half_v] * yx_n
        + [
            pltpu.VMEM((group_atoms, members * z.sites), BF16),
            pltpu.VMEM((z.tall * stride, z.band), BF16),
        ],
        (where, shared, *near, *far),
        [
            partial_v,
            pltpu.VMEM((cores_n, rows_n, z.packed, z.lanes), F32),
            own_v,
            pltpu.VMEM((members * z.sites, group_atoms), BF16),
        ],
    )
    other_half = call(
        functools.partial(rest_kernel, z, grid, stride),
        [half_v] * yx_n,
        (where, across, wide_part),
        [partial_v],
    )
    parts = [
        block if step == 0 else met(block, "yx", yx_n, step)
        for half in (first_half, other_half)
        for step, block in enumerate(half)
    ]
    new_dictionary, new_momentum = call(
        functools.partial(finish_kernel, z, yx_n),
        [jax.ShapeDtypeStruct(momentum.shape, F32)] * 2,
        (where, momentum, atoms, *parts),
        [
            pltpu.VMEM(momentum.shape, F32),
            pltpu.VMEM(momentum.shape, F32),
            pltpu.SemaphoreType.DMA((4,)),
        ],
        leave=HBM,
    )
    return (final_codes, new_dictionary, new_momentum)


def solution(mesh):
    rows_n, cols_n = (mesh.shape["row"], mesh.shape["col"])
    split = Mesh(mesh.devices.reshape(rows_n, cols_n // 2, 2), ("row", "yx", "core"))
    col = ("yx", "core")
    return jax.shard_map(
        shards,
        mesh=split,
        in_specs=(P(None, "row", col), P("row", col, None), P(), P(("row",) + col, None)),
        out_specs=(P("row", col, None), P(("row",) + col, None), P(("row",) + col, None)),
        check_vma=False,
    )
```

profile of v0, /device:TPU:0, one launch (start us, length us, event | category | flops | bytes accessed | tf_op | source)
XLA Modules:
  0.0 80.2 jit_solution(8935643414861769467)
XLA Ops:
  0.7 4.4 %shard_map.67 = (f32[11,24,256]{2,1,0:T(8,128)S(1)}, bf16[3,16,256]{2,1,0:T(8,128)(2,1)S(1)}, bf16[3,16,256]{2,1,0:T(8,128)(2,1)S(1)}, f32[128,192]{1,0:T(8,128)...) custom-call(s32[2]{0:T(128)S(1)} %pad_add_fusion.where, ...), custom_call_target="tpu_custom_call" | custom-call | tf_op jit(solution)/shard_map/pallas_call | solution.py:424
  5.7 3.5 %collective-permute-start.1 = (bf16[3,16,256]{2,1,0:T(8,128)(2,1)S(1)}, bf16[3,16,256]{2,1,0:T(8,128)(2,1)S(1)}, u32[]{:S(2)}, u32[]{:S(2)}) collective-permute-start(bf16[3,16,256]{2,1,0:T(8,128)(2,1)S(1)} %get-tuple-element.40), channel_id=1, source_target_pairs={{0,7},{1,2},{2,1},{3,4},{4,3},{5,6},{6,5},{7,0},{8,15},{9,10},{10,... | collective-permute-start | bytes 73736 | tf_op jit(solution)/shard_map/ppermute | solution.py:451
  9.2 1.5 %collective-permute-done.1.from_odd = bf16[3,16,256]{2,1,0:T(8,128)(2,1)S(1)} collective-permute-done((bf16[3,16,256]{2,1,0:T(8,128)(2,1)S(1)}, bf16[3,16,256]{2,1,0:T(8,128)(2,1)S(1)}, u32[]{:S(2)}, u32[]{:S(2)}) %collective-permute-start.1) | collective-permute-done | bytes 24608 | tf_op jit(solution)/shard_map/ppermute | solution.py:451
  11.4 1.8 %collective-permute-start.2 = (bf16[64,256]{1,0:T(8,128)(2,1)S(1)}, bf16[64,256]{1,0:T(8,128)(2,1)S(1)}, u32[]{:S(2)}, u32[]{:S(2)}) collective-permute-start(bf16[64,256]{1,0:T(8,128)(2,1)S(1)} %get-tuple-element.42), channel_id=1, source_target_pairs={{0,8},{8,0},{16,24},{24,16},{1,9},{9,1},{17,25},{25,17},{2,10},{10... | collective-permute-start | bytes 98312 | tf_op jit(solution)/shard_map/ppermute | solution.py:446
  13.2 2.5 %collective-permute-start.3 = (bf16[64,256]{1,0:T(8,128)(2,1)S(1)}, bf16[64,256]{1,0:T(8,128)(2,1)S(1)}, u32[]{:S(2)}, u32[]{:S(2)}) collective-permute-start(bf16[64,256]{1,0:T(8,128)(2,1)S(1)} %get-tuple-element.43), channel_id=1, source_target_pairs={{0,24},{8,16},{16,8},{24,0},{1,25},{9,17},{17,9},{25,1},{2,26},{10... | collective-permute-start | bytes 98312 | tf_op jit(solution)/shard_map/ppermute | solution.py:446
  15.6 3.2 %collective-permute-done.3.from_odd = bf16[64,256]{1,0:T(8,128)(2,1)S(1)} collective-permute-done((bf16[64,256]{1,0:T(8,128)(2,1)S(1)}, bf16[64,256]{1,0:T(8,128)(2,1)S(1)}, u32[]{:S(2)}, u32[]{:S(2)}) %collective-permute-start.3) | collective-permute-done | bytes 32800 | tf_op jit(solution)/shard_map/ppermute | solution.py:446
  18.9 4.3 %shard_map.69 = (f32[128,1024]{1,0:T(8,128)S(1)}, f32[11,24,256]{2,1,0:T(8,128)S(1)}, bf16[3,16,256]{2,1,0:T(8,128)(2,1)S(1)}, bf16[3,16,256]{2,1,0:T(8,128)(2,1)S(1)}) custom-call(s32[2]{0:T(128)S(1)} %pad_add_fusion.where, f32[128,1024]{1,0:T(8,128)S(1)} %get-tuple-element.37.potential, f32[11,24,256]{2,1,0:T(8,128)S(1)} %get-tuple-element.41.joined, ...), custom_call_target="tpu_custom_call" | custom-call | tf_op jit(solution)/shard_map/pallas_call | solution.py:424
  23.3 2.0 %collective-permute-start.5 = (bf16[3,16,256]{2,1,0:T(8,128)(2,1)S(1)}, bf16[3,16,256]{2,1,0:T(8,128)(2,1)S(1)}, u32[]{:S(2)}, u32[]{:S(2)}) collective-permute-start(bf16[3,16,256]{2,1,0:T(8,128)(2,1)S(1)} %get-tuple-element.49), channel_id=1, source_target_pairs={{0,7},{1,2},{2,1},{3,4},{4,3},{5,6},{6,5},{7,0},{8,15},{9,10},{10,... | collective-permute-start | bytes 73736 | tf_op jit(solution)/shard_map/ppermute | solution.py:451
  25.3 2.2 %collective-permute-done.5.from_odd = bf16[3,16,256]{2,1,0:T(8,128)(2,1)S(1)} collective-permute-done((bf16[3,16,256]{2,1,0:T(8,128)(2,1)S(1)}, bf16[3,16,256]{2,1,0:T(8,128)(2,1)S(1)}, u32[]{:S(2)}, u32[]{:S(2)}) %collective-permute-start.5) | collective-permute-done | bytes 24608 | tf_op jit(solution)/shard_map/ppermute | solution.py:451
  28.2 2.5 %collective-permute-start.7 = (bf16[64,256]{1,0:T(8,128)(2,1)S(1)}, bf16[64,256]{1,0:T(8,128)(2,1)S(1)}, u32[]{:S(2)}, u32[]{:S(2)}) collective-permute-start(bf16[64,256]{1,0:T(8,128)(2,1)S(1)} %get-tuple-element.52), channel_id=1, source_target_pairs={{0,24},{8,16},{16,8},{24,0},{1,25},{9,17},{17,9},{25,1},{2,26},{10... | collective-permute-start | bytes 98312 | tf_op jit(solution)/shard_map/ppermute | solution.py:446
  30.8 1.4 %collective-permute-done.6.from_even = bf16[64,256]{1,0:T(8,128)(2,1)S(1)} collective-permute-done((bf16[64,256]{1,0:T(8,128)(2,1)S(1)}, bf16[64,256]{1,0:T(8,128)(2,1)S(1)}, u32[]{:S(2)}, u32[]{:S(2)}) %collective-permute-start.6) | collective-permute-done | bytes 32800 | tf_op jit(solution)/shard_map/ppermute | solution.py:446
  32.1 1.9 %collective-permute-done.7.from_odd = bf16[64,256]{1,0:T(8,128)(2,1)S(1)} collective-permute-done((bf16[64,256]{1,0:T(8,128)(2,1)S(1)}, bf16[64,256]{1,0:T(8,128)(2,1)S(1)}, u32[]{:S(2)}, u32[]{:S(2)}) %collective-permute-start.7) | collective-permute-done | bytes 32800 | tf_op jit(solution)/shard_map/ppermute | solution.py:446
  34.0 4.3 %shard_map.71 = (f32[128,1024]{1,0:T(8,128)S(1)}, f32[11,24,256]{2,1,0:T(8,128)S(1)}, bf16[3,16,256]{2,1,0:T(8,128)(2,1)S(1)}, bf16[3,16,256]{2,1,0:T(8,128)(2,1)S(1)}, bf16[128,1024]{1,0:T(8,128)(2,1)S(1)}) custom-call(s32[2]{0:T(128)S(1)} %pad_add_fusion.where, f32[128,1024]{1,0:T(8,128)S(1)} %get-tuple-element.46.potential, ...), custom_call_target="tpu_custom_call" | custom-call | tf_op jit(solution)/shard_map/pallas_call | solution.py:424
  38.4 1.2 %collective-permute-done.8._.from_even = bf16[3,16,256]{2,1,0:T(8,128)(2,1)S(1)} collective-permute-done((bf16[3,16,256]{2,1,0:T(8,128)(2,1)S(1)}, bf16[3,16,256]{2,1,0:T(8,128)(2,1)S(1)}, u32[]{:S(2)}, u32[]{:S(2)}) %collective-permute-start.8) | collective-permute-done | bytes 24608 | tf_op jit(solution)/shard_map/ppermute | solution.py:450
  39.6 1.5 %shard_map.72 = bf16[8,128,128]{2,1,0:T(8,128)(2,1)} custom-call(s32[2]{0:T(128)S(1)} %pad_add_fusion.where, bf16[128,1024]{1,0:T(8,128)(2,1)S(1)} %get-tuple-element.55.codes, bf16[3,16,256]{2,1,0:T(8,128)(2,1)S(1)} %collective-permute-done.8._.from_even), custom_call_target="tpu_custom_call" | custom-call | tf_op jit(solution)/shard_map/pallas_call | solution.py:424
  41.1 3.7 %all-to-all-start = ((bf16[8,128,128]{2,1,0:T(8,128)(2,1)}), bf16[8,128,128]{2,1,0:T(8,128)(2,1)S(1)}, u32[]{:S(2)}, u32[]{:S(2)}) async-start(bf16[8,128,128]{2,1,0:T(8,128)(2,1)} %shard_map.72), calls=%async_computation | async-start | bytes 524288 | tf_op jit(solution)/shard_map/all_to_all | solution.py:511
  44.9 1.3 %collective-permute-start.9 = (bf16[3,16,256]{2,1,0:T(8,128)(2,1)S(1)}, bf16[3,16,256]{2,1,0:T(8,128)(2,1)S(1)}, u32[]{:S(2)}, u32[]{:S(2)}) collective-permute-start(bf16[3,16,256]{2,1,0:T(8,128)(2,1)S(1)} %get-tuple-element.58), channel_id=1, source_target_pairs={{0,7},{1,2},{2,1},{3,4},{4,3},{5,6},{6,5},{7,0},{8,15},{9,10},{10,... | collective-permute-start | bytes 73736 | tf_op jit(solution)/shard_map/ppermute | solution.py:451
  46.1 2.9 %collective-permute-done.9.from_odd = bf16[3,16,256]{2,1,0:T(8,128)(2,1)S(1)} collective-permute-done((bf16[3,16,256]{2,1,0:T(8,128)(2,1)S(1)}, bf16[3,16,256]{2,1,0:T(8,128)(2,1)S(1)}, u32[]{:S(2)}, u32[]{:S(2)}) %collective-permute-start.9) | collective-permute-done | bytes 24608 | tf_op jit(solution)/shard_map/ppermute | solution.py:451
  49.0 0.9 %shard_map.73.rest_0_ = bf16[336,128]{1,0:T(8,128)(2,1)S(1)} custom-call(s32[2]{0:T(128)S(1)} %pad_add_fusion.where, f32[11,24,256]{2,1,0:T(8,128)S(1)} %get-tuple-element.57.own, bf16[3,16,256]{2,1,0:T(8,128)(2,1)S(1)} %collective-permute-done.8._.from_even, bf16[3,16,256]{2,1,0:T(8,128)(2,1)S(1)} %collective-permute-done.9.from_odd), custom_call_target="tpu_custom_call" | custom-call | tf_op jit(solution)/shard_map/pallas_call | solution.py:424
  49.9 3.9 %collective-permute-start.12 = (bf16[336,128]{1,0:T(8,128)(2,1)S(1)}, bf16[336,128]{1,0:T(8,128)(2,1)S(1)}, u32[]{:S(2)}, u32[]{:S(2)}) collective-permute-start(bf16[336,128]{1,0:T(8,128)(2,1)S(1)} %shard_map.73.rest_0_), channel_id=1, source_target_pairs={{0,24},{8,16},{16,8},{24,0},{1,25},{9,17},{17,9},{25,1},{2,26},{10... | collective-permute-start | bytes 258056 | tf_op jit(solution)/shard_map/ppermute | solution.py:520
  54.4 2.7 %collective-permute-done.12.rest_3_ = bf16[336,128]{1,0:T(8,128)(2,1)S(1)} collective-permute-done((bf16[336,128]{1,0:T(8,128)(2,1)S(1)}, bf16[336,128]{1,0:T(8,128)(2,1)S(1)}, u32[]{:S(2)}, u32[]{:S(2)}) %collective-permute-start.12) | collective-permute-done | bytes 86048 | tf_op jit(solution)/shard_map/ppermute | solution.py:520
  57.1 4.8 %collective-permute-done.11.rest_2_ = bf16[336,128]{1,0:T(8,128)(2,1)S(1)} collective-permute-done((bf16[336,128]{1,0:T(8,128)(2,1)S(1)}, bf16[336,128]{1,0:T(8,128)(2,1)S(1)}, u32[]{:S(2)}, u32[]{:S(2)}) %collective-permute-start.11) | collective-permute-done | bytes 86048 | tf_op jit(solution)/shard_map/ppermute | solution.py:520
  63.4 2.5 %shard_map.74 = (bf16[32,1536]{1,0:T(8,128)(2,1)S(1)}, bf16[32,1536]{1,0:T(8,128)(2,1)S(1)}, bf16[32,1536]{1,0:T(8,128)(2,1)S(1)}, bf16[32,1536]{1,0:T(8,128)(2,...) custom-call(s32[2]{0:T(128)S(1)} %pad_add_fusion.where, ...), custom_call_target="tpu_custom_call" | custom-call | tf_op jit(solution)/shard_map/pallas_call | solution.py:424
  66.2 1.6 %collective-permute-start.18 = (bf16[32,1536]{1,0:T(8,128)(2,1)S(1)}, bf16[32,1536]{1,0:T(8,128)(2,1)S(1)}, u32[]{:S(2)}, u32[]{:S(2)}) collective-permute-start(bf16[32,1536]{1,0:T(8,128)(2,1)S(1)} %get-tuple-element.61), channel_id=1, source_target_pairs={{0,4},{2,6},{4,0},{6,2},{1,5},{3,7},{5,1},{7,3},{8,12},{10,14},{12... | collective-permute-start | bytes 294920 | tf_op jit(solution)/shard_map/ppermute | solution.py:520
  67.8 1.7 %collective-permute-start.19 = (bf16[32,1536]{1,0:T(8,128)(2,1)S(1)}, bf16[32,1536]{1,0:T(8,128)(2,1)S(1)}, u32[]{:S(2)}, u32[]{:S(2)}) collective-permute-start(bf16[32,1536]{1,0:T(8,128)(2,1)S(1)} %get-tuple-element.62), channel_id=1, source_target_pairs={{0,6},{2,4},{4,2},{6,0},{1,7},{3,5},{5,3},{7,1},{8,14},{10,12},{12... | collective-permute-start | bytes 294920 | tf_op jit(solution)/shard_map/ppermute | solution.py:520
  69.5 1.1 %shard_map.75 = (bf16[32,1536]{1,0:T(8,128)(2,1)S(1)}, bf16[32,1536]{1,0:T(8,128)(2,1)S(1)}, bf16[32,1536]{1,0:T(8,128)(2,1)S(1)}, bf16[32,1536]{1,0:T(8,128)(2,1)S(1)}) custom-call(s32[2]{0:T(128)S(1)} %pad_add_fusion.where, bf16[128,1024]{1,0:T(8,128)(2,1)S(1)} %get-tuple-element.63.across, bf16[1408,768]{1,0:T(8,128)(2,1)S(1)} %get-tuple-element.64.wide_part), custom_call_target="tpu_custom_call" | custom-call | tf_op jit(solution)/shard_map/pallas_call | solution.py:424
  70.9 1.6 %collective-permute-start.21 = (bf16[32,1536]{1,0:T(8,128)(2,1)S(1)}, bf16[32,1536]{1,0:T(8,128)(2,1)S(1)}, u32[]{:S(2)}, u32[]{:S(2)}) collective-permute-start(bf16[32,1536]{1,0:T(8,128)(2,1)S(1)} %get-tuple-element.67), channel_id=1, source_target_pairs={{0,4},{2,6},{4,0},{6,2},{1,5},{3,7},{5,1},{7,3},{8,12},{10,14},{12... | collective-permute-start | bytes 294920 | tf_op jit(solution)/shard_map/ppermute | solution.py:520
  72.5 1.7 %collective-permute-start.22 = (bf16[32,1536]{1,0:T(8,128)(2,1)S(1)}, bf16[32,1536]{1,0:T(8,128)(2,1)S(1)}, u32[]{:S(2)}, u32[]{:S(2)}) collective-permute-start(bf16[32,1536]{1,0:T(8,128)(2,1)S(1)} %get-tuple-element.68), channel_id=1, source_target_pairs={{0,6},{2,4},{4,2},{6,0},{1,7},{3,5},{5,3},{7,1},{8,14},{10,12},{12... | collective-permute-start | bytes 294920 | tf_op jit(solution)/shard_map/ppermute | solution.py:520
  75.0 1.4 %collective-permute-done.20.rest_5_ = bf16[32,1536]{1,0:T(8,128)(2,1)S(1)} collective-permute-done((bf16[32,1536]{1,0:T(8,128)(2,1)S(1)}, bf16[32,1536]{1,0:T(8,128)(2,1)S(1)}, u32[]{:S(2)}, u32[]{:S(2)}) %collective-permute-start.20) | collective-permute-done | bytes 98336 | tf_op jit(solution)/shard_map/ppermute | solution.py:520
  76.4 1.0 %collective-permute-done.21.rest_6_ = bf16[32,1536]{1,0:T(8,128)(2,1)S(1)} collective-permute-done((bf16[32,1536]{1,0:T(8,128)(2,1)S(1)}, bf16[32,1536]{1,0:T(8,128)(2,1)S(1)}, u32[]{:S(2)}, u32[]{:S(2)}) %collective-permute-start.21) | collective-permute-done | bytes 98336 | tf_op jit(solution)/shard_map/ppermute | solution.py:520
  77.3 1.1 %collective-permute-done.22.rest_7_ = bf16[32,1536]{1,0:T(8,128)(2,1)S(1)} collective-permute-done((bf16[32,1536]{1,0:T(8,128)(2,1)S(1)}, bf16[32,1536]{1,0:T(8,128)(2,1)S(1)}, u32[]{:S(2)}, u32[]{:S(2)}) %collective-permute-start.22) | collective-permute-done | bytes 98336 | tf_op jit(solution)/shard_map/ppermute | solution.py:520
  78.4 1.6 %shard_map.76 = (f32[32,3072]{1,0:T(8,128)}, f32[32,3072]{1,0:T(8,128)}) custom-call(s32[2]{0:T(128)S(1)} %pad_add_fusion.where, f32[32,3072]{1,0:T(8,128)S(1)} %copy-done, bf16[32,3072]{1,0:T(8,128)(2,1)S(1)} %get-tuple-element.54.atoms, bf16[32,1536]{1,0:T(8,128)(2,1)S(1)} %get-tuple-element.59.rest_0_, ...), custom_call_target="tpu_custom_call" | custom-call | tf_op jit(solution)/shard_map/pallas_call | solution.py:424
  (30 shorter events, 5.5 us)
Async XLA Ops:
  5.1 4.1 %collective-permute-start = (bf16[3,16,256]{2,1,0:T(8,128)(2,1)S(1)}, bf16[3,16,256]{2,1,0:T(8,128)(2,1)S(1)}, u32[]{:S(2)}, u32[]{:S(2)}) collective-permute-start(bf16[3,16,256]{2,1,0:T(8,128)(2,1)S(1)} %get-tuple-element.39), channel_id=1, source_target_pairs={{0,1},{1,0},{2,3},{3,2},{4,5},{5,4},{6,7},{7,6},{8,9},{9,8},{10,11... | collective-permute-start | bytes 73736 | tf_op jit(solution)/shard_map/ppermute | solution.py:450
  5.7 5.1 %collective-permute-start.1 = (bf16[3,16,256]{2,1,0:T(8,128)(2,1)S(1)}, bf16[3,16,256]{2,1,0:T(8,128)(2,1)S(1)}, u32[]{:S(2)}, u32[]{:S(2)}) collective-permute-start(bf16[3,16,256]{2,1,0:T(8,128)(2,1)S(1)} %get-tuple-element.40), channel_id=1, source_target_pairs={{0,7},{1,2},{2,1},{3,4},{4,3},{5,6},{6,5},{7,0},{8,15},{9,10},{10,... | collective-permute-start | bytes 73736 | tf_op jit(solution)/shard_map/ppermute | solution.py:451
  11.4 4.3 %collective-permute-start.2 = (bf16[64,256]{1,0:T(8,128)(2,1)S(1)}, bf16[64,256]{1,0:T(8,128)(2,1)S(1)}, u32[]{:S(2)}, u32[]{:S(2)}) collective-permute-start(bf16[64,256]{1,0:T(8,128)(2,1)S(1)} %get-tuple-element.42), channel_id=1, source_target_pairs={{0,8},{8,0},{16,24},{24,16},{1,9},{9,1},{17,25},{25,17},{2,10},{10... | collective-permute-start | bytes 98312 | tf_op jit(solution)/shard_map/ppermute | solution.py:446
  13.2 5.7 %collective-permute-start.3 = (bf16[64,256]{1,0:T(8,128)(2,1)S(1)}, bf16[64,256]{1,0:T(8,128)(2,1)S(1)}, u32[]{:S(2)}, u32[]{:S(2)}) collective-permute-start(bf16[64,256]{1,0:T(8,128)(2,1)S(1)} %get-tuple-element.43), channel_id=1, source_target_pairs={{0,24},{8,16},{16,8},{24,0},{1,25},{9,17},{17,9},{25,1},{2,26},{10... | collective-permute-start | bytes 98312 | tf_op jit(solution)/shard_map/ppermute | solution.py:446
  23.2 2.1 %collective-permute-start.4 = (bf16[3,16,256]{2,1,0:T(8,128)(2,1)S(1)}, bf16[3,16,256]{2,1,0:T(8,128)(2,1)S(1)}, u32[]{:S(2)}, u32[]{:S(2)}) collective-permute-start(bf16[3,16,256]{2,1,0:T(8,128)(2,1)S(1)} %get-tuple-element.48), channel_id=1, source_target_pairs={{0,1},{1,0},{2,3},{3,2},{4,5},{5,4},{6,7},{7,6},{8,9},{9,8},{10,11... | collective-permute-start | bytes 73736 | tf_op jit(solution)/shard_map/ppermute | solution.py:450
  23.3 4.2 %collective-permute-start.5 = (bf16[3,16,256]{2,1,0:T(8,128)(2,1)S(1)}, bf16[3,16,256]{2,1,0:T(8,128)(2,1)S(1)}, u32[]{:S(2)}, u32[]{:S(2)}) collective-permute-start(bf16[3,16,256]{2,1,0:T(8,128)(2,1)S(1)} %get-tuple-element.49), channel_id=1, source_target_pairs={{0,7},{1,2},{2,1},{3,4},{4,3},{5,6},{6,5},{7,0},{8,15},{9,10},{10,... | collective-permute-start | bytes 73736 | tf_op jit(solution)/shard_map/ppermute | solution.py:451
  28.1 4.0 %collective-permute-start.6 = (bf16[64,256]{1,0:T(8,128)(2,1)S(1)}, bf16[64,256]{1,0:T(8,128)(2,1)S(1)}, u32[]{:S(2)}, u32[]{:S(2)}) collective-permute-start(bf16[64,256]{1,0:T(8,128)(2,1)S(1)} %get-tuple-element.51), channel_id=1, source_target_pairs={{0,8},{8,0},{16,24},{24,16},{1,9},{9,1},{17,25},{25,17},{2,10},{10... | collective-permute-start | bytes 98312 | tf_op jit(solution)/shard_map/ppermute | solution.py:446
  28.2 5.8 %collective-permute-start.7 = (bf16[64,256]{1,0:T(8,128)(2,1)S(1)}, bf16[64,256]{1,0:T(8,128)(2,1)S(1)}, u32[]{:S(2)}, u32[]{:S(2)}) collective-permute-start(bf16[64,256]{1,0:T(8,128)(2,1)S(1)} %get-tuple-element.52), channel_id=1, source_target_pairs={{0,24},{8,16},{16,8},{24,0},{1,25},{9,17},{17,9},{25,1},{2,26},{10... | collective-permute-start | bytes 98312 | tf_op jit(solution)/shard_map/ppermute | solution.py:446
  34.0 44.4 %copy-start = (f32[32,3072]{1,0:T(8,128)S(1)}, f32[32,3072]{1,0:T(8,128)}, u32[]{:S(2)}) copy-start(f32[32,3072]{1,0:T(8,128)} %momentum.1) | copy-start | bytes 1179652
  38.4 1.3 %collective-permute-start.8 = (bf16[3,16,256]{2,1,0:T(8,128)(2,1)S(1)}, bf16[3,16,256]{2,1,0:T(8,128)(2,1)S(1)}, u32[]{:S(2)}, u32[]{:S(2)}) collective-permute-start(bf16[3,16,256]{2,1,0:T(8,128)(2,1)S(1)} %get-tuple-element.56), channel_id=1, source_target_pairs={{0,1},{1,0},{2,3},{3,2},{4,5},{5,4},{6,7},{7,6},{8,9},{9,8},{10,11... | collective-permute-start | bytes 73736 | tf_op jit(solution)/shard_map/ppermute | solution.py:450
  41.1 22.3 %all-to-all-start = ((bf16[8,128,128]{2,1,0:T(8,128)(2,1)}), bf16[8,128,128]{2,1,0:T(8,128)(2,1)S(1)}, u32[]{:S(2)}, u32[]{:S(2)}) async-start(bf16[8,128,128]{2,1,0:T(8,128)(2,1)} %shard_map.72), calls=%async_computation | async-start | bytes 524288 | tf_op jit(solution)/shard_map/all_to_all | solution.py:511
  44.9 4.2 %collective-permute-start.9 = (bf16[3,16,256]{2,1,0:T(8,128)(2,1)S(1)}, bf16[3,16,256]{2,1,0:T(8,128)(2,1)S(1)}, u32[]{:S(2)}, u32[]{:S(2)}) collective-permute-start(bf16[3,16,256]{2,1,0:T(8,128)(2,1)S(1)} %get-tuple-element.58), channel_id=1, source_target_pairs={{0,7},{1,2},{2,1},{3,4},{4,3},{5,6},{6,5},{7,0},{8,15},{9,10},{10,... | collective-permute-start | bytes 73736 | tf_op jit(solution)/shard_map/ppermute | solution.py:451
  49.9 7.3 %collective-permute-start.12 = (bf16[336,128]{1,0:T(8,128)(2,1)S(1)}, bf16[336,128]{1,0:T(8,128)(2,1)S(1)}, u32[]{:S(2)}, u32[]{:S(2)}) collective-permute-start(bf16[336,128]{1,0:T(8,128)(2,1)S(1)} %shard_map.73.rest_0_), channel_id=1, source_target_pairs={{0,24},{8,16},{16,8},{24,0},{1,25},{9,17},{17,9},{25,1},{2,26},{10... | collective-permute-start | bytes 258056 | tf_op jit(solution)/shard_map/ppermute | solution.py:520
  53.8 8.2 %collective-permute-start.11 = (bf16[336,128]{1,0:T(8,128)(2,1)S(1)}, bf16[336,128]{1,0:T(8,128)(2,1)S(1)}, u32[]{:S(2)}, u32[]{:S(2)}) collective-permute-start(bf16[336,128]{1,0:T(8,128)(2,1)S(1)} %shard_map.73.rest_0_), channel_id=1, source_target_pairs={{0,16},{8,24},{16,0},{24,8},{1,17},{9,25},{17,1},{25,9},{2,18},{10... | collective-permute-start | bytes 258056 | tf_op jit(solution)/shard_map/ppermute | solution.py:520
  53.8 8.2 %collective-permute-start.10 = (bf16[336,128]{1,0:T(8,128)(2,1)S(1)}, bf16[336,128]{1,0:T(8,128)(2,1)S(1)}, u32[]{:S(2)}, u32[]{:S(2)}) collective-permute-start(bf16[336,128]{1,0:T(8,128)(2,1)S(1)} %shard_map.73.rest_0_), channel_id=1, source_target_pairs={{0,8},{8,0},{16,24},{24,16},{1,9},{9,1},{17,25},{25,17},{2,10},{10... | collective-permute-start | bytes 258056 | tf_op jit(solution)/shard_map/ppermute | solution.py:520
  54.4 8.1 %collective-permute-start.13 = (bf16[336,128]{1,0:T(8,128)(2,1)S(1)}, bf16[336,128]{1,0:T(8,128)(2,1)S(1)}, u32[]{:S(2)}, u32[]{:S(2)}) collective-permute-start(bf16[336,128]{1,0:T(8,128)(2,1)S(1)} %shard_map.73.rest_0_), channel_id=1, source_target_pairs={{0,1},{1,0},{2,3},{3,2},{4,5},{5,4},{6,7},{7,6},{8,9},{9,8},{10,11... | collective-permute-start | bytes 258056 | tf_op jit(solution)/shard_map/ppermute | solution.py:520
  57.1 5.3 %collective-permute-start.16 = (bf16[336,128]{1,0:T(8,128)(2,1)S(1)}, bf16[336,128]{1,0:T(8,128)(2,1)S(1)}, u32[]{:S(2)}, u32[]{:S(2)}) collective-permute-start(bf16[336,128]{1,0:T(8,128)(2,1)S(1)} %collective-permute-done.12.rest_3_), channel_id=1, source_target_pairs={{0,1},{1,0},{2,3},{3,2},{4,5},{5,4},{6,7},{7,6},{8,9},{9,8},{10,11... | collective-permute-start | bytes 258056 | tf_op jit(solution)/shard_map/ppermute | solution.py:520
  61.9 1.3 %collective-permute-start.15 = (bf16[336,128]{1,0:T(8,128)(2,1)S(1)}, bf16[336,128]{1,0:T(8,128)(2,1)S(1)}, u32[]{:S(2)}, u32[]{:S(2)}) collective-permute-start(bf16[336,128]{1,0:T(8,128)(2,1)S(1)} %collective-permute-done.11.rest_2_), channel_id=1, source_target_pairs={{0,1},{1,0},{2,3},{3,2},{4,5},{5,4},{6,7},{7,6},{8,9},{9,8},{10,11... | collective-permute-start | bytes 258056 | tf_op jit(solution)/shard_map/ppermute | solution.py:520
  61.9 1.4 %collective-permute-start.14 = (bf16[336,128]{1,0:T(8,128)(2,1)S(1)}, bf16[336,128]{1,0:T(8,128)(2,1)S(1)}, u32[]{:S(2)}, u32[]{:S(2)}) collective-permute-start(bf16[336,128]{1,0:T(8,128)(2,1)S(1)} %collective-permute-done.10.rest_1_), channel_id=1, source_target_pairs={{0,1},{1,0},{2,3},{3,2},{4,5},{5,4},{6,7},{7,6},{8,9},{9,8},{10,11... | collective-permute-start | bytes 258056 | tf_op jit(solution)/shard_map/ppermute | solution.py:520
  65.9 6.5 %collective-permute-start.17 = (bf16[32,1536]{1,0:T(8,128)(2,1)S(1)}, bf16[32,1536]{1,0:T(8,128)(2,1)S(1)}, u32[]{:S(2)}, u32[]{:S(2)}) collective-permute-start(bf16[32,1536]{1,0:T(8,128)(2,1)S(1)} %get-tuple-element.60), channel_id=1, source_target_pairs={{0,2},{2,0},{4,6},{6,4},{1,3},{3,1},{5,7},{7,5},{8,10},{10,8},{12,... | collective-permute-start | bytes 294920 | tf_op jit(solution)/shard_map/ppermute | solution.py:520
  66.2 8.8 %collective-permute-start.18 = (bf16[32,1536]{1,0:T(8,128)(2,1)S(1)}, bf16[32,1536]{1,0:T(8,128)(2,1)S(1)}, u32[]{:S(2)}, u32[]{:S(2)}) collective-permute-start(bf16[32,1536]{1,0:T(8,128)(2,1)S(1)} %get-tuple-element.61), channel_id=1, source_target_pairs={{0,4},{2,6},{4,0},{6,2},{1,5},{3,7},{5,1},{7,3},{8,12},{10,14},{12... | collective-permute-start | bytes 294920 | tf_op jit(solution)/shard_map/ppermute | solution.py:520
  67.8 7.2 %collective-permute-start.19 = (bf16[32,1536]{1,0:T(8,128)(2,1)S(1)}, bf16[32,1536]{1,0:T(8,128)(2,1)S(1)}, u32[]{:S(2)}, u32[]{:S(2)}) collective-permute-start(bf16[32,1536]{1,0:T(8,128)(2,1)S(1)} %get-tuple-element.62), channel_id=1, source_target_pairs={{0,6},{2,4},{4,2},{6,0},{1,7},{3,5},{5,3},{7,1},{8,14},{10,12},{12... | collective-permute-start | bytes 294920 | tf_op jit(solution)/shard_map/ppermute | solution.py:520
  70.6 5.7 %collective-permute-start.20 = (bf16[32,1536]{1,0:T(8,128)(2,1)S(1)}, bf16[32,1536]{1,0:T(8,128)(2,1)S(1)}, u32[]{:S(2)}, u32[]{:S(2)}) collective-permute-start(bf16[32,1536]{1,0:T(8,128)(2,1)S(1)} %get-tuple-element.66), channel_id=1, source_target_pairs={{0,2},{2,0},{4,6},{6,4},{1,3},{3,1},{5,7},{7,5},{8,10},{10,8},{12,... | collective-permute-start | bytes 294920 | tf_op jit(solution)/shard_map/ppermute | solution.py:520
  70.9 6.4 %collective-permute-start.21 = (bf16[32,1536]{1,0:T(8,128)(2,1)S(1)}, bf16[32,1536]{1,0:T(8,128)(2,1)S(1)}, u32[]{:S(2)}, u32[]{:S(2)}) collective-permute-start(bf16[32,1536]{1,0:T(8,128)(2,1)S(1)} %get-tuple-element.67), channel_id=1, source_target_pairs={{0,4},{2,6},{4,0},{6,2},{1,5},{3,7},{5,1},{7,3},{8,12},{10,14},{12... | collective-permute-start | bytes 294920 | tf_op jit(solution)/shard_map/ppermute | solution.py:520
  72.5 5.9 %collective-permute-start.22 = (bf16[32,1536]{1,0:T(8,128)(2,1)S(1)}, bf16[32,1536]{1,0:T(8,128)(2,1)S(1)}, u32[]{:S(2)}, u32[]{:S(2)}) collective-permute-start(bf16[32,1536]{1,0:T(8,128)(2,1)S(1)} %get-tuple-element.68), channel_id=1, source_target_pairs={{0,6},{2,4},{4,2},{6,0},{1,7},{3,5},{5,3},{7,1},{8,14},{10,12},{12... | collective-permute-start | bytes 294920 | tf_op jit(solution)/shard_map/ppermute | solution.py:520
where the time goes:
time: 80.4 us; the launch traced here: 80.2 us
  starting transfers between devices  30.3 us (38%)
  waiting for transfers between devices  26.1 us (32%)
  Pallas kernels  22 us (27%)
  between operations  0.9 us (1%)
    pallas_call x10, Pallas kernels, call(): pl.pallas_call(kernel, out_shape=outs, in_specs=specs, out_specs=[leave]...  22 us
    ppermute x13, starting transfers between devices, met(): lax.ppermute(block, axis, [(i, offset(i, step, n)) for i in range(n)])  12.1 us
    ppermute x13, waiting for transfers between devices, met(): lax.ppermute(block, axis, [(i, offset(i, step, n)) for i in range(n)])  11.8 us
    ppermute x4, starting transfers between devices, swapped(): lax.ppermute(b, axis, route)  6.87 us
    ppermute x3, starting transfers between devices, sideways(): far_rim = lax.ppermute(blocks[1], ('yx', 'core'), odd)  6.83 us
    ppermute x3, waiting for transfers between devices, sideways(): far_rim = lax.ppermute(blocks[1], ('yx', 'core'), odd)  6.6 us
    ppermute x4, waiting for transfers between devices, swapped(): lax.ppermute(b, axis, route)  6.47 us
    all_to_all x1, starting transfers between devices, shards(): shared = lax.all_to_all(shared, ('row', 'core'), 0, 0, tiled=True)  3.74 us
  transfers between devices with their start and end apart: 24, of which 14 were waited for; matrix products, arithmetic and copies ran while one was open for 1% of the time, Pallas kernels for 3%

commit v1 on v0

--- a/solution.py
+++ b/solution.py
@@ -149,14 +149,14 @@
 
     shape = (channels * height, z.cell)
     line, entry = iota(shape, 0), iota(shape, 1)
-    channel, image_row = line // height, line % height
+    channel, image_row = lax.div(line, height), lax.rem(line, height)
     away = (
-        (channel * STRIDE + image_row % STRIDE) * STRIDE
-        + image_row // STRIDE * z.cell
-        - entry // STRIDE * STRIDE
+        (channel * STRIDE + lax.rem(image_row, STRIDE)) * STRIDE
+        + lax.div(image_row, STRIDE) * z.cell
+        - lax.div(entry, STRIDE) * STRIDE
     )
     shape = (width, z.cell)
-    mine = (iota(shape, 0) % STRIDE == iota(shape, 1) % STRIDE).astype(F32)
+    mine = (lax.rem(iota(shape, 0), STRIDE) == lax.rem(iota(shape, 1), STRIDE)).astype(F32)
     for i in range(z.rows):
         moved = jnp.dot(
             spread[...], is_equal(away, i * z.cell), preferred_element_type=F32
@@ -268,19 +268,32 @@
     send_sides(z, place, own, sends)
 
 
-def sort_kernel(z, groups, where, codes, _, shared):
+def sort_kernel(z, grid, groups, where, codes, _, mine, other):
     rows_n, cores_n, owned = groups
     span = z.atoms // rows_n
     src = lax.broadcasted_iota(jnp.int32, (span, span), 0)
     dst = lax.broadcasted_iota(jnp.int32, (span, span), 1)
     per_core = span // cores_n
-    core, rem = dst // per_core, dst % per_core
-    wanted = (rem // owned) * (owned * cores_n) + core * owned + rem % owned
+    core, rem = lax.div(dst, per_core), lax.rem(dst, per_core)
+    wanted = lax.div(rem, owned) * (owned * cores_n) + core * owned + lax.rem(rem, owned)
     order = is_equal(src, wanted)
+    place = Place(where, *grid)
     for r in range(rows_n):
         line = jnp.dot(codes[:, r * span : (r + 1) * span], order, preferred_element_type=F32)
+        halves = [line[:, k * per_core : (k + 1) * per_core].astype(BF16) for k in range(cores_n)]
+        step = place.row ^ r if rows_n & (rows_n - 1) == 0 else (place.row - r) % rows_n
         for k in range(cores_n):
-            shared[r * cores_n + k] = line[:, k * per_core : (k + 1) * per_core].astype(BF16)
+
+            @pl.when(place.col % 2 == k)
+            def _(k=k, halves=halves, step=step):
+                mine[step] = halves[k]
+                other[step] = halves[1 - k]
+
+
+def join_kernel(where, mine, other, *joint):
+    for step, out in enumerate(joint):
+        out[0] = mine[step + 1]
+        out[1] = other[step + 1]
 
 
 def pack_kernel(z, grid, where, own, from_even, from_odd, packed, joined, flat):
@@ -318,9 +331,10 @@
         out[...] = partial[pl.ds(pl.multiple_of(at * owned, owned), owned), :]
 
 
-def learn_kernel(z, grid, groups, yx_n, where, shared, *rest):
+def learn_kernel(z, grid, groups, yx_n, where, first_near, first_far, *rest):
     rows_n, cores_n, _ = groups
     members = rows_n * cores_n
+    met, rest = rest[: rows_n - 1], rest[rows_n - 1 :]
     near, far, outs = rest[:rows_n], rest[rows_n : 2 * rows_n], rest[2 * rows_n :]
     outs, (across, wide_part, partial, flat, whole, codes) = outs[:yx_n], outs[yx_n:]
     stride = members * z.cols
@@ -337,6 +351,15 @@
             ends = block[z.packed :, :].astype(F32)
             flat[k, d, 0:half, 128 : z.cell] = ends[:, 0:tail]
             flat[k, d, half:, 128 : z.cell] = ends[:, tail : 2 * tail]
+            own_core = block is near[x]
+            for i in range(z.rows):
+                sites = slice(i * z.cols, (i + 1) * z.cols)
+                if x == 0:
+                    lines = (first_near if own_core else first_far)[0, sites, :]
+                else:
+                    lines = met[x - 1][0 if own_core else 1, sites, :]
+                at = i * stride + (d * cores_n + k) * z.cols
+                codes[pl.ds(pl.multiple_of(at, z.cols), z.cols), :] = lines
     for k in range(cores_n):
         for r in range(rows_n):
             d = r * cores_n + k
@@ -363,10 +386,6 @@
                     for c in range(MARGIN):
                         whole[at : at + n, z.cols + c, :] += side[c]
             windows_of(z, whole, wide_part, d * z.cols, stride)
-            for i in range(z.rows):
-                codes[i * stride + d * z.cols : i * stride + (d + 1) * z.cols, :] = shared[
-                    d, i * z.cols : (i + 1) * z.cols, :
-                ]
     across[...] = codes[...].astype(F32).T.astype(BF16)
     learn_half(
         z, grid, where, across[...], wide_part, stride, range(SPAN // 2), outs, partial
@@ -441,6 +460,9 @@
     members = rows_n * cores_n
     grid = (rows_n, cols_n)
     where = jnp.stack([lax.axis_index("row"), lax.axis_index(("yx", "core"))]).astype(jnp.int32)
+
+    def met(block, axis, n, step):
+        return lax.ppermute(block, axis, [(i, offset(i, step, n)) for i in range(n)])
 
     def swapped(axis, n, blocks):
         return [lax.ppermute(b, axis, route) for b, route in zip(blocks, partners(n))]
@@ -502,13 +524,25 @@
         sides = rest[:2]
     final_codes = potential.reshape(membrane.shape)
     sides = sideways(sides)
-    (shared,) = call(
-        functools.partial(sort_kernel, z, groups),
-        [pltpu.VMEM((members, z.sites, atom_count // members), BF16)],
+    codes_v = pltpu.VMEM((rows_n, z.sites, atom_count // members), BF16)
+    mine, other = call(
+        functools.partial(sort_kernel, z, grid, groups),
+        [codes_v, codes_v],
         (where, rest[2], sides[0]),
         [],
     )
-    shared = lax.all_to_all(shared, ("row", "core"), 0, 0, tiled=True)
+    other = met(other, "core", 2, 1)
+    joint = call(
+        join_kernel,
+        [pltpu.VMEM((2,) + codes_v.shape[1:], BF16)] * (rows_n - 1),
+        (where, mine, other),
+        [],
+    )
+    power = rows_n & (rows_n - 1) == 0
+    joint = [
+        met(block, "row", rows_n, x if power else rows_n - x)
+        for x, block in enumerate(joint, 1)
+    ]
     (packed,) = call(
         functools.partial(pack_kernel, z, grid),
         [pltpu.VMEM((z.packed * 3 // 2, 128), BF16)],
@@ -516,12 +550,9 @@
         [own_v, flat_v],
     )
 
-    def met(block, axis, n, step):
-        return lax.ppermute(block, axis, [(i, offset(i, step, n)) for i in range(n)])
-
-    power = rows_n & (rows_n - 1) == 0
     near = [packed] + [
-        met(packed, "row", rows_n, x if power else rows_n - x) for x in range(1, rows_n)
+        met(packed, "row", rows_n, x if power else rows_n - x)
+        for x in range(1, rows_n)
     ]
     far = [met(block, "core", 2, 1) for block in near]
     stride = members * z.cols
@@ -535,7 +566,7 @@
             pltpu.VMEM((group_atoms, members * z.sites), BF16),
             pltpu.VMEM((z.tall * stride, z.band), BF16),
         ],
-        (where, shared, *near, *far),
+        (where, mine, other, *joint, *near, *far),
         [
             partial_v,
             pltpu.VMEM((cores_n, rows_n, z.packed, z.lanes), F32),

time: 80.4 us -> 80.7 us (level)
    ppermute x13 -> x17, starting transfers between devices: 12.1 us -> 16.6 us  [met(): lax.ppermute(block, axis, [(i, offset(i, step, n)) for i in range(n)])]
    all_to_all x1 -> x0, starting transfers between devices: 3.74 us -> none  [shards(): shared = lax.all_to_all(shared, ('row', 'core'), 0, 0, tiled=True)]
    ppermute x3, waiting for transfers between devices: 1.19 us -> 0.01 us  [sideways(): near_rim = lax.ppermute(blocks[0], ('yx', 'core'), even)]
    ppermute x13 -> x17, waiting for transfers between devices: 11.8 us -> 12.3 us  [met(): lax.ppermute(block, axis, [(i, offset(i, step, n)) for i in range(n)])]
    pallas_call x10 -> x11, Pallas kernels: 22 us -> 22.4 us  [call(): pl.pallas_call(kernel, out_shape=outs, in_specs=specs, out_specs=[leave]...]
  transfers between devices with their start and end apart: 24 -> 27, of which waited for: 14 -> 15; matrix products, arithmetic and copies ran while one was open for 1% -> 1% of each run, Pallas kernels for 3% -> 4%
where the time goes in v1:
time: 80.7 us; the launch traced here: 80.6 us
  starting transfers between devices  31 us (38%)
  waiting for transfers between devices  25.4 us (31%)
  Pallas kernels  22.4 us (28%)
  between operations  0.93 us (1%)
    pallas_call x11, Pallas kernels, call(): pl.pallas_call(kernel, out_shape=outs, in_specs=specs, out_specs=[leave]...  22.4 us
    ppermute x17, starting transfers between devices, met(): lax.ppermute(block, axis, [(i, offset(i, step, n)) for i in range(n)])  16.6 us
    ppermute x17, waiting for transfers between devices, met(): lax.ppermute(block, axis, [(i, offset(i, step, n)) for i in range(n)])  12.3 us
    ppermute x4, starting transfers between devices, swapped(): lax.ppermute(b, axis, route)  6.87 us
    ppermute x3, starting transfers between devices, sideways(): far_rim = lax.ppermute(blocks[1], ('yx', 'core'), odd)  6.84 us
    ppermute x3, waiting for transfers between devices, sideways(): far_rim = lax.ppermute(blocks[1], ('yx', 'core'), odd)  6.65 us
    ppermute x4, waiting for transfers between devices, swapped(): lax.ppermute(b, axis, route)  6.48 us
  transfers between devices with their start and end apart: 27, of which 15 were waited for; matrix products, arithmetic and copies ran while one was open for 1% of the time, Pallas kernels for 4%

profile of v1, /device:TPU:0, one launch (start us, length us, event | category | flops | bytes accessed | tf_op | source)
XLA Modules:
  0.0 80.6 jit_solution(4775372062436482609)
XLA Ops:
  0.7 4.4 %shard_map.67 = (f32[11,24,256]{2,1,0:T(8,128)S(1)}, bf16[3,16,256]{2,1,0:T(8,128)(2,1)S(1)}, bf16[3,16,256]{2,1,0:T(8,128)(2,1)S(1)}, f32[128,192]{1,0:T(8,128)...) custom-call(s32[2]{0:T(128)S(1)} %pad_add_fusion.where, ...), custom_call_target="tpu_custom_call" | custom-call | tf_op jit(solution)/shard_map/pallas_call | solution.py:443
  5.7 3.5 %collective-permute-start.1 = (bf16[3,16,256]{2,1,0:T(8,128)(2,1)S(1)}, bf16[3,16,256]{2,1,0:T(8,128)(2,1)S(1)}, u32[]{:S(2)}, u32[]{:S(2)}) collective-permute-start(bf16[3,16,256]{2,1,0:T(8,128)(2,1)S(1)} %get-tuple-element.45), channel_id=1, source_target_pairs={{0,7},{1,2},{2,1},{3,4},{4,3},{5,6},{6,5},{7,0},{8,15},{9,10},{10,... | collective-permute-start | bytes 73736 | tf_op jit(solution)/shard_map/ppermute | solution.py:473
  9.2 1.5 %collective-permute-done.1.from_odd = bf16[3,16,256]{2,1,0:T(8,128)(2,1)S(1)} collective-permute-done((bf16[3,16,256]{2,1,0:T(8,128)(2,1)S(1)}, bf16[3,16,256]{2,1,0:T(8,128)(2,1)S(1)}, u32[]{:S(2)}, u32[]{:S(2)}) %collective-permute-start.1) | collective-permute-done | bytes 24608 | tf_op jit(solution)/shard_map/ppermute | solution.py:473
  11.4 1.8 %collective-permute-start.2 = (bf16[64,256]{1,0:T(8,128)(2,1)S(1)}, bf16[64,256]{1,0:T(8,128)(2,1)S(1)}, u32[]{:S(2)}, u32[]{:S(2)}) collective-permute-start(bf16[64,256]{1,0:T(8,128)(2,1)S(1)} %get-tuple-element.47), channel_id=1, source_target_pairs={{0,8},{8,0},{16,24},{24,16},{1,9},{9,1},{17,25},{25,17},{2,10},{10... | collective-permute-start | bytes 98312 | tf_op jit(solution)/shard_map/ppermute | solution.py:468
  13.2 2.5 %collective-permute-start.3 = (bf16[64,256]{1,0:T(8,128)(2,1)S(1)}, bf16[64,256]{1,0:T(8,128)(2,1)S(1)}, u32[]{:S(2)}, u32[]{:S(2)}) collective-permute-start(bf16[64,256]{1,0:T(8,128)(2,1)S(1)} %get-tuple-element.48), channel_id=1, source_target_pairs={{0,24},{8,16},{16,8},{24,0},{1,25},{9,17},{17,9},{25,1},{2,26},{10... | collective-permute-start | bytes 98312 | tf_op jit(solution)/shard_map/ppermute | solution.py:468
  15.6 3.2 %collective-permute-done.3.from_odd = bf16[64,256]{1,0:T(8,128)(2,1)S(1)} collective-permute-done((bf16[64,256]{1,0:T(8,128)(2,1)S(1)}, bf16[64,256]{1,0:T(8,128)(2,1)S(1)}, u32[]{:S(2)}, u32[]{:S(2)}) %collective-permute-start.3) | collective-permute-done | bytes 32800 | tf_op jit(solution)/shard_map/ppermute | solution.py:468
  18.9 4.3 %shard_map.69 = (f32[128,1024]{1,0:T(8,128)S(1)}, f32[11,24,256]{2,1,0:T(8,128)S(1)}, bf16[3,16,256]{2,1,0:T(8,128)(2,1)S(1)}, bf16[3,16,256]{2,1,0:T(8,128)(2,1)S(1)}) custom-call(s32[2]{0:T(128)S(1)} %pad_add_fusion.where, f32[128,1024]{1,0:T(8,128)S(1)} %get-tuple-element.42.potential, f32[11,24,256]{2,1,0:T(8,128)S(1)} %get-tuple-element.46.joined, ...), custom_call_target="tpu_custom_call" | custom-call | tf_op jit(solution)/shard_map/pallas_call | solution.py:443
  23.3 2.0 %collective-permute-start.5 = (bf16[3,16,256]{2,1,0:T(8,128)(2,1)S(1)}, bf16[3,16,256]{2,1,0:T(8,128)(2,1)S(1)}, u32[]{:S(2)}, u32[]{:S(2)}) collective-permute-start(bf16[3,16,256]{2,1,0:T(8,128)(2,1)S(1)} %get-tuple-element.54), channel_id=1, source_target_pairs={{0,7},{1,2},{2,1},{3,4},{4,3},{5,6},{6,5},{7,0},{8,15},{9,10},{10,... | collective-permute-start | bytes 73736 | tf_op jit(solution)/shard_map/ppermute | solution.py:473
  25.3 2.2 %collective-permute-done.5.from_odd = bf16[3,16,256]{2,1,0:T(8,128)(2,1)S(1)} collective-permute-done((bf16[3,16,256]{2,1,0:T(8,128)(2,1)S(1)}, bf16[3,16,256]{2,1,0:T(8,128)(2,1)S(1)}, u32[]{:S(2)}, u32[]{:S(2)}) %collective-permute-start.5) | collective-permute-done | bytes 24608 | tf_op jit(solution)/shard_map/ppermute | solution.py:473
  28.2 2.5 %collective-permute-start.7 = (bf16[64,256]{1,0:T(8,128)(2,1)S(1)}, bf16[64,256]{1,0:T(8,128)(2,1)S(1)}, u32[]{:S(2)}, u32[]{:S(2)}) collective-permute-start(bf16[64,256]{1,0:T(8,128)(2,1)S(1)} %get-tuple-element.57), channel_id=1, source_target_pairs={{0,24},{8,16},{16,8},{24,0},{1,25},{9,17},{17,9},{25,1},{2,26},{10... | collective-permute-start | bytes 98312 | tf_op jit(solution)/shard_map/ppermute | solution.py:468
  30.8 1.4 %collective-permute-done.6.from_even = bf16[64,256]{1,0:T(8,128)(2,1)S(1)} collective-permute-done((bf16[64,256]{1,0:T(8,128)(2,1)S(1)}, bf16[64,256]{1,0:T(8,128)(2,1)S(1)}, u32[]{:S(2)}, u32[]{:S(2)}) %collective-permute-start.6) | collective-permute-done | bytes 32800 | tf_op jit(solution)/shard_map/ppermute | solution.py:468
  32.1 1.9 %collective-permute-done.7.from_odd = bf16[64,256]{1,0:T(8,128)(2,1)S(1)} collective-permute-done((bf16[64,256]{1,0:T(8,128)(2,1)S(1)}, bf16[64,256]{1,0:T(8,128)(2,1)S(1)}, u32[]{:S(2)}, u32[]{:S(2)}) %collective-permute-start.7) | collective-permute-done | bytes 32800 | tf_op jit(solution)/shard_map/ppermute | solution.py:468
  34.0 4.3 %shard_map.71 = (f32[128,1024]{1,0:T(8,128)S(1)}, f32[11,24,256]{2,1,0:T(8,128)S(1)}, bf16[3,16,256]{2,1,0:T(8,128)(2,1)S(1)}, bf16[3,16,256]{2,1,0:T(8,128)(2,1)S(1)}, bf16[128,1024]{1,0:T(8,128)(2,1)S(1)}) custom-call(s32[2]{0:T(128)S(1)} %pad_add_fusion.where, f32[128,1024]{1,0:T(8,128)S(1)} %get-tuple-element.51.potential, ...), custom_call_target="tpu_custom_call" | custom-call | tf_op jit(solution)/shard_map/pallas_call | solution.py:443
  38.4 1.3 %collective-permute-start.13 = (bf16[3,16,256]{2,1,0:T(8,128)(2,1)S(1)}, bf16[3,16,256]{2,1,0:T(8,128)(2,1)S(1)}, u32[]{:S(2)}, u32[]{:S(2)}) collective-permute-start(bf16[3,16,256]{2,1,0:T(8,128)(2,1)S(1)} %get-tuple-element.68), channel_id=1, source_target_pairs={{0,7},{1,2},{2,1},{3,4},{4,3},{5,6},{6,5},{7,0},{8,15},{9,10},{10,... | collective-permute-start | bytes 73736 | tf_op jit(solution)/shard_map/ppermute | solution.py:473
  39.7 2.9 %collective-permute-done.13.from_odd = bf16[3,16,256]{2,1,0:T(8,128)(2,1)S(1)} collective-permute-done((bf16[3,16,256]{2,1,0:T(8,128)(2,1)S(1)}, bf16[3,16,256]{2,1,0:T(8,128)(2,1)S(1)}, u32[]{:S(2)}, u32[]{:S(2)}) %collective-permute-start.13) | collective-permute-done | bytes 24608 | tf_op jit(solution)/shard_map/ppermute | solution.py:473
  43.3 2.5 %collective-permute-start.16 = (bf16[336,128]{1,0:T(8,128)(2,1)S(1)}, bf16[336,128]{1,0:T(8,128)(2,1)S(1)}, u32[]{:S(2)}, u32[]{:S(2)}) collective-permute-start(bf16[336,128]{1,0:T(8,128)(2,1)S(1)} %shard_map.74.rest_3_), channel_id=1, source_target_pairs={{0,24},{8,16},{16,8},{24,0},{1,25},{9,17},{17,9},{25,1},{2,26},{10... | collective-permute-start | bytes 258056 | tf_op jit(solution)/shard_map/ppermute | solution.py:465
  45.9 1.5 %shard_map.72 = (bf16[4,128,128]{2,1,0:T(8,128)(2,1)S(1)}, bf16[4,128,128]{2,1,0:T(8,128)(2,1)S(1)}) custom-call(s32[2]{0:T(128)S(1)} %pad_add_fusion.where, bf16[128,1024]{1,0:T(8,128)(2,1)S(1)} %get-tuple-element.60.codes, bf16[3,16,256]{2,1,0:T(8,128)(2,1)S(1)} %collective-permute-done.8._.from_even), custom_call_target="tpu_custom_call" | custom-call | tf_op jit(solution)/shard_map/pallas_call | solution.py:443
  47.5 1.9 %collective-permute-start.14 = (bf16[336,128]{1,0:T(8,128)(2,1)S(1)}, bf16[336,128]{1,0:T(8,128)(2,1)S(1)}, u32[]{:S(2)}, u32[]{:S(2)}) collective-permute-start(bf16[336,128]{1,0:T(8,128)(2,1)S(1)} %shard_map.74.rest_3_), channel_id=1, source_target_pairs={{0,8},{8,0},{16,24},{24,16},{1,9},{9,1},{17,25},{25,17},{2,10},{10... | collective-permute-start | bytes 258056 | tf_op jit(solution)/shard_map/ppermute | solution.py:465
  49.9 4.0 %collective-permute-done.15.rest_5_ = bf16[336,128]{1,0:T(8,128)(2,1)S(1)} collective-permute-done((bf16[336,128]{1,0:T(8,128)(2,1)S(1)}, bf16[336,128]{1,0:T(8,128)(2,1)S(1)}, u32[]{:S(2)}, u32[]{:S(2)}) %collective-permute-start.15) | collective-permute-done | bytes 86048 | tf_op jit(solution)/shard_map/ppermute | solution.py:465
  55.1 3.0 %collective-permute-start.11 = (bf16[2,128,128]{2,1,0:T(8,128)(2,1)S(1)}, bf16[2,128,128]{2,1,0:T(8,128)(2,1)S(1)}, u32[]{:S(2)}, u32[]{:S(2)}) collective-permute-start(bf16[2,128,128]{2,1,0:T(8,128)(2,1)S(1)} %get-tuple-element.65), channel_id=1, source_target_pairs={{0,16},{8,24},{16,0},{24,8},{1,17},{9,25},{17,1},{25,9},{2,18},{10... | collective-permute-start | bytes 196616 | tf_op jit(solution)/shard_map/ppermute | solution.py:465
  58.1 1.4 %collective-permute-start.12 = (bf16[2,128,128]{2,1,0:T(8,128)(2,1)S(1)}, bf16[2,128,128]{2,1,0:T(8,128)(2,1)S(1)}, u32[]{:S(2)}, u32[]{:S(2)}) collective-permute-start(bf16[2,128,128]{2,1,0:T(8,128)(2,1)S(1)} %get-tuple-element.66), channel_id=1, source_target_pairs={{0,24},{8,16},{16,8},{24,0},{1,25},{9,17},{17,9},{25,1},{2,26},{10... | collective-permute-start | bytes 196616 | tf_op jit(solution)/shard_map/ppermute | solution.py:465
  59.5 1.0 %collective-permute-done.10.rest_0_ = bf16[2,128,128]{2,1,0:T(8,128)(2,1)S(1)} collective-permute-done((bf16[2,128,128]{2,1,0:T(8,128)(2,1)S(1)}, bf16[2,128,128]{2,1,0:T(8,128)(2,1)S(1)}, u32[]{:S(2)}, u32[]{:S(2)}) %collective-permute-start.10) | collective-permute-done | bytes 65568 | tf_op jit(solution)/shard_map/ppermute | solution.py:465
  60.5 1.6 %collective-permute-done.11.rest_1_ = bf16[2,128,128]{2,1,0:T(8,128)(2,1)S(1)} collective-permute-done((bf16[2,128,128]{2,1,0:T(8,128)(2,1)S(1)}, bf16[2,128,128]{2,1,0:T(8,128)(2,1)S(1)}, u32[]{:S(2)}, u32[]{:S(2)}) %collective-permute-start.11) | collective-permute-done | bytes 65568 | tf_op jit(solution)/shard_map/ppermute | solution.py:465
  62.0 2.2 %collective-permute-done.12.rest_2_ = bf16[2,128,128]{2,1,0:T(8,128)(2,1)S(1)} collective-permute-done((bf16[2,128,128]{2,1,0:T(8,128)(2,1)S(1)}, bf16[2,128,128]{2,1,0:T(8,128)(2,1)S(1)}, u32[]{:S(2)}, u32[]{:S(2)}) %collective-permute-start.12) | collective-permute-done | bytes 65568 | tf_op jit(solution)/shard_map/ppermute | solution.py:465
  64.3 2.6 %shard_map.75 = (bf16[32,1536]{1,0:T(8,128)(2,1)S(1)}, bf16[32,1536]{1,0:T(8,128)(2,1)S(1)}, bf16[32,1536]{1,0:T(8,128)(2,1)S(1)}, bf16[32,1536]{1,0:T(8,128)(2,...) custom-call(s32[2]{0:T(128)S(1)} %pad_add_fusion.where, ...), custom_call_target="tpu_custom_call" | custom-call | tf_op jit(solution)/shard_map/pallas_call | solution.py:443
  66.9 1.6 %collective-permute-start.22 = (bf16[32,1536]{1,0:T(8,128)(2,1)S(1)}, bf16[32,1536]{1,0:T(8,128)(2,1)S(1)}, u32[]{:S(2)}, u32[]{:S(2)}) collective-permute-start(bf16[32,1536]{1,0:T(8,128)(2,1)S(1)} %get-tuple-element.71), channel_id=1, source_target_pairs={{0,4},{2,6},{4,0},{6,2},{1,5},{3,7},{5,1},{7,3},{8,12},{10,14},{12... | collective-permute-start | bytes 294920 | tf_op jit(solution)/shard_map/ppermute | solution.py:465
  68.6 1.8 %collective-permute-start.23 = (bf16[32,1536]{1,0:T(8,128)(2,1)S(1)}, bf16[32,1536]{1,0:T(8,128)(2,1)S(1)}, u32[]{:S(2)}, u32[]{:S(2)}) collective-permute-start(bf16[32,1536]{1,0:T(8,128)(2,1)S(1)} %get-tuple-element.72), channel_id=1, source_target_pairs={{0,6},{2,4},{4,2},{6,0},{1,7},{3,5},{5,3},{7,1},{8,14},{10,12},{12... | collective-permute-start | bytes 294920 | tf_op jit(solution)/shard_map/ppermute | solution.py:465
  70.4 1.1 %shard_map.76 = (bf16[32,1536]{1,0:T(8,128)(2,1)S(1)}, bf16[32,1536]{1,0:T(8,128)(2,1)S(1)}, bf16[32,1536]{1,0:T(8,128)(2,1)S(1)}, bf16[32,1536]{1,0:T(8,128)(2,1)S(1)}) custom-call(s32[2]{0:T(128)S(1)} %pad_add_fusion.where, bf16[128,1024]{1,0:T(8,128)(2,1)S(1)} %get-tuple-element.73.across, bf16[1408,768]{1,0:T(8,128)(2,1)S(1)} %get-tuple-element.74.wide_part), custom_call_target="tpu_custom_call" | custom-call | tf_op jit(solution)/shard_map/pallas_call | solution.py:443
  71.7 1.5 %collective-permute-start.25 = (bf16[32,1536]{1,0:T(8,128)(2,1)S(1)}, bf16[32,1536]{1,0:T(8,128)(2,1)S(1)}, u32[]{:S(2)}, u32[]{:S(2)}) collective-permute-start(bf16[32,1536]{1,0:T(8,128)(2,1)S(1)} %get-tuple-element.77), channel_id=1, source_target_pairs={{0,4},{2,6},{4,0},{6,2},{1,5},{3,7},{5,1},{7,3},{8,12},{10,14},{12... | collective-permute-start | bytes 294920 | tf_op jit(solution)/shard_map/ppermute | solution.py:465
  73.3 1.8 %collective-permute-start.26 = (bf16[32,1536]{1,0:T(8,128)(2,1)S(1)}, bf16[32,1536]{1,0:T(8,128)(2,1)S(1)}, u32[]{:S(2)}, u32[]{:S(2)}) collective-permute-start(bf16[32,1536]{1,0:T(8,128)(2,1)S(1)} %get-tuple-element.78), channel_id=1, source_target_pairs={{0,6},{2,4},{4,2},{6,0},{1,7},{3,5},{5,3},{7,1},{8,14},{10,12},{12... | collective-permute-start | bytes 294920 | tf_op jit(solution)/shard_map/ppermute | solution.py:465
  77.0 1.8 %collective-permute-done.26.rest_7_ = bf16[32,1536]{1,0:T(8,128)(2,1)S(1)} collective-permute-done((bf16[32,1536]{1,0:T(8,128)(2,1)S(1)}, bf16[32,1536]{1,0:T(8,128)(2,1)S(1)}, u32[]{:S(2)}, u32[]{:S(2)}) %collective-permute-start.26) | collective-permute-done | bytes 98336 | tf_op jit(solution)/shard_map/ppermute | solution.py:465
  78.8 1.6 %shard_map.77 = (f32[32,3072]{1,0:T(8,128)}, f32[32,3072]{1,0:T(8,128)}) custom-call(s32[2]{0:T(128)S(1)} %pad_add_fusion.where, f32[32,3072]{1,0:T(8,128)S(1)} %copy-done, bf16[32,3072]{1,0:T(8,128)(2,1)S(1)} %get-tuple-element.59.atoms, bf16[32,1536]{1,0:T(8,128)(2,1)S(1)} %get-tuple-element.69.rest_0_, ...), custom_call_target="tpu_custom_call" | custom-call | tf_op jit(solution)/shard_map/pallas_call | solution.py:443
  (37 shorter events, 6.8 us)
Async XLA Ops:
  5.1 4.1 %collective-permute-start = (bf16[3,16,256]{2,1,0:T(8,128)(2,1)S(1)}, bf16[3,16,256]{2,1,0:T(8,128)(2,1)S(1)}, u32[]{:S(2)}, u32[]{:S(2)}) collective-permute-start(bf16[3,16,256]{2,1,0:T(8,128)(2,1)S(1)} %get-tuple-element.44), channel_id=1, source_target_pairs={{0,1},{1,0},{2,3},{3,2},{4,5},{5,4},{6,7},{7,6},{8,9},{9,8},{10,11... | collective-permute-start | bytes 73736 | tf_op jit(solution)/shard_map/ppermute | solution.py:472
  5.7 5.1 %collective-permute-start.1 = (bf16[3,16,256]{2,1,0:T(8,128)(2,1)S(1)}, bf16[3,16,256]{2,1,0:T(8,128)(2,1)S(1)}, u32[]{:S(2)}, u32[]{:S(2)}) collective-permute-start(bf16[3,16,256]{2,1,0:T(8,128)(2,1)S(1)} %get-tuple-element.45), channel_id=1, source_target_pairs={{0,7},{1,2},{2,1},{3,4},{4,3},{5,6},{6,5},{7,0},{8,15},{9,10},{10,... | collective-permute-start | bytes 73736 | tf_op jit(solution)/shard_map/ppermute | solution.py:473
  11.4 4.3 %collective-permute-start.2 = (bf16[64,256]{1,0:T(8,128)(2,1)S(1)}, bf16[64,256]{1,0:T(8,128)(2,1)S(1)}, u32[]{:S(2)}, u32[]{:S(2)}) collective-permute-start(bf16[64,256]{1,0:T(8,128)(2,1)S(1)} %get-tuple-element.47), channel_id=1, source_target_pairs={{0,8},{8,0},{16,24},{24,16},{1,9},{9,1},{17,25},{25,17},{2,10},{10... | collective-permute-start | bytes 98312 | tf_op jit(solution)/shard_map/ppermute | solution.py:468
  13.2 5.7 %collective-permute-start.3 = (bf16[64,256]{1,0:T(8,128)(2,1)S(1)}, bf16[64,256]{1,0:T(8,128)(2,1)S(1)}, u32[]{:S(2)}, u32[]{:S(2)}) collective-permute-start(bf16[64,256]{1,0:T(8,128)(2,1)S(1)} %get-tuple-element.48), channel_id=1, source_target_pairs={{0,24},{8,16},{16,8},{24,0},{1,25},{9,17},{17,9},{25,1},{2,26},{10... | collective-permute-start | bytes 98312 | tf_op jit(solution)/shard_map/ppermute | solution.py:468
  23.2 2.1 %collective-permute-start.4 = (bf16[3,16,256]{2,1,0:T(8,128)(2,1)S(1)}, bf16[3,16,256]{2,1,0:T(8,128)(2,1)S(1)}, u32[]{:S(2)}, u32[]{:S(2)}) collective-permute-start(bf16[3,16,256]{2,1,0:T(8,128)(2,1)S(1)} %get-tuple-element.53), channel_id=1, source_target_pairs={{0,1},{1,0},{2,3},{3,2},{4,5},{5,4},{6,7},{7,6},{8,9},{9,8},{10,11... | collective-permute-start | bytes 73736 | tf_op jit(solution)/shard_map/ppermute | solution.py:472
  23.3 4.2 %collective-permute-start.5 = (bf16[3,16,256]{2,1,0:T(8,128)(2,1)S(1)}, bf16[3,16,256]{2,1,0:T(8,128)(2,1)S(1)}, u32[]{:S(2)}, u32[]{:S(2)}) collective-permute-start(bf16[3,16,256]{2,1,0:T(8,128)(2,1)S(1)} %get-tuple-element.54), channel_id=1, source_target_pairs={{0,7},{1,2},{2,1},{3,4},{4,3},{5,6},{6,5},{7,0},{8,15},{9,10},{10,... | collective-permute-start | bytes 73736 | tf_op jit(solution)/shard_map/ppermute | solution.py:473
  28.1 4.0 %collective-permute-start.6 = (bf16[64,256]{1,0:T(8,128)(2,1)S(1)}, bf16[64,256]{1,0:T(8,128)(2,1)S(1)}, u32[]{:S(2)}, u32[]{:S(2)}) collective-permute-start(bf16[64,256]{1,0:T(8,128)(2,1)S(1)} %get-tuple-element.56), channel_id=1, source_target_pairs={{0,8},{8,0},{16,24},{24,16},{1,9},{9,1},{17,25},{25,17},{2,10},{10... | collective-permute-start | bytes 98312 | tf_op jit(solution)/shard_map/ppermute | solution.py:468
  28.2 5.8 %collective-permute-start.7 = (bf16[64,256]{1,0:T(8,128)(2,1)S(1)}, bf16[64,256]{1,0:T(8,128)(2,1)S(1)}, u32[]{:S(2)}, u32[]{:S(2)}) collective-permute-start(bf16[64,256]{1,0:T(8,128)(2,1)S(1)} %get-tuple-element.57), channel_id=1, source_target_pairs={{0,24},{8,16},{16,8},{24,0},{1,25},{9,17},{17,9},{25,1},{2,26},{10... | collective-permute-start | bytes 98312 | tf_op jit(solution)/shard_map/ppermute | solution.py:468
  34.0 44.8 %copy-start = (f32[32,3072]{1,0:T(8,128)S(1)}, f32[32,3072]{1,0:T(8,128)}, u32[]{:S(2)}) copy-start(f32[32,3072]{1,0:T(8,128)} %momentum.1) | copy-start | bytes 1179652
  38.4 1.4 %collective-permute-start.8 = (bf16[3,16,256]{2,1,0:T(8,128)(2,1)S(1)}, bf16[3,16,256]{2,1,0:T(8,128)(2,1)S(1)}, u32[]{:S(2)}, u32[]{:S(2)}) collective-permute-start(bf16[3,16,256]{2,1,0:T(8,128)(2,1)S(1)} %get-tuple-element.61), channel_id=1, source_target_pairs={{0,1},{1,0},{2,3},{3,2},{4,5},{5,4},{6,7},{7,6},{8,9},{9,8},{10,11... | collective-permute-start | bytes 73736 | tf_op jit(solution)/shard_map/ppermute | solution.py:472
  38.4 4.2 %collective-permute-start.13 = (bf16[3,16,256]{2,1,0:T(8,128)(2,1)S(1)}, bf16[3,16,256]{2,1,0:T(8,128)(2,1)S(1)}, u32[]{:S(2)}, u32[]{:S(2)}) collective-permute-start(bf16[3,16,256]{2,1,0:T(8,128)(2,1)S(1)} %get-tuple-element.68), channel_id=1, source_target_pairs={{0,7},{1,2},{2,1},{3,4},{4,3},{5,6},{6,5},{7,0},{8,15},{9,10},{10,... | collective-permute-start | bytes 73736 | tf_op jit(solution)/shard_map/ppermute | solution.py:473
  43.3 6.3 %collective-permute-start.16 = (bf16[336,128]{1,0:T(8,128)(2,1)S(1)}, bf16[336,128]{1,0:T(8,128)(2,1)S(1)}, u32[]{:S(2)}, u32[]{:S(2)}) collective-permute-start(bf16[336,128]{1,0:T(8,128)(2,1)S(1)} %shard_map.74.rest_3_), channel_id=1, source_target_pairs={{0,24},{8,16},{16,8},{24,0},{1,25},{9,17},{17,9},{25,1},{2,26},{10... | collective-permute-start | bytes 258056 | tf_op jit(solution)/shard_map/ppermute | solution.py:465
  47.3 7.1 %collective-permute-start.9 = (bf16[4,128,128]{2,1,0:T(8,128)(2,1)S(1)}, bf16[4,128,128]{2,1,0:T(8,128)(2,1)S(1)}, u32[]{:S(2)}, u32[]{:S(2)}) collective-permute-start(bf16[4,128,128]{2,1,0:T(8,128)(2,1)S(1)} %get-tuple-element.63), channel_id=1, source_target_pairs={{0,1},{1,0},{2,3},{3,2},{4,5},{5,4},{6,7},{7,6},{8,9},{9,8},{10,11... | collective-permute-start | bytes 393224 | tf_op jit(solution)/shard_map/ppermute | solution.py:465
  47.4 6.5 %collective-permute-start.15 = (bf16[336,128]{1,0:T(8,128)(2,1)S(1)}, bf16[336,128]{1,0:T(8,128)(2,1)S(1)}, u32[]{:S(2)}, u32[]{:S(2)}) collective-permute-start(bf16[336,128]{1,0:T(8,128)(2,1)S(1)} %shard_map.74.rest_3_), channel_id=1, source_target_pairs={{0,16},{8,24},{16,0},{24,8},{1,17},{9,25},{17,1},{25,9},{2,18},{10... | collective-permute-start | bytes 258056 | tf_op jit(solution)/shard_map/ppermute | solution.py:465
  47.5 6.7 %collective-permute-start.14 = (bf16[336,128]{1,0:T(8,128)(2,1)S(1)}, bf16[336,128]{1,0:T(8,128)(2,1)S(1)}, u32[]{:S(2)}, u32[]{:S(2)}) collective-permute-start(bf16[336,128]{1,0:T(8,128)(2,1)S(1)} %shard_map.74.rest_3_), channel_id=1, source_target_pairs={{0,8},{8,0},{16,24},{24,16},{1,9},{9,1},{17,25},{25,17},{2,10},{10... | collective-permute-start | bytes 258056 | tf_op jit(solution)/shard_map/ppermute | solution.py:465
  49.4 5.7 %collective-permute-start.17 = (bf16[336,128]{1,0:T(8,128)(2,1)S(1)}, bf16[336,128]{1,0:T(8,128)(2,1)S(1)}, u32[]{:S(2)}, u32[]{:S(2)}) collective-permute-start(bf16[336,128]{1,0:T(8,128)(2,1)S(1)} %shard_map.74.rest_3_), channel_id=1, source_target_pairs={{0,1},{1,0},{2,3},{3,2},{4,5},{5,4},{6,7},{7,6},{8,9},{9,8},{10,11... | collective-permute-start | bytes 258056 | tf_op jit(solution)/shard_map/ppermute | solution.py:465
  49.7 8.4 %collective-permute-start.20 = (bf16[336,128]{1,0:T(8,128)(2,1)S(1)}, bf16[336,128]{1,0:T(8,128)(2,1)S(1)}, u32[]{:S(2)}, u32[]{:S(2)}) collective-permute-start(bf16[336,128]{1,0:T(8,128)(2,1)S(1)} %collective-permute-done.16.rest_6_), channel_id=1, source_target_pairs={{0,1},{1,0},{2,3},{3,2},{4,5},{5,4},{6,7},{7,6},{8,9},{9,8},{10,11... | collective-permute-start | bytes 258056 | tf_op jit(solution)/shard_map/ppermute | solution.py:465
  53.9 5.5 %collective-permute-start.19 = (bf16[336,128]{1,0:T(8,128)(2,1)S(1)}, bf16[336,128]{1,0:T(8,128)(2,1)S(1)}, u32[]{:S(2)}, u32[]{:S(2)}) collective-permute-start(bf16[336,128]{1,0:T(8,128)(2,1)S(1)} %collective-permute-done.15.rest_5_), channel_id=1, source_target_pairs={{0,1},{1,0},{2,3},{3,2},{4,5},{5,4},{6,7},{7,6},{8,9},{9,8},{10,11... | collective-permute-start | bytes 258056 | tf_op jit(solution)/shard_map/ppermute | solution.py:465
  54.2 5.3 %collective-permute-start.18 = (bf16[336,128]{1,0:T(8,128)(2,1)S(1)}, bf16[336,128]{1,0:T(8,128)(2,1)S(1)}, u32[]{:S(2)}, u32[]{:S(2)}) collective-permute-start(bf16[336,128]{1,0:T(8,128)(2,1)S(1)} %collective-permute-done.14.rest_4_), channel_id=1, source_target_pairs={{0,1},{1,0},{2,3},{3,2},{4,5},{5,4},{6,7},{7,6},{8,9},{9,8},{10,11... | collective-permute-start | bytes 258056 | tf_op jit(solution)/shard_map/ppermute | solution.py:465
  55.0 5.5 %collective-permute-start.10 = (bf16[2,128,128]{2,1,0:T(8,128)(2,1)S(1)}, bf16[2,128,128]{2,1,0:T(8,128)(2,1)S(1)}, u32[]{:S(2)}, u32[]{:S(2)}) collective-permute-start(bf16[2,128,128]{2,1,0:T(8,128)(2,1)S(1)} %get-tuple-element.64), channel_id=1, source_target_pairs={{0,8},{8,0},{16,24},{24,16},{1,9},{9,1},{17,25},{25,17},{2,10},{10... | collective-permute-start | bytes 196616 | tf_op jit(solution)/shard_map/ppermute | solution.py:465
  55.1 6.9 %collective-permute-start.11 = (bf16[2,128,128]{2,1,0:T(8,128)(2,1)S(1)}, bf16[2,128,128]{2,1,0:T(8,128)(2,1)S(1)}, u32[]{:S(2)}, u32[]{:S(2)}) collective-permute-start(bf16[2,128,128]{2,1,0:T(8,128)(2,1)S(1)} %get-tuple-element.65), channel_id=1, source_target_pairs={{0,16},{8,24},{16,0},{24,8},{1,17},{9,25},{17,1},{25,9},{2,18},{10... | collective-permute-start | bytes 196616 | tf_op jit(solution)/shard_map/ppermute | solution.py:465
  58.1 6.2 %collective-permute-start.12 = (bf16[2,128,128]{2,1,0:T(8,128)(2,1)S(1)}, bf16[2,128,128]{2,1,0:T(8,128)(2,1)S(1)}, u32[]{:S(2)}, u32[]{:S(2)}) collective-permute-start(bf16[2,128,128]{2,1,0:T(8,128)(2,1)S(1)} %get-tuple-element.66), channel_id=1, source_target_pairs={{0,24},{8,16},{16,8},{24,0},{1,25},{9,17},{17,9},{25,1},{2,26},{10... | collective-permute-start | bytes 196616 | tf_op jit(solution)/shard_map/ppermute | solution.py:465
  66.8 6.5 %collective-permute-start.21 = (bf16[32,1536]{1,0:T(8,128)(2,1)S(1)}, bf16[32,1536]{1,0:T(8,128)(2,1)S(1)}, u32[]{:S(2)}, u32[]{:S(2)}) collective-permute-start(bf16[32,1536]{1,0:T(8,128)(2,1)S(1)} %get-tuple-element.70), channel_id=1, source_target_pairs={{0,2},{2,0},{4,6},{6,4},{1,3},{3,1},{5,7},{7,5},{8,10},{10,8},{12,... | collective-permute-start | bytes 294920 | tf_op jit(solution)/shard_map/ppermute | solution.py:465
  66.9 9.0 %collective-permute-start.22 = (bf16[32,1536]{1,0:T(8,128)(2,1)S(1)}, bf16[32,1536]{1,0:T(8,128)(2,1)S(1)}, u32[]{:S(2)}, u32[]{:S(2)}) collective-permute-start(bf16[32,1536]{1,0:T(8,128)(2,1)S(1)} %get-tuple-element.71), channel_id=1, source_target_pairs={{0,4},{2,6},{4,0},{6,2},{1,5},{3,7},{5,1},{7,3},{8,12},{10,14},{12... | collective-permute-start | bytes 294920 | tf_op jit(solution)/shard_map/ppermute | solution.py:465
  68.6 7.3 %collective-permute-start.23 = (bf16[32,1536]{1,0:T(8,128)(2,1)S(1)}, bf16[32,1536]{1,0:T(8,128)(2,1)S(1)}, u32[]{:S(2)}, u32[]{:S(2)}) collective-permute-start(bf16[32,1536]{1,0:T(8,128)(2,1)S(1)} %get-tuple-element.72), channel_id=1, source_target_pairs={{0,6},{2,4},{4,2},{6,0},{1,7},{3,5},{5,3},{7,1},{8,14},{10,12},{12... | collective-permute-start | bytes 294920 | tf_op jit(solution)/shard_map/ppermute | solution.py:465
  71.5 4.7 %collective-permute-start.24 = (bf16[32,1536]{1,0:T(8,128)(2,1)S(1)}, bf16[32,1536]{1,0:T(8,128)(2,1)S(1)}, u32[]{:S(2)}, u32[]{:S(2)}) collective-permute-start(bf16[32,1536]{1,0:T(8,128)(2,1)S(1)} %get-tuple-element.76), channel_id=1, source_target_pairs={{0,2},{2,0},{4,6},{6,4},{1,3},{3,1},{5,7},{7,5},{8,10},{10,8},{12,... | collective-permute-start | bytes 294920 | tf_op jit(solution)/shard_map/ppermute | solution.py:465
  71.7 5.2 %collective-permute-start.25 = (bf16[32,1536]{1,0:T(8,128)(2,1)S(1)}, bf16[32,1536]{1,0:T(8,128)(2,1)S(1)}, u32[]{:S(2)}, u32[]{:S(2)}) collective-permute-start(bf16[32,1536]{1,0:T(8,128)(2,1)S(1)} %get-tuple-element.77), channel_id=1, source_target_pairs={{0,4},{2,6},{4,0},{6,2},{1,5},{3,7},{5,1},{7,3},{8,12},{10,14},{12... | collective-permute-start | bytes 294920 | tf_op jit(solution)/shard_map/ppermute | solution.py:465
  73.3 5.5 %collective-permute-start.26 = (bf16[32,1536]{1,0:T(8,128)(2,1)S(1)}, bf16[32,1536]{1,0:T(8,128)(2,1)S(1)}, u32[]{:S(2)}, u32[]{:S(2)}) collective-permute-start(bf16[32,1536]{1,0:T(8,128)(2,1)S(1)} %get-tuple-element.78), channel_id=1, source_target_pairs={{0,6},{2,4},{4,2},{6,0},{1,7},{3,5},{5,3},{7,1},{8,14},{10,12},{12... | collective-permute-start | bytes 294920 | tf_op jit(solution)/shard_map/ppermute | solution.py:465

commit v2 on v0

--- a/solution.py
+++ b/solution.py
@@ -149,14 +149,14 @@
 
     shape = (channels * height, z.cell)
     line, entry = iota(shape, 0), iota(shape, 1)
-    channel, image_row = line // height, line % height
+    channel, image_row = lax.div(line, height), lax.rem(line, height)
     away = (
-        (channel * STRIDE + image_row % STRIDE) * STRIDE
-        + image_row // STRIDE * z.cell
-        - entry // STRIDE * STRIDE
+        (channel * STRIDE + lax.rem(image_row, STRIDE)) * STRIDE
+        + lax.div(image_row, STRIDE) * z.cell
+        - lax.div(entry, STRIDE) * STRIDE
     )
     shape = (width, z.cell)
-    mine = (iota(shape, 0) % STRIDE == iota(shape, 1) % STRIDE).astype(F32)
+    mine = (lax.rem(iota(shape, 0), STRIDE) == lax.rem(iota(shape, 1), STRIDE)).astype(F32)
     for i in range(z.rows):
         moved = jnp.dot(
             spread[...], is_equal(away, i * z.cell), preferred_element_type=F32
@@ -268,19 +268,40 @@
     send_sides(z, place, own, sends)
 
 
-def sort_kernel(z, groups, where, codes, _, shared):
+def sort_kernel(z, grid, groups, where, codes, _, *messages):
     rows_n, cores_n, owned = groups
     span = z.atoms // rows_n
     src = lax.broadcasted_iota(jnp.int32, (span, span), 0)
     dst = lax.broadcasted_iota(jnp.int32, (span, span), 1)
     per_core = span // cores_n
-    core, rem = dst // per_core, dst % per_core
-    wanted = (rem // owned) * (owned * cores_n) + core * owned + rem % owned
+    core, rem = lax.div(dst, per_core), lax.rem(dst, per_core)
+    wanted = lax.div(rem, owned) * (owned * cores_n) + core * owned + lax.rem(rem, owned)
     order = is_equal(src, wanted)
-    for r in range(rows_n):
-        line = jnp.dot(codes[:, r * span : (r + 1) * span], order, preferred_element_type=F32)
+    place = Place(where, *grid)
+    for x, message in enumerate(messages):
+        r = place.row ^ x if rows_n & (rows_n - 1) == 0 else (place.row - x) % rows_n
+        block = codes[:, pl.ds(pl.multiple_of(r * span, span), span)]
+        line = jnp.dot(block, order, preferred_element_type=F32).astype(BF16)
         for k in range(cores_n):
-            shared[r * cores_n + k] = line[:, k * per_core : (k + 1) * per_core].astype(BF16)
+            message[k] = line[:, k * per_core : (k + 1) * per_core]
+
+
+def turn_kernel(z, grid, groups, where, *rest):
+    rows_n, cores_n, _ = groups
+    stride = rows_n * cores_n * z.cols
+    near, far, (across, codes) = rest[:rows_n], rest[rows_n : 2 * rows_n], rest[2 * rows_n :]
+    place = Place(where, *grid)
+    mine = place.col % 2
+    for x in range(rows_n):
+        d = offset(place.row, x, rows_n)
+        for k, message in ((mine, near[x]), (1 - mine, far[x])):
+            lines = message[mine]
+            for i in range(z.rows):
+                at = i * stride + (d * cores_n + k) * z.cols
+                codes[pl.ds(pl.multiple_of(at, z.cols), z.cols), :] = lines[
+                    i * z.cols : (i + 1) * z.cols, :
+                ]
+    across[...] = codes[...].astype(F32).T.astype(BF16)
 
 
 def pack_kernel(z, grid, where, own, from_even, from_odd, packed, joined, flat):
@@ -318,11 +339,11 @@
         out[...] = partial[pl.ds(pl.multiple_of(at * owned, owned), owned), :]
 
 
-def learn_kernel(z, grid, groups, yx_n, where, shared, *rest):
+def learn_kernel(z, grid, groups, yx_n, where, across, *rest):
     rows_n, cores_n, _ = groups
     members = rows_n * cores_n
     near, far, outs = rest[:rows_n], rest[rows_n : 2 * rows_n], rest[2 * rows_n :]
-    outs, (across, wide_part, partial, flat, whole, codes) = outs[:yx_n], outs[yx_n:]
+    outs, (wide_part, partial, flat, whole) = outs[:yx_n], outs[yx_n:]
     stride = members * z.cols
     base = z.tall * z.cols
     half = z.packed // 2
@@ -363,11 +384,6 @@
                     for c in range(MARGIN):
                         whole[at : at + n, z.cols + c, :] += side[c]
             windows_of(z, whole, wide_part, d * z.cols, stride)
-            for i in range(z.rows):
-                codes[i * stride + d * z.cols : i * stride + (d + 1) * z.cols, :] = shared[
-                    d, i * z.cols : (i + 1) * z.cols, :
-                ]
-    across[...] = codes[...].astype(F32).T.astype(BF16)
     learn_half(
         z, grid, where, across[...], wide_part, stride, range(SPAN // 2), outs, partial
     )
@@ -441,6 +457,9 @@
     members = rows_n * cores_n
     grid = (rows_n, cols_n)
     where = jnp.stack([lax.axis_index("row"), lax.axis_index(("yx", "core"))]).astype(jnp.int32)
+
+    def met(block, axis, n, step):
+        return lax.ppermute(block, axis, [(i, offset(i, step, n)) for i in range(n)])
 
     def swapped(axis, n, blocks):
         return [lax.ppermute(b, axis, route) for b, route in zip(blocks, partners(n))]
@@ -502,13 +521,26 @@
         sides = rest[:2]
     final_codes = potential.reshape(membrane.shape)
     sides = sideways(sides)
-    (shared,) = call(
-        functools.partial(sort_kernel, z, groups),
-        [pltpu.VMEM((members, z.sites, atom_count // members), BF16)],
+    message_v = pltpu.VMEM((2, z.sites, atom_count // members), BF16)
+    messages = call(
+        functools.partial(sort_kernel, z, grid, groups),
+        [message_v] * rows_n,
         (where, rest[2], sides[0]),
         [],
     )
-    shared = lax.all_to_all(shared, ("row", "core"), 0, 0, tiled=True)
+    power = rows_n & (rows_n - 1) == 0
+
+    def along_row(blocks):
+        return [blocks[0]] + [
+            met(block, "row", rows_n, x if power else rows_n - x)
+            for x, block in enumerate(blocks[1:], 1)
+        ]
+
+    def across_chip(blocks):
+        return [met(block, "core", 2, 1) for block in blocks]
+
+    near_codes = along_row(messages)
+    far_codes = across_chip(near_codes)
     (packed,) = call(
         functools.partial(pack_kernel, z, grid),
         [pltpu.VMEM((z.packed * 3 // 2, 128), BF16)],
@@ -516,31 +548,26 @@
         [own_v, flat_v],
     )
 
-    def met(block, axis, n, step):
-        return lax.ppermute(block, axis, [(i, offset(i, step, n)) for i in range(n)])
-
-    power = rows_n & (rows_n - 1) == 0
-    near = [packed] + [
-        met(packed, "row", rows_n, x if power else rows_n - x) for x in range(1, rows_n)
-    ]
-    far = [met(block, "core", 2, 1) for block in near]
+    near = along_row([packed] * rows_n)
+    far = across_chip(near)
     stride = members * z.cols
     group_atoms = atom_count // members
     half_v = pltpu.VMEM((owned, z.patch // 2), BF16)
     partial_v = pltpu.VMEM((group_atoms, z.patch // 2), BF16)
-    *first_half, across, wide_part = call(
+    (across,) = call(
+        functools.partial(turn_kernel, z, grid, groups),
+        [pltpu.VMEM((group_atoms, members * z.sites), BF16)],
+        (where, *near_codes, *far_codes),
+        [pltpu.VMEM((members * z.sites, group_atoms), BF16)],
+    )
+    *first_half, wide_part = call(
         functools.partial(learn_kernel, z, grid, groups, yx_n),
-        [half_v] * yx_n
-        + [
-            pltpu.VMEM((group_atoms, members * z.sites), BF16),
-            pltpu.VMEM((z.tall * stride, z.band), BF16),
-        ],
-        (where, shared, *near, *far),
+        [half_v] * yx_n + [pltpu.VMEM((z.tall * stride, z.band), BF16)],
+        (where, across, *near, *far),
         [
             partial_v,
             pltpu.VMEM((cores_n, rows_n, z.packed, z.lanes), F32),
             own_v,
-            pltpu.VMEM((members * z.sites, group_atoms), BF16),
         ],
     )
     other_half = call(

time: 80.4 us -> 78.8 us (0.980)
  waiting for transfers between devices: 26.1 us -> 23.9 us
    ppermute x13 -> x20, starting transfers between devices: 12.1 us -> 17.7 us  [met(): lax.ppermute(block, axis, [(i, offset(i, step, n)) for i in range(n)])]
    all_to_all x1 -> x0, starting transfers between devices: 3.74 us -> none  [shards(): shared = lax.all_to_all(shared, ('row', 'core'), 0, 0, tiled=True)]
    ppermute x13 -> x20, waiting for transfers between devices: 11.8 us -> 8.61 us  [met(): lax.ppermute(block, axis, [(i, offset(i, step, n)) for i in range(n)])]
    ppermute x3, starting transfers between devices: 6.83 us -> 5.66 us  [sideways(): far_rim = lax.ppermute(blocks[1], ('yx', 'core'), odd)]
    ppermute x3, waiting for transfers between devices: 6.6 us -> 7.63 us  [sideways(): far_rim = lax.ppermute(blocks[1], ('yx', 'core'), odd)]
    pallas_call x10 -> x11, Pallas kernels: 22 us -> 22 us  [call(): pl.pallas_call(kernel, out_shape=outs, in_specs=specs, out_specs=[leave]...]
  transfers between devices with their start and end apart: 24 -> 30, of which waited for: 14 -> 12; matrix products, arithmetic and copies ran while one was open for 1% -> 1% of each run, Pallas kernels for 3% -> 4%
where the time goes in v2:
time: 78.8 us; the launch traced here: 78.7 us
  starting transfers between devices  30.9 us (39%)
  waiting for transfers between devices  23.9 us (30%)
  Pallas kernels  22 us (28%)
  between operations  0.96 us (1%)
  local copies, waits for them, and re-layouts  0.8 us (1%)
    pallas_call x11, Pallas kernels, call(): pl.pallas_call(kernel, out_shape=outs, in_specs=specs, out_specs=[leave]...  22 us
    ppermute x20, starting transfers between devices, met(): lax.ppermute(block, axis, [(i, offset(i, step, n)) for i in range(n)])  17.7 us
    ppermute x20, waiting for transfers between devices, met(): lax.ppermute(block, axis, [(i, offset(i, step, n)) for i in range(n)])  8.61 us
    ppermute x3, waiting for transfers between devices, sideways(): far_rim = lax.ppermute(blocks[1], ('yx', 'core'), odd)  7.63 us
    ppermute x4, starting transfers between devices, swapped(): lax.ppermute(b, axis, route)  6.87 us
    ppermute x4, waiting for transfers between devices, swapped(): lax.ppermute(b, axis, route)  6.48 us
    ppermute x3, starting transfers between devices, sideways(): far_rim = lax.ppermute(blocks[1], ('yx', 'core'), odd)  5.66 us
  transfers between devices with their start and end apart: 30, of which 12 were waited for; matrix products, arithmetic and copies ran while one was open for 1% of the time, Pallas kernels for 4%

profile of v2, /device:TPU:0, one launch (start us, length us, event | category | flops | bytes accessed | tf_op | source)
XLA Modules:
  0.0 78.7 jit_solution(14392068049445885611)
XLA Ops:
  0.7 4.4 %shard_map.67 = (f32[11,24,256]{2,1,0:T(8,128)S(1)}, bf16[3,16,256]{2,1,0:T(8,128)(2,1)S(1)}, bf16[3,16,256]{2,1,0:T(8,128)(2,1)S(1)}, f32[128,192]{1,0:T(8,128)...) custom-call(s32[2]{0:T(128)S(1)} %pad_add_fusion.where, ...), custom_call_target="tpu_custom_call" | custom-call | tf_op jit(solution)/shard_map/pallas_call | solution.py:440
  5.7 3.5 %collective-permute-start.1 = (bf16[3,16,256]{2,1,0:T(8,128)(2,1)S(1)}, bf16[3,16,256]{2,1,0:T(8,128)(2,1)S(1)}, u32[]{:S(2)}, u32[]{:S(2)}) collective-permute-start(bf16[3,16,256]{2,1,0:T(8,128)(2,1)S(1)} %get-tuple-element.43), channel_id=1, source_target_pairs={{0,7},{1,2},{2,1},{3,4},{4,3},{5,6},{6,5},{7,0},{8,15},{9,10},{10,... | collective-permute-start | bytes 73736 | tf_op jit(solution)/shard_map/ppermute | solution.py:470
  9.2 1.5 %collective-permute-done.1.from_odd = bf16[3,16,256]{2,1,0:T(8,128)(2,1)S(1)} collective-permute-done((bf16[3,16,256]{2,1,0:T(8,128)(2,1)S(1)}, bf16[3,16,256]{2,1,0:T(8,128)(2,1)S(1)}, u32[]{:S(2)}, u32[]{:S(2)}) %collective-permute-start.1) | collective-permute-done | bytes 24608 | tf_op jit(solution)/shard_map/ppermute | solution.py:470
  11.4 1.8 %collective-permute-start.2 = (bf16[64,256]{1,0:T(8,128)(2,1)S(1)}, bf16[64,256]{1,0:T(8,128)(2,1)S(1)}, u32[]{:S(2)}, u32[]{:S(2)}) collective-permute-start(bf16[64,256]{1,0:T(8,128)(2,1)S(1)} %get-tuple-element.45), channel_id=1, source_target_pairs={{0,8},{8,0},{16,24},{24,16},{1,9},{9,1},{17,25},{25,17},{2,10},{10... | collective-permute-start | bytes 98312 | tf_op jit(solution)/shard_map/ppermute | solution.py:465
  13.2 2.5 %collective-permute-start.3 = (bf16[64,256]{1,0:T(8,128)(2,1)S(1)}, bf16[64,256]{1,0:T(8,128)(2,1)S(1)}, u32[]{:S(2)}, u32[]{:S(2)}) collective-permute-start(bf16[64,256]{1,0:T(8,128)(2,1)S(1)} %get-tuple-element.46), channel_id=1, source_target_pairs={{0,24},{8,16},{16,8},{24,0},{1,25},{9,17},{17,9},{25,1},{2,26},{10... | collective-permute-start | bytes 98312 | tf_op jit(solution)/shard_map/ppermute | solution.py:465
  15.6 3.2 %collective-permute-done.3.from_odd = bf16[64,256]{1,0:T(8,128)(2,1)S(1)} collective-permute-done((bf16[64,256]{1,0:T(8,128)(2,1)S(1)}, bf16[64,256]{1,0:T(8,128)(2,1)S(1)}, u32[]{:S(2)}, u32[]{:S(2)}) %collective-permute-start.3) | collective-permute-done | bytes 32800 | tf_op jit(solution)/shard_map/ppermute | solution.py:465
  18.9 4.3 %shard_map.69 = (f32[128,1024]{1,0:T(8,128)S(1)}, f32[11,24,256]{2,1,0:T(8,128)S(1)}, bf16[3,16,256]{2,1,0:T(8,128)(2,1)S(1)}, bf16[3,16,256]{2,1,0:T(8,128)(2,1)S(1)}) custom-call(s32[2]{0:T(128)S(1)} %pad_add_fusion.where, f32[128,1024]{1,0:T(8,128)S(1)} %get-tuple-element.40.potential, f32[11,24,256]{2,1,0:T(8,128)S(1)} %get-tuple-element.44.joined, ...), custom_call_target="tpu_custom_call" | custom-call | tf_op jit(solution)/shard_map/pallas_call | solution.py:440
  23.3 2.0 %collective-permute-start.5 = (bf16[3,16,256]{2,1,0:T(8,128)(2,1)S(1)}, bf16[3,16,256]{2,1,0:T(8,128)(2,1)S(1)}, u32[]{:S(2)}, u32[]{:S(2)}) collective-permute-start(bf16[3,16,256]{2,1,0:T(8,128)(2,1)S(1)} %get-tuple-element.52), channel_id=1, source_target_pairs={{0,7},{1,2},{2,1},{3,4},{4,3},{5,6},{6,5},{7,0},{8,15},{9,10},{10,... | collective-permute-start | bytes 73736 | tf_op jit(solution)/shard_map/ppermute | solution.py:470
  25.3 2.2 %collective-permute-done.5.from_odd = bf16[3,16,256]{2,1,0:T(8,128)(2,1)S(1)} collective-permute-done((bf16[3,16,256]{2,1,0:T(8,128)(2,1)S(1)}, bf16[3,16,256]{2,1,0:T(8,128)(2,1)S(1)}, u32[]{:S(2)}, u32[]{:S(2)}) %collective-permute-start.5) | collective-permute-done | bytes 24608 | tf_op jit(solution)/shard_map/ppermute | solution.py:470
  28.2 2.5 %collective-permute-start.7 = (bf16[64,256]{1,0:T(8,128)(2,1)S(1)}, bf16[64,256]{1,0:T(8,128)(2,1)S(1)}, u32[]{:S(2)}, u32[]{:S(2)}) collective-permute-start(bf16[64,256]{1,0:T(8,128)(2,1)S(1)} %get-tuple-element.55), channel_id=1, source_target_pairs={{0,24},{8,16},{16,8},{24,0},{1,25},{9,17},{17,9},{25,1},{2,26},{10... | collective-permute-start | bytes 98312 | tf_op jit(solution)/shard_map/ppermute | solution.py:465
  30.8 1.4 %collective-permute-done.6.from_even = bf16[64,256]{1,0:T(8,128)(2,1)S(1)} collective-permute-done((bf16[64,256]{1,0:T(8,128)(2,1)S(1)}, bf16[64,256]{1,0:T(8,128)(2,1)S(1)}, u32[]{:S(2)}, u32[]{:S(2)}) %collective-permute-start.6) | collective-permute-done | bytes 32800 | tf_op jit(solution)/shard_map/ppermute | solution.py:465
  32.1 1.9 %collective-permute-done.7.from_odd = bf16[64,256]{1,0:T(8,128)(2,1)S(1)} collective-permute-done((bf16[64,256]{1,0:T(8,128)(2,1)S(1)}, bf16[64,256]{1,0:T(8,128)(2,1)S(1)}, u32[]{:S(2)}, u32[]{:S(2)}) %collective-permute-start.7) | collective-permute-done | bytes 32800 | tf_op jit(solution)/shard_map/ppermute | solution.py:465
  34.0 4.3 %shard_map.71 = (f32[128,1024]{1,0:T(8,128)S(1)}, f32[11,24,256]{2,1,0:T(8,128)S(1)}, bf16[3,16,256]{2,1,0:T(8,128)(2,1)S(1)}, bf16[3,16,256]{2,1,0:T(8,128)(2,1)S(1)}, bf16[128,1024]{1,0:T(8,128)(2,1)S(1)}) custom-call(s32[2]{0:T(128)S(1)} %pad_add_fusion.where, f32[128,1024]{1,0:T(8,128)S(1)} %get-tuple-element.49.potential, ...), custom_call_target="tpu_custom_call" | custom-call | tf_op jit(solution)/shard_map/pallas_call | solution.py:440
  38.4 1.2 %collective-permute-done.8._.from_even = bf16[3,16,256]{2,1,0:T(8,128)(2,1)S(1)} collective-permute-done((bf16[3,16,256]{2,1,0:T(8,128)(2,1)S(1)}, bf16[3,16,256]{2,1,0:T(8,128)(2,1)S(1)}, u32[]{:S(2)}, u32[]{:S(2)}) %collective-permute-start.8) | collective-permute-done | bytes 24608 | tf_op jit(solution)/shard_map/ppermute | solution.py:469
  40.6 2.9 %collective-permute-start.10 = (bf16[2,128,128]{2,1,0:T(8,128)(2,1)S(1)}, bf16[2,128,128]{2,1,0:T(8,128)(2,1)S(1)}, u32[]{:S(2)}, u32[]{:S(2)}) collective-permute-start(bf16[2,128,128]{2,1,0:T(8,128)(2,1)S(1)} %get-tuple-element.62), channel_id=1, source_target_pairs={{0,16},{8,24},{16,0},{24,8},{1,17},{9,25},{17,1},{25,9},{2,18},{10... | collective-permute-start | bytes 196616 | tf_op jit(solution)/shard_map/ppermute | solution.py:462
  43.5 1.4 %collective-permute-start.11 = (bf16[2,128,128]{2,1,0:T(8,128)(2,1)S(1)}, bf16[2,128,128]{2,1,0:T(8,128)(2,1)S(1)}, u32[]{:S(2)}, u32[]{:S(2)}) collective-permute-start(bf16[2,128,128]{2,1,0:T(8,128)(2,1)S(1)} %get-tuple-element.63), channel_id=1, source_target_pairs={{0,24},{8,16},{16,8},{24,0},{1,25},{9,17},{17,9},{25,1},{2,26},{10... | collective-permute-start | bytes 196616 | tf_op jit(solution)/shard_map/ppermute | solution.py:462
  45.1 3.9 %collective-permute-done.16.from_odd = bf16[3,16,256]{2,1,0:T(8,128)(2,1)S(1)} collective-permute-done((bf16[3,16,256]{2,1,0:T(8,128)(2,1)S(1)}, bf16[3,16,256]{2,1,0:T(8,128)(2,1)S(1)}, u32[]{:S(2)}, u32[]{:S(2)}) %collective-permute-start.16) | collective-permute-done | bytes 24608 | tf_op jit(solution)/shard_map/ppermute | solution.py:470
  49.9 2.5 %collective-permute-start.19 = (bf16[336,128]{1,0:T(8,128)(2,1)S(1)}, bf16[336,128]{1,0:T(8,128)(2,1)S(1)}, u32[]{:S(2)}, u32[]{:S(2)}) collective-permute-start(bf16[336,128]{1,0:T(8,128)(2,1)S(1)} %shard_map.74.rest_0_), channel_id=1, source_target_pairs={{0,24},{8,16},{16,8},{24,0},{1,25},{9,17},{17,9},{25,1},{2,26},{10... | collective-permute-start | bytes 258056 | tf_op jit(solution)/shard_map/ppermute | solution.py:462
  52.4 1.9 %collective-permute-start.17 = (bf16[336,128]{1,0:T(8,128)(2,1)S(1)}, bf16[336,128]{1,0:T(8,128)(2,1)S(1)}, u32[]{:S(2)}, u32[]{:S(2)}) collective-permute-start(bf16[336,128]{1,0:T(8,128)(2,1)S(1)} %shard_map.74.rest_0_), channel_id=1, source_target_pairs={{0,8},{8,0},{16,24},{24,16},{1,9},{9,1},{17,25},{25,17},{2,10},{10... | collective-permute-start | bytes 258056 | tf_op jit(solution)/shard_map/ppermute | solution.py:462
  54.9 2.1 %collective-permute-done.19.rest_3_ = bf16[336,128]{1,0:T(8,128)(2,1)S(1)} collective-permute-done((bf16[336,128]{1,0:T(8,128)(2,1)S(1)}, bf16[336,128]{1,0:T(8,128)(2,1)S(1)}, u32[]{:S(2)}, u32[]{:S(2)}) %collective-permute-start.19) | collective-permute-done | bytes 86048 | tf_op jit(solution)/shard_map/ppermute | solution.py:462
  57.0 1.8 %collective-permute-done.18.rest_2_ = bf16[336,128]{1,0:T(8,128)(2,1)S(1)} collective-permute-done((bf16[336,128]{1,0:T(8,128)(2,1)S(1)}, bf16[336,128]{1,0:T(8,128)(2,1)S(1)}, u32[]{:S(2)}, u32[]{:S(2)}) %collective-permute-start.18) | collective-permute-done | bytes 86048 | tf_op jit(solution)/shard_map/ppermute | solution.py:462
  61.5 2.5 %shard_map.75 = (bf16[32,1536]{1,0:T(8,128)(2,1)S(1)}, bf16[32,1536]{1,0:T(8,128)(2,1)S(1)}, bf16[32,1536]{1,0:T(8,128)(2,1)S(1)}, bf16[32,1536]{1,0:T(8,128)(2,1)S(1)}, bf16[1408,768]{1,0:T(8,128)(2,1)S(1)}) custom-call(s32[2]{0:T(128)S(1)} %pad_add_fusion.where, bf16[128,1024]{1,0:T(8,128)(2,1)S(1)} %shard_map.73.across, ...), custom_call_target="tpu_custom_call" | custom-call | tf_op jit(solution)/shard_map/pallas_call | solution.py:440
  64.0 1.4 %collective-permute-start.24 = (bf16[32,1536]{1,0:T(8,128)(2,1)S(1)}, bf16[32,1536]{1,0:T(8,128)(2,1)S(1)}, u32[]{:S(2)}, u32[]{:S(2)}) collective-permute-start(bf16[32,1536]{1,0:T(8,128)(2,1)S(1)} %get-tuple-element.67), channel_id=1, source_target_pairs={{0,2},{2,0},{4,6},{6,4},{1,3},{3,1},{5,7},{7,5},{8,10},{10,8},{12,... | collective-permute-start | bytes 294920 | tf_op jit(solution)/shard_map/ppermute | solution.py:462
  65.5 1.1 %collective-permute-start.25 = (bf16[32,1536]{1,0:T(8,128)(2,1)S(1)}, bf16[32,1536]{1,0:T(8,128)(2,1)S(1)}, u32[]{:S(2)}, u32[]{:S(2)}) collective-permute-start(bf16[32,1536]{1,0:T(8,128)(2,1)S(1)} %get-tuple-element.68), channel_id=1, source_target_pairs={{0,4},{2,6},{4,0},{6,2},{1,5},{3,7},{5,1},{7,3},{8,12},{10,14},{12... | collective-permute-start | bytes 294920 | tf_op jit(solution)/shard_map/ppermute | solution.py:462
  66.6 1.0 %collective-permute-start.26 = (bf16[32,1536]{1,0:T(8,128)(2,1)S(1)}, bf16[32,1536]{1,0:T(8,128)(2,1)S(1)}, u32[]{:S(2)}, u32[]{:S(2)}) collective-permute-start(bf16[32,1536]{1,0:T(8,128)(2,1)S(1)} %get-tuple-element.69), channel_id=1, source_target_pairs={{0,6},{2,4},{4,2},{6,0},{1,7},{3,5},{5,3},{7,1},{8,14},{10,12},{12... | collective-permute-start | bytes 294920 | tf_op jit(solution)/shard_map/ppermute | solution.py:462
  67.6 1.1 %shard_map.76 = (bf16[32,1536]{1,0:T(8,128)(2,1)S(1)}, bf16[32,1536]{1,0:T(8,128)(2,1)S(1)}, bf16[32,1536]{1,0:T(8,128)(2,1)S(1)}, bf16[32,1536]{1,0:T(8,128)(2,1)S(1)}) custom-call(s32[2]{0:T(128)S(1)} %pad_add_fusion.where, bf16[128,1024]{1,0:T(8,128)(2,1)S(1)} %shard_map.73.across, bf16[1408,768]{1,0:T(8,128)(2,1)S(1)} %get-tuple-element.70.wide_part), custom_call_target="tpu_custom_call" | custom-call | tf_op jit(solution)/shard_map/pallas_call | solution.py:440
  68.8 1.4 %collective-permute-start.27 = (bf16[32,1536]{1,0:T(8,128)(2,1)S(1)}, bf16[32,1536]{1,0:T(8,128)(2,1)S(1)}, u32[]{:S(2)}, u32[]{:S(2)}) collective-permute-start(bf16[32,1536]{1,0:T(8,128)(2,1)S(1)} %get-tuple-element.72), channel_id=1, source_target_pairs={{0,2},{2,0},{4,6},{6,4},{1,3},{3,1},{5,7},{7,5},{8,10},{10,8},{12,... | collective-permute-start | bytes 294920 | tf_op jit(solution)/shard_map/ppermute | solution.py:462
  70.2 1.1 %collective-permute-start.28 = (bf16[32,1536]{1,0:T(8,128)(2,1)S(1)}, bf16[32,1536]{1,0:T(8,128)(2,1)S(1)}, u32[]{:S(2)}, u32[]{:S(2)}) collective-permute-start(bf16[32,1536]{1,0:T(8,128)(2,1)S(1)} %get-tuple-element.73), channel_id=1, source_target_pairs={{0,4},{2,6},{4,0},{6,2},{1,5},{3,7},{5,1},{7,3},{8,12},{10,14},{12... | collective-permute-start | bytes 294920 | tf_op jit(solution)/shard_map/ppermute | solution.py:462
  71.3 1.0 %collective-permute-start.29 = (bf16[32,1536]{1,0:T(8,128)(2,1)S(1)}, bf16[32,1536]{1,0:T(8,128)(2,1)S(1)}, u32[]{:S(2)}, u32[]{:S(2)}) collective-permute-start(bf16[32,1536]{1,0:T(8,128)(2,1)S(1)} %get-tuple-element.74), channel_id=1, source_target_pairs={{0,6},{2,4},{4,2},{6,0},{1,7},{3,5},{5,3},{7,1},{8,14},{10,12},{12... | collective-permute-start | bytes 294920 | tf_op jit(solution)/shard_map/ppermute | solution.py:462
  73.1 1.0 %collective-permute-done.27.rest_5_ = bf16[32,1536]{1,0:T(8,128)(2,1)S(1)} collective-permute-done((bf16[32,1536]{1,0:T(8,128)(2,1)S(1)}, bf16[32,1536]{1,0:T(8,128)(2,1)S(1)}, u32[]{:S(2)}, u32[]{:S(2)}) %collective-permute-start.27) | collective-permute-done | bytes 98336 | tf_op jit(solution)/shard_map/ppermute | solution.py:462
  74.1 2.8 %collective-permute-done.28.rest_6_ = bf16[32,1536]{1,0:T(8,128)(2,1)S(1)} collective-permute-done((bf16[32,1536]{1,0:T(8,128)(2,1)S(1)}, bf16[32,1536]{1,0:T(8,128)(2,1)S(1)}, u32[]{:S(2)}, u32[]{:S(2)}) %collective-permute-start.28) | collective-permute-done | bytes 98336 | tf_op jit(solution)/shard_map/ppermute | solution.py:462
  76.9 1.6 %shard_map.77 = (f32[32,3072]{1,0:T(8,128)}, f32[32,3072]{1,0:T(8,128)}) custom-call(s32[2]{0:T(128)S(1)} %pad_add_fusion.where, f32[32,3072]{1,0:T(8,128)S(1)} %copy-done, bf16[32,3072]{1,0:T(8,128)(2,1)S(1)} %get-tuple-element.57.atoms, bf16[32,1536]{1,0:T(8,128)(2,1)S(1)} %get-tuple-element.66.rest_0_, ...), custom_call_target="tpu_custom_call" | custom-call | tf_op jit(solution)/shard_map/pallas_call | solution.py:440
  (43 shorter events, 8.3 us)
Async XLA Ops:
  5.1 4.1 %collective-permute-start = (bf16[3,16,256]{2,1,0:T(8,128)(2,1)S(1)}, bf16[3,16,256]{2,1,0:T(8,128)(2,1)S(1)}, u32[]{:S(2)}, u32[]{:S(2)}) collective-permute-start(bf16[3,16,256]{2,1,0:T(8,128)(2,1)S(1)} %get-tuple-element.42), channel_id=1, source_target_pairs={{0,1},{1,0},{2,3},{3,2},{4,5},{5,4},{6,7},{7,6},{8,9},{9,8},{10,11... | collective-permute-start | bytes 73736 | tf_op jit(solution)/shard_map/ppermute | solution.py:469
  5.7 5.1 %collective-permute-start.1 = (bf16[3,16,256]{2,1,0:T(8,128)(2,1)S(1)}, bf16[3,16,256]{2,1,0:T(8,128)(2,1)S(1)}, u32[]{:S(2)}, u32[]{:S(2)}) collective-permute-start(bf16[3,16,256]{2,1,0:T(8,128)(2,1)S(1)} %get-tuple-element.43), channel_id=1, source_target_pairs={{0,7},{1,2},{2,1},{3,4},{4,3},{5,6},{6,5},{7,0},{8,15},{9,10},{10,... | collective-permute-start | bytes 73736 | tf_op jit(solution)/shard_map/ppermute | solution.py:470
  11.4 4.3 %collective-permute-start.2 = (bf16[64,256]{1,0:T(8,128)(2,1)S(1)}, bf16[64,256]{1,0:T(8,128)(2,1)S(1)}, u32[]{:S(2)}, u32[]{:S(2)}) collective-permute-start(bf16[64,256]{1,0:T(8,128)(2,1)S(1)} %get-tuple-element.45), channel_id=1, source_target_pairs={{0,8},{8,0},{16,24},{24,16},{1,9},{9,1},{17,25},{25,17},{2,10},{10... | collective-permute-start | bytes 98312 | tf_op jit(solution)/shard_map/ppermute | solution.py:465
  13.2 5.7 %collective-permute-start.3 = (bf16[64,256]{1,0:T(8,128)(2,1)S(1)}, bf16[64,256]{1,0:T(8,128)(2,1)S(1)}, u32[]{:S(2)}, u32[]{:S(2)}) collective-permute-start(bf16[64,256]{1,0:T(8,128)(2,1)S(1)} %get-tuple-element.46), channel_id=1, source_target_pairs={{0,24},{8,16},{16,8},{24,0},{1,25},{9,17},{17,9},{25,1},{2,26},{10... | collective-permute-start | bytes 98312 | tf_op jit(solution)/shard_map/ppermute | solution.py:465
  23.2 2.1 %collective-permute-start.4 = (bf16[3,16,256]{2,1,0:T(8,128)(2,1)S(1)}, bf16[3,16,256]{2,1,0:T(8,128)(2,1)S(1)}, u32[]{:S(2)}, u32[]{:S(2)}) collective-permute-start(bf16[3,16,256]{2,1,0:T(8,128)(2,1)S(1)} %get-tuple-element.51), channel_id=1, source_target_pairs={{0,1},{1,0},{2,3},{3,2},{4,5},{5,4},{6,7},{7,6},{8,9},{9,8},{10,11... | collective-permute-start | bytes 73736 | tf_op jit(solution)/shard_map/ppermute | solution.py:469
  23.3 4.2 %collective-permute-start.5 = (bf16[3,16,256]{2,1,0:T(8,128)(2,1)S(1)}, bf16[3,16,256]{2,1,0:T(8,128)(2,1)S(1)}, u32[]{:S(2)}, u32[]{:S(2)}) collective-permute-start(bf16[3,16,256]{2,1,0:T(8,128)(2,1)S(1)} %get-tuple-element.52), channel_id=1, source_target_pairs={{0,7},{1,2},{2,1},{3,4},{4,3},{5,6},{6,5},{7,0},{8,15},{9,10},{10,... | collective-permute-start | bytes 73736 | tf_op jit(solution)/shard_map/ppermute | solution.py:470
  28.1 4.0 %collective-permute-start.6 = (bf16[64,256]{1,0:T(8,128)(2,1)S(1)}, bf16[64,256]{1,0:T(8,128)(2,1)S(1)}, u32[]{:S(2)}, u32[]{:S(2)}) collective-permute-start(bf16[64,256]{1,0:T(8,128)(2,1)S(1)} %get-tuple-element.54), channel_id=1, source_target_pairs={{0,8},{8,0},{16,24},{24,16},{1,9},{9,1},{17,25},{25,17},{2,10},{10... | collective-permute-start | bytes 98312 | tf_op jit(solution)/shard_map/ppermute | solution.py:465
  28.2 5.8 %collective-permute-start.7 = (bf16[64,256]{1,0:T(8,128)(2,1)S(1)}, bf16[64,256]{1,0:T(8,128)(2,1)S(1)}, u32[]{:S(2)}, u32[]{:S(2)}) collective-permute-start(bf16[64,256]{1,0:T(8,128)(2,1)S(1)} %get-tuple-element.55), channel_id=1, source_target_pairs={{0,24},{8,16},{16,8},{24,0},{1,25},{9,17},{17,9},{25,1},{2,26},{10... | collective-permute-start | bytes 98312 | tf_op jit(solution)/shard_map/ppermute | solution.py:465
  34.0 42.9 %copy-start = (f32[32,3072]{1,0:T(8,128)S(1)}, f32[32,3072]{1,0:T(8,128)}, u32[]{:S(2)}) copy-start(f32[32,3072]{1,0:T(8,128)} %momentum.1) | copy-start | bytes 1179652
  38.4 1.3 %collective-permute-start.8 = (bf16[3,16,256]{2,1,0:T(8,128)(2,1)S(1)}, bf16[3,16,256]{2,1,0:T(8,128)(2,1)S(1)}, u32[]{:S(2)}, u32[]{:S(2)}) collective-permute-start(bf16[3,16,256]{2,1,0:T(8,128)(2,1)S(1)} %get-tuple-element.59), channel_id=1, source_target_pairs={{0,1},{1,0},{2,3},{3,2},{4,5},{5,4},{6,7},{7,6},{8,9},{9,8},{10,11... | collective-permute-start | bytes 73736 | tf_op jit(solution)/shard_map/ppermute | solution.py:469
  40.4 12.0 %collective-permute-start.9 = (bf16[2,128,128]{2,1,0:T(8,128)(2,1)S(1)}, bf16[2,128,128]{2,1,0:T(8,128)(2,1)S(1)}, u32[]{:S(2)}, u32[]{:S(2)}) collective-permute-start(bf16[2,128,128]{2,1,0:T(8,128)(2,1)S(1)} %get-tuple-element.61), channel_id=1, source_target_pairs={{0,8},{8,0},{16,24},{24,16},{1,9},{9,1},{17,25},{25,17},{2,10},{10... | collective-permute-start | bytes 196616 | tf_op jit(solution)/shard_map/ppermute | solution.py:462
  40.6 11.8 %collective-permute-start.10 = (bf16[2,128,128]{2,1,0:T(8,128)(2,1)S(1)}, bf16[2,128,128]{2,1,0:T(8,128)(2,1)S(1)}, u32[]{:S(2)}, u32[]{:S(2)}) collective-permute-start(bf16[2,128,128]{2,1,0:T(8,128)(2,1)S(1)} %get-tuple-element.62), channel_id=1, source_target_pairs={{0,16},{8,24},{16,0},{24,8},{1,17},{9,25},{17,1},{25,9},{2,18},{10... | collective-permute-start | bytes 196616 | tf_op jit(solution)/shard_map/ppermute | solution.py:462
  43.5 10.8 %collective-permute-start.11 = (bf16[2,128,128]{2,1,0:T(8,128)(2,1)S(1)}, bf16[2,128,128]{2,1,0:T(8,128)(2,1)S(1)}, u32[]{:S(2)}, u32[]{:S(2)}) collective-permute-start(bf16[2,128,128]{2,1,0:T(8,128)(2,1)S(1)} %get-tuple-element.63), channel_id=1, source_target_pairs={{0,24},{8,16},{16,8},{24,0},{1,25},{9,17},{17,9},{25,1},{2,26},{10... | collective-permute-start | bytes 196616 | tf_op jit(solution)/shard_map/ppermute | solution.py:462
  44.9 4.2 %collective-permute-start.16 = (bf16[3,16,256]{2,1,0:T(8,128)(2,1)S(1)}, bf16[3,16,256]{2,1,0:T(8,128)(2,1)S(1)}, u32[]{:S(2)}, u32[]{:S(2)}) collective-permute-start(bf16[3,16,256]{2,1,0:T(8,128)(2,1)S(1)} %get-tuple-element.65), channel_id=1, source_target_pairs={{0,7},{1,2},{2,1},{3,4},{4,3},{5,6},{6,5},{7,0},{8,15},{9,10},{10,... | collective-permute-start | bytes 73736 | tf_op jit(solution)/shard_map/ppermute | solution.py:470
  45.0 9.4 %collective-permute-start.12 = (bf16[2,128,128]{2,1,0:T(8,128)(2,1)S(1)}, bf16[2,128,128]{2,1,0:T(8,128)(2,1)S(1)}, u32[]{:S(2)}, u32[]{:S(2)}) collective-permute-start(bf16[2,128,128]{2,1,0:T(8,128)(2,1)S(1)} %get-tuple-element.60.rest_0_), channel_id=1, source_target_pairs={{0,1},{1,0},{2,3},{3,2},{4,5},{5,4},{6,7},{7,6},{8,9},{9,8},{10,11... | collective-permute-start | bytes 196616 | tf_op jit(solution)/shard_map/ppermute | solution.py:462
  49.9 7.1 %collective-permute-start.19 = (bf16[336,128]{1,0:T(8,128)(2,1)S(1)}, bf16[336,128]{1,0:T(8,128)(2,1)S(1)}, u32[]{:S(2)}, u32[]{:S(2)}) collective-permute-start(bf16[336,128]{1,0:T(8,128)(2,1)S(1)} %shard_map.74.rest_0_), channel_id=1, source_target_pairs={{0,24},{8,16},{16,8},{24,0},{1,25},{9,17},{17,9},{25,1},{2,26},{10... | collective-permute-start | bytes 258056 | tf_op jit(solution)/shard_map/ppermute | solution.py:462
  52.4 6.4 %collective-permute-start.18 = (bf16[336,128]{1,0:T(8,128)(2,1)S(1)}, bf16[336,128]{1,0:T(8,128)(2,1)S(1)}, u32[]{:S(2)}, u32[]{:S(2)}) collective-permute-start(bf16[336,128]{1,0:T(8,128)(2,1)S(1)} %shard_map.74.rest_0_), channel_id=1, source_target_pairs={{0,16},{8,24},{16,0},{24,8},{1,17},{9,25},{17,1},{25,9},{2,18},{10... | collective-permute-start | bytes 258056 | tf_op jit(solution)/shard_map/ppermute | solution.py:462
  52.4 6.3 %collective-permute-start.17 = (bf16[336,128]{1,0:T(8,128)(2,1)S(1)}, bf16[336,128]{1,0:T(8,128)(2,1)S(1)}, u32[]{:S(2)}, u32[]{:S(2)}) collective-permute-start(bf16[336,128]{1,0:T(8,128)(2,1)S(1)} %shard_map.74.rest_0_), channel_id=1, source_target_pairs={{0,8},{8,0},{16,24},{24,16},{1,9},{9,1},{17,25},{25,17},{2,10},{10... | collective-permute-start | bytes 258056 | tf_op jit(solution)/shard_map/ppermute | solution.py:462
  54.3 4.9 %collective-permute-start.13 = (bf16[2,128,128]{2,1,0:T(8,128)(2,1)S(1)}, bf16[2,128,128]{2,1,0:T(8,128)(2,1)S(1)}, u32[]{:S(2)}, u32[]{:S(2)}) collective-permute-start(bf16[2,128,128]{2,1,0:T(8,128)(2,1)S(1)} %collective-permute-done.9.rest_1_), channel_id=1, source_target_pairs={{0,1},{1,0},{2,3},{3,2},{4,5},{5,4},{6,7},{7,6},{8,9},{9,8},{10,11... | collective-permute-start | bytes 196616 | tf_op jit(solution)/shard_map/ppermute | solution.py:462
  54.4 5.0 %collective-permute-start.14 = (bf16[2,128,128]{2,1,0:T(8,128)(2,1)S(1)}, bf16[2,128,128]{2,1,0:T(8,128)(2,1)S(1)}, u32[]{:S(2)}, u32[]{:S(2)}) collective-permute-start(bf16[2,128,128]{2,1,0:T(8,128)(2,1)S(1)} %collective-permute-done.10.rest_2_), channel_id=1, source_target_pairs={{0,1},{1,0},{2,3},{3,2},{4,5},{5,4},{6,7},{7,6},{8,9},{9,8},{10,11... | collective-permute-start | bytes 196616 | tf_op jit(solution)/shard_map/ppermute | solution.py:462
  57.0 4.5 %collective-permute-start.20 = (bf16[336,128]{1,0:T(8,128)(2,1)S(1)}, bf16[336,128]{1,0:T(8,128)(2,1)S(1)}, u32[]{:S(2)}, u32[]{:S(2)}) collective-permute-start(bf16[336,128]{1,0:T(8,128)(2,1)S(1)} %shard_map.74.rest_0_), channel_id=1, source_target_pairs={{0,1},{1,0},{2,3},{3,2},{4,5},{5,4},{6,7},{7,6},{8,9},{9,8},{10,11... | collective-permute-start | bytes 258056 | tf_op jit(solution)/shard_map/ppermute | solution.py:462
  58.8 2.7 %collective-permute-start.23 = (bf16[336,128]{1,0:T(8,128)(2,1)S(1)}, bf16[336,128]{1,0:T(8,128)(2,1)S(1)}, u32[]{:S(2)}, u32[]{:S(2)}) collective-permute-start(bf16[336,128]{1,0:T(8,128)(2,1)S(1)} %collective-permute-done.19.rest_3_), channel_id=1, source_target_pairs={{0,1},{1,0},{2,3},{3,2},{4,5},{5,4},{6,7},{7,6},{8,9},{9,8},{10,11... | collective-permute-start | bytes 258056 | tf_op jit(solution)/shard_map/ppermute | solution.py:462
  58.8 2.7 %collective-permute-start.22 = (bf16[336,128]{1,0:T(8,128)(2,1)S(1)}, bf16[336,128]{1,0:T(8,128)(2,1)S(1)}, u32[]{:S(2)}, u32[]{:S(2)}) collective-permute-start(bf16[336,128]{1,0:T(8,128)(2,1)S(1)} %collective-permute-done.18.rest_2_), channel_id=1, source_target_pairs={{0,1},{1,0},{2,3},{3,2},{4,5},{5,4},{6,7},{7,6},{8,9},{9,8},{10,11... | collective-permute-start | bytes 258056 | tf_op jit(solution)/shard_map/ppermute | solution.py:462
  59.3 2.2 %collective-permute-start.21 = (bf16[336,128]{1,0:T(8,128)(2,1)S(1)}, bf16[336,128]{1,0:T(8,128)(2,1)S(1)}, u32[]{:S(2)}, u32[]{:S(2)}) collective-permute-start(bf16[336,128]{1,0:T(8,128)(2,1)S(1)} %collective-permute-done.17.rest_1_), channel_id=1, source_target_pairs={{0,1},{1,0},{2,3},{3,2},{4,5},{5,4},{6,7},{7,6},{8,9},{9,8},{10,11... | collective-permute-start | bytes 258056 | tf_op jit(solution)/shard_map/ppermute | solution.py:462
  59.4 1.3 %collective-permute-start.15 = (bf16[2,128,128]{2,1,0:T(8,128)(2,1)S(1)}, bf16[2,128,128]{2,1,0:T(8,128)(2,1)S(1)}, u32[]{:S(2)}, u32[]{:S(2)}) collective-permute-start(bf16[2,128,128]{2,1,0:T(8,128)(2,1)S(1)} %collective-permute-done.11.rest_3_), channel_id=1, source_target_pairs={{0,1},{1,0},{2,3},{3,2},{4,5},{5,4},{6,7},{7,6},{8,9},{9,8},{10,11... | collective-permute-start | bytes 196616 | tf_op jit(solution)/shard_map/ppermute | solution.py:462
  64.0 7.3 %collective-permute-start.24 = (bf16[32,1536]{1,0:T(8,128)(2,1)S(1)}, bf16[32,1536]{1,0:T(8,128)(2,1)S(1)}, u32[]{:S(2)}, u32[]{:S(2)}) collective-permute-start(bf16[32,1536]{1,0:T(8,128)(2,1)S(1)} %get-tuple-element.67), channel_id=1, source_target_pairs={{0,2},{2,0},{4,6},{6,4},{1,3},{3,1},{5,7},{7,5},{8,10},{10,8},{12,... | collective-permute-start | bytes 294920 | tf_op jit(solution)/shard_map/ppermute | solution.py:462
  65.5 7.7 %collective-permute-start.25 = (bf16[32,1536]{1,0:T(8,128)(2,1)S(1)}, bf16[32,1536]{1,0:T(8,128)(2,1)S(1)}, u32[]{:S(2)}, u32[]{:S(2)}) collective-permute-start(bf16[32,1536]{1,0:T(8,128)(2,1)S(1)} %get-tuple-element.68), channel_id=1, source_target_pairs={{0,4},{2,6},{4,0},{6,2},{1,5},{3,7},{5,1},{7,3},{8,12},{10,14},{12... | collective-permute-start | bytes 294920 | tf_op jit(solution)/shard_map/ppermute | solution.py:462
  66.6 6.5 %collective-permute-start.26 = (bf16[32,1536]{1,0:T(8,128)(2,1)S(1)}, bf16[32,1536]{1,0:T(8,128)(2,1)S(1)}, u32[]{:S(2)}, u32[]{:S(2)}) collective-permute-start(bf16[32,1536]{1,0:T(8,128)(2,1)S(1)} %get-tuple-element.69), channel_id=1, source_target_pairs={{0,6},{2,4},{4,2},{6,0},{1,7},{3,5},{5,3},{7,1},{8,14},{10,12},{12... | collective-permute-start | bytes 294920 | tf_op jit(solution)/shard_map/ppermute | solution.py:462
  68.8 5.3 %collective-permute-start.27 = (bf16[32,1536]{1,0:T(8,128)(2,1)S(1)}, bf16[32,1536]{1,0:T(8,128)(2,1)S(1)}, u32[]{:S(2)}, u32[]{:S(2)}) collective-permute-start(bf16[32,1536]{1,0:T(8,128)(2,1)S(1)} %get-tuple-element.72), channel_id=1, source_target_pairs={{0,2},{2,0},{4,6},{6,4},{1,3},{3,1},{5,7},{7,5},{8,10},{10,8},{12,... | collective-permute-start | bytes 294920 | tf_op jit(solution)/shard_map/ppermute | solution.py:462
  70.2 6.7 %collective-permute-start.28 = (bf16[32,1536]{1,0:T(8,128)(2,1)S(1)}, bf16[32,1536]{1,0:T(8,128)(2,1)S(1)}, u32[]{:S(2)}, u32[]{:S(2)}) collective-permute-start(bf16[32,1536]{1,0:T(8,128)(2,1)S(1)} %get-tuple-element.73), channel_id=1, source_target_pairs={{0,4},{2,6},{4,0},{6,2},{1,5},{3,7},{5,1},{7,3},{8,12},{10,14},{12... | collective-permute-start | bytes 294920 | tf_op jit(solution)/shard_map/ppermute | solution.py:462
  71.3 5.6 %collective-permute-start.29 = (bf16[32,1536]{1,0:T(8,128)(2,1)S(1)}, bf16[32,1536]{1,0:T(8,128)(2,1)S(1)}, u32[]{:S(2)}, u32[]{:S(2)}) collective-permute-start(bf16[32,1536]{1,0:T(8,128)(2,1)S(1)} %get-tuple-element.74), channel_id=1, source_target_pairs={{0,6},{2,4},{4,2},{6,0},{1,7},{3,5},{5,3},{7,1},{8,14},{10,12},{12... | collective-permute-start | bytes 294920 | tf_op jit(solution)/shard_map/ppermute | solution.py:462

commit v3 on v2

--- a/solution.py
+++ b/solution.py
@@ -25,7 +25,6 @@
 F32 = jnp.float32
 BF16 = jnp.bfloat16
 VMEM = pl.BlockSpec(memory_space=pltpu.VMEM)
-SMEM = pl.BlockSpec(memory_space=pltpu.SMEM)
 HBM = pl.BlockSpec(memory_space=pltpu.HBM)
 PARAMS = pltpu.CompilerParams(vmem_limit_bytes=24 * 1024 * 1024)
 
@@ -55,15 +54,18 @@
 
 
 class Place:
-    def __init__(self, where, rows_n, cols_n):
-        self.row, self.col = where[0], where[1]
+    def __init__(self, rows_n, cols_n):
+        self.row = lax.axis_index("row")
+        self.core = lax.axis_index("core")
+        self.yx = lax.axis_index("yx")
+        self.col = self.yx * 2 + self.core
         self.rows_n, self.cols_n = rows_n, cols_n
         self.owner = self.row * cols_n + self.col
 
     def pairs(self, axis):
         at, n = (self.row, self.rows_n) if axis == 0 else (self.col, self.cols_n)
         before, after = at > 0, at < n - 1
-        odd = at % 2
+        odd = at & 1
         return [
             (odd == 0, ((True, after), (False, before))),
             (odd == 1, ((False, before), (True, after))),
@@ -167,10 +169,10 @@
 
 
 def first_kernel(
-    z, grid, where, membrane, picture, source, own, *rest
+    z, grid, membrane, picture, source, own, *rest
 ):
     (*sends, pixels, dic, potential, atoms, tall_sum, spread, drawing, sems) = rest
-    place = Place(where, *grid)
+    place = Place(*grid)
     early = [
         pltpu.make_async_copy(picture, drawing, sems.at[SPAN]),
         pltpu.make_async_copy(membrane, potential, sems.at[SPAN + 1]),
@@ -195,8 +197,8 @@
     atoms[...] = dic[pl.ds(pl.multiple_of(place.owner * owned, owned), owned), :]
 
 
-def side_kernel(z, grid, where, own, from_even, from_odd, joined, even, odd, rim):
-    place = Place(where, *grid)
+def side_kernel(z, grid, own, from_even, from_odd, joined, even, odd, rim):
+    place = Place(*grid)
     joined[...] = own[...]
     add_sides(z, place, joined, (from_even, from_odd))
     rim[MARGIN * z.wide :, :] = jnp.zeros((z.rim - MARGIN * z.wide, z.lanes), F32)
@@ -236,13 +238,13 @@
 
 
 def sweep_kernel(
-    z, grid, last, where, potential, joined, from_even, from_odd, pixels, dic, *rest
+    z, grid, last, potential, joined, from_even, from_odd, pixels, dic, *rest
 ):
     if last:
         new_potential, own, *sends, codes, tall_sum, whole, wide_part, rim = rest
     else:
         new_potential, own, *sends, tall_sum, whole, wide_part, rim = rest
-    place = Place(where, *grid)
+    place = Place(*grid)
     whole[...] = joined[...]
     add_ends(z, place, whole, (from_even, from_odd), rim)
     windows_of(z, whole, wide_part, 0, z.cols)
@@ -268,7 +270,7 @@
     send_sides(z, place, own, sends)
 
 
-def sort_kernel(z, grid, groups, where, codes, _, *messages):
+def sort_kernel(z, grid, groups, codes, _, *messages):
     rows_n, cores_n, owned = groups
     span = z.atoms // rows_n
     src = lax.broadcasted_iota(jnp.int32, (span, span), 0)
@@ -277,7 +279,7 @@
     core, rem = lax.div(dst, per_core), lax.rem(dst, per_core)
     wanted = lax.div(rem, owned) * (owned * cores_n) + core * owned + lax.rem(rem, owned)
     order = is_equal(src, wanted)
-    place = Place(where, *grid)
+    place = Place(*grid)
     for x, message in enumerate(messages):
         r = place.row ^ x if rows_n & (rows_n - 1) == 0 else (place.row - x) % rows_n
         block = codes[:, pl.ds(pl.multiple_of(r * span, span), span)]
@@ -286,12 +288,12 @@
             message[k] = line[:, k * per_core : (k + 1) * per_core]
 
 
-def turn_kernel(z, grid, groups, where, *rest):
+def turn_kernel(z, grid, groups, *rest):
     rows_n, cores_n, _ = groups
     stride = rows_n * cores_n * z.cols
     near, far, (across, codes) = rest[:rows_n], rest[rows_n : 2 * rows_n], rest[2 * rows_n :]
-    place = Place(where, *grid)
-    mine = place.col % 2
+    place = Place(*grid)
+    mine = place.core
     for x in range(rows_n):
         d = offset(place.row, x, rows_n)
         for k, message in ((mine, near[x]), (1 - mine, far[x])):
@@ -304,9 +306,9 @@
     across[...] = codes[...].astype(F32).T.astype(BF16)
 
 
-def pack_kernel(z, grid, where, own, from_even, from_odd, packed, joined, flat):
+def pack_kernel(z, grid, own, from_even, from_odd, packed, joined, flat):
     joined[...] = own[...]
-    add_sides(z, Place(where, *grid), joined, (from_even, from_odd))
+    add_sides(z, Place(*grid), joined, (from_even, from_odd))
     base = z.tall * z.cols
     flat[base:, :] = jnp.zeros((z.packed - base, z.lanes), F32)
     for p in range(z.tall):
@@ -325,7 +327,7 @@
     return at ^ step if n & (n - 1) == 0 else (at + step) % n
 
 
-def learn_half(z, grid, where, across, wide_part, stride, bands, outs, partial):
+def learn_half(z, grid, across, wide_part, stride, bands, outs, partial):
     count = z.rows * stride
     for n, i in enumerate(bands):
         term = jnp.dot(
@@ -333,13 +335,13 @@
         )
         partial[:, n * z.band : (n + 1) * z.band] = (term * z.scale).astype(BF16)
     owned = outs[0].shape[0]
-    place = Place(where, *grid)
+    place = Place(*grid)
     for step, out in enumerate(outs):
-        at = offset(place.col // 2, step, len(outs))
+        at = offset(place.yx, step, len(outs))
         out[...] = partial[pl.ds(pl.multiple_of(at * owned, owned), owned), :]
 
 
-def learn_kernel(z, grid, groups, yx_n, where, across, *rest):
+def learn_kernel(z, grid, groups, yx_n, across, *rest):
     rows_n, cores_n, _ = groups
     members = rows_n * cores_n
     near, far, outs = rest[:rows_n], rest[rows_n : 2 * rows_n], rest[2 * rows_n :]
@@ -348,8 +350,8 @@
     base = z.tall * z.cols
     half = z.packed // 2
     tail = z.cell - 128
-    place = Place(where, *grid)
-    mine = place.col % 2
+    place = Place(*grid)
+    mine = place.core
 
     for x in range(rows_n):
         d = offset(place.row, x, rows_n)
@@ -385,46 +387,52 @@
                         whole[at : at + n, z.cols + c, :] += side[c]
             windows_of(z, whole, wide_part, d * z.cols, stride)
     learn_half(
-        z, grid, where, across[...], wide_part, stride, range(SPAN // 2), outs, partial
-    )
-
-
-def rest_kernel(z, grid, stride, where, across, wide_part, *rest):
+        z, grid, across[...], wide_part, stride, range(SPAN // 2), outs, partial
+    )
+
+
+def rest_kernel(z, grid, stride, across, wide_part, *rest):
     *outs, partial = rest
     learn_half(
-        z, grid, where, across[...], wide_part, stride, range(SPAN // 2, SPAN), outs, partial
-    )
-
-
-def finish_kernel(z, yx_n, where, momentum, atoms, *rest):
-    *parts, new_dictionary, new_momentum, weights, updated, sems = rest
+        z, grid, across[...], wide_part, stride, range(SPAN // 2, SPAN), outs, partial
+    )
+
+
+def half_finished(half, momentum, atoms, parts, updated, weights):
+    lanes = pl.ds(half * weights.shape[1], weights.shape[1])
+    learning = parts[0][...].astype(F32)
+    for part in parts[1:]:
+        learning = learning + part[...].astype(F32)
+    momentum_out = DECAY * momentum[:, lanes] + learning
+    updated[...] = momentum_out
+    weight = atoms[:, lanes].astype(F32) + LEARNING * momentum_out
+    weights[...] = weight
+    return jnp.sum(weight * weight, axis=1, keepdims=True)
+
+
+def early_kernel(momentum, atoms, *rest):
+    *parts, updated, weights, power = rest
+    total = half_finished(0, momentum, atoms, parts, updated, weights)
+    power[...] = jnp.broadcast_to(total, power.shape)
+
+
+def finish_kernel(z, first_updated, first_weights, first_power, momentum, atoms, *rest):
+    *parts, new_dictionary, new_momentum, updated, weights, scaled, sems = rest
     width = z.patch // 2
-    power = 0.0
-    copies = []
-    for h in range(2):
-        lanes = pl.ds(h * width, width)
-        learning = parts[h * yx_n][...].astype(F32)
-        for part in parts[h * yx_n + 1 : (h + 1) * yx_n]:
-            learning = learning + part[...].astype(F32)
-        momentum_out = DECAY * momentum[:, lanes] + learning
-        updated[:, lanes] = momentum_out
-        copies.append(
-            pltpu.make_async_copy(updated.at[:, lanes], new_momentum.at[:, lanes], sems.at[h])
-        )
-        copies[-1].start()
-        weight = atoms[:, lanes].astype(F32) + LEARNING * momentum_out
-        weights[:, lanes] = weight
-        power = power + jnp.sum(weight * weight, axis=1, keepdims=True)
-    norm = lax.rsqrt(power * (1.0 / z.patch) + EPSILON)
-    for h in range(2):
-        lanes = pl.ds(h * width, width)
-        weights[:, lanes] = weights[:, lanes] * norm
-        copies.append(
-            pltpu.make_async_copy(
-                weights.at[:, lanes], new_dictionary.at[:, lanes], sems.at[2 + h]
-            )
-        )
-        copies[-1].start()
+    halves = [pl.ds(0, width), pl.ds(width, width)]
+    copies = [
+        pltpu.make_async_copy(first_updated, new_momentum.at[:, halves[0]], sems.at[0]),
+        pltpu.make_async_copy(updated, new_momentum.at[:, halves[1]], sems.at[1]),
+        pltpu.make_async_copy(scaled.at[0], new_dictionary.at[:, halves[0]], sems.at[2]),
+        pltpu.make_async_copy(scaled.at[1], new_dictionary.at[:, halves[1]], sems.at[3]),
+    ]
+    copies[0].start()
+    power = half_finished(1, momentum, atoms, parts, updated, weights)
+    copies[1].start()
+    norm = lax.rsqrt((first_power[:, 0:1] + power) * (1.0 / z.patch) + EPSILON)
+    for h, source in enumerate((first_weights, weights)):
+        scaled[h] = source[...] * norm
+        copies[2 + h].start()
     for copy in copies:
         copy.wait()
 
@@ -434,9 +442,8 @@
 
 
 def call(kernel, outs, inputs, scratch, far=0, leave=VMEM):
-    specs = [SMEM] + [HBM] * far + [VMEM] * (len(inputs) - 1 - far)
-    where, *others = inputs
-    placed = [kept(x, pltpu.HBM) for x in others[:far]] + [kept(x) for x in others[far:]]
+    specs = [HBM] * far + [VMEM] * (len(inputs) - far)
+    placed = [kept(x, pltpu.HBM) for x in inputs[:far]] + [kept(x) for x in inputs[far:]]
     return pl.pallas_call(
         kernel,
         out_shape=outs,
@@ -444,7 +451,7 @@
         out_specs=[leave] * len(outs),
         scratch_shapes=scratch,
         compiler_params=PARAMS,
-    )(where, *placed)
+    )(*placed)
 
 
 def shards(picture, membrane, dictionary, momentum):
@@ -456,7 +463,6 @@
     groups = (rows_n, cores_n, owned)
     members = rows_n * cores_n
     grid = (rows_n, cols_n)
-    where = jnp.stack([lax.axis_index("row"), lax.axis_index(("yx", "core"))]).astype(jnp.int32)
 
     def met(block, axis, n, step):
         return lax.ppermute(block, axis, [(i, offset(i, step, n)) for i in range(n)])
@@ -489,7 +495,7 @@
             site_v,
             pltpu.VMEM(momentum.shape, BF16),
         ],
-        (where, membrane.reshape(z.sites, atom_count), picture, dictionary),
+        (membrane.reshape(z.sites, atom_count), picture, dictionary),
         [
             tall_v,
             pltpu.VMEM((3 * picture.shape[2], z.cell), BF16),
@@ -503,7 +509,7 @@
         joined, *ends = call(
             functools.partial(side_kernel, z, grid),
             [own_v, end_v, end_v],
-            (where, own, *sideways(sides)),
+            (own, *sideways(sides)),
             [rim_v],
         )
         ends = swapped("row", rows_n, ends)
@@ -515,7 +521,7 @@
         potential, own, *rest = call(
             functools.partial(sweep_kernel, z, grid, last),
             final if last else [site_v] + outs,
-            (where, potential, joined, *ends, pixels, dic),
+            (potential, joined, *ends, pixels, dic),
             [tall_v, own_v, wide_v, rim_v],
         )
         sides = rest[:2]
@@ -525,7 +531,7 @@
     messages = call(
         functools.partial(sort_kernel, z, grid, groups),
         [message_v] * rows_n,
-        (where, rest[2], sides[0]),
+        (rest[2], sides[0]),
         [],
     )
     power = rows_n & (rows_n - 1) == 0
@@ -544,7 +550,7 @@
     (packed,) = call(
         functools.partial(pack_kernel, z, grid),
         [pltpu.VMEM((z.packed * 3 // 2, 128), BF16)],
-        (where, own, *sides),
+        (own, *sides),
         [own_v, flat_v],
     )
 
@@ -557,13 +563,13 @@
     (across,) = call(
         functools.partial(turn_kernel, z, grid, groups),
         [pltpu.VMEM((group_atoms, members * z.sites), BF16)],
-        (where, *near_codes, *far_codes),
+        (*near_codes, *far_codes),
         [pltpu.VMEM((members * z.sites, group_atoms), BF16)],
     )
     *first_half, wide_part = call(
         functools.partial(learn_kernel, z, grid, groups, yx_n),
         [half_v] * yx_n + [pltpu.VMEM((z.tall * stride, z.band), BF16)],
-        (where, across, *near, *far),
+        (across, *near, *far),
         [
             partial_v,
             pltpu.VMEM((cores_n, rows_n, z.packed, z.lanes), F32),
@@ -573,21 +579,28 @@
     other_half = call(
         functools.partial(rest_kernel, z, grid, stride),
         [half_v] * yx_n,
-        (where, across, wide_part),
+        (across, wide_part),
         [partial_v],
     )
     parts = [
-        block if step == 0 else met(block, "yx", yx_n, step)
+        [block if step == 0 else met(block, "yx", yx_n, step) for step, block in enumerate(half)]
         for half in (first_half, other_half)
-        for step, block in enumerate(half)
     ]
+    wide_half = (owned, z.patch // 2)
+    early = call(
+        early_kernel,
+        [pltpu.VMEM(s, F32) for s in (wide_half, wide_half, (owned, 128))],
+        (momentum, atoms, *parts[0]),
+        [],
+    )
     new_dictionary, new_momentum = call(
-        functools.partial(finish_kernel, z, yx_n),
+        functools.partial(finish_kernel, z),
         [jax.ShapeDtypeStruct(momentum.shape, F32)] * 2,
-        (where, momentum, atoms, *parts),
+        (*early, momentum, atoms, *parts[1]),
         [
-            pltpu.VMEM(momentum.shape, F32),
-            pltpu.VMEM(momentum.shape, F32),
+            pltpu.VMEM(wide_half, F32),
+            pltpu.VMEM(wide_half, F32),
+            pltpu.VMEM((2,) + wide_half, F32),
             pltpu.SemaphoreType.DMA((4,)),
         ],
         leave=HBM,

time: 78.8 us -> 72.8 us (0.924)
  Pallas kernels: 22 us -> 16 us
    pallas_call x11 -> x12, Pallas kernels: 22 us -> 16 us  [call(): pl.pallas_call(kernel, out_shape=outs, in_specs=specs, out_specs=[leave]...]
  transfers between devices with their start and end apart: 30 -> 30, of which waited for: 12 -> 13; matrix products, arithmetic and copies ran while one was open for 1% -> 1% of each run, Pallas kernels for 4% -> 2%
where the time goes in v3:
time: 72.8 us; the launch traced here: 72.6 us
  starting transfers between devices  30.9 us (42%)
  waiting for transfers between devices  24 us (33%)
  Pallas kernels  16 us (22%)
  between operations  0.95 us (1%)
  local copies, waits for them, and re-layouts  0.8 us (1%)
    ppermute x20, starting transfers between devices, met(): lax.ppermute(block, axis, [(i, offset(i, step, n)) for i in range(n)])  17.7 us
    pallas_call x12, Pallas kernels, call(): pl.pallas_call(kernel, out_shape=outs, in_specs=specs, out_specs=[leave]...  16 us
    ppermute x20, waiting for transfers between devices, met(): lax.ppermute(block, axis, [(i, offset(i, step, n)) for i in range(n)])  8.65 us
    ppermute x3, waiting for transfers between devices, sideways(): far_rim = lax.ppermute(blocks[1], ('yx', 'core'), odd)  7.62 us
    ppermute x4, starting transfers between devices, swapped(): lax.ppermute(b, axis, route)  6.87 us
    ppermute x4, waiting for transfers between devices, swapped(): lax.ppermute(b, axis, route)  6.49 us
    ppermute x3, starting transfers between devices, sideways(): far_rim = lax.ppermute(blocks[1], ('yx', 'core'), odd)  5.6 us
  transfers between devices with their start and end apart: 30, of which 13 were waited for; matrix products, arithmetic and copies ran while one was open for 1% of the time, Pallas kernels for 2%

profile of v3, /device:TPU:0, one launch (start us, length us, event | category | flops | bytes accessed | tf_op | source)
XLA Modules:
  0.0 72.6 jit_solution(6048798132221578704)
XLA Ops:
  0.6 3.9 %shard_map.67 = (f32[11,24,256]{2,1,0:T(8,128)S(1)}, bf16[3,16,256]{2,1,0:T(8,128)(2,1)S(1)}, bf16[3,16,256]{2,1,0:T(8,128)(2,1)S(1)}, f32[128,192]{1,0:T(8,128)...) custom-call(f32[128,1024]{1,0:T(8,128)} %bitcast.3, ...), custom_call_target="tpu_custom_call" | custom-call | tf_op jit(solution)/shard_map/pallas_call | solution.py:447
  5.0 3.5 %collective-permute-start.1 = (bf16[3,16,256]{2,1,0:T(8,128)(2,1)S(1)}, bf16[3,16,256]{2,1,0:T(8,128)(2,1)S(1)}, u32[]{:S(2)}, u32[]{:S(2)}) collective-permute-start(bf16[3,16,256]{2,1,0:T(8,128)(2,1)S(1)} %get-tuple-element.46), channel_id=1, source_target_pairs={{0,7},{1,2},{2,1},{3,4},{4,3},{5,6},{6,5},{7,0},{8,15},{9,10},{10,... | collective-permute-start | bytes 73736 | tf_op jit(solution)/shard_map/ppermute | solution.py:476
  8.6 1.5 %collective-permute-done.1.from_odd = bf16[3,16,256]{2,1,0:T(8,128)(2,1)S(1)} collective-permute-done((bf16[3,16,256]{2,1,0:T(8,128)(2,1)S(1)}, bf16[3,16,256]{2,1,0:T(8,128)(2,1)S(1)}, u32[]{:S(2)}, u32[]{:S(2)}) %collective-permute-start.1) | collective-permute-done | bytes 24608 | tf_op jit(solution)/shard_map/ppermute | solution.py:476
  10.2 1.8 %collective-permute-start.2 = (bf16[64,256]{1,0:T(8,128)(2,1)S(1)}, bf16[64,256]{1,0:T(8,128)(2,1)S(1)}, u32[]{:S(2)}, u32[]{:S(2)}) collective-permute-start(bf16[64,256]{1,0:T(8,128)(2,1)S(1)} %get-tuple-element.48), channel_id=1, source_target_pairs={{0,8},{8,0},{16,24},{24,16},{1,9},{9,1},{17,25},{25,17},{2,10},{10... | collective-permute-start | bytes 98312 | tf_op jit(solution)/shard_map/ppermute | solution.py:471
  12.0 2.5 %collective-permute-start.3 = (bf16[64,256]{1,0:T(8,128)(2,1)S(1)}, bf16[64,256]{1,0:T(8,128)(2,1)S(1)}, u32[]{:S(2)}, u32[]{:S(2)}) collective-permute-start(bf16[64,256]{1,0:T(8,128)(2,1)S(1)} %get-tuple-element.49), channel_id=1, source_target_pairs={{0,24},{8,16},{16,8},{24,0},{1,25},{9,17},{17,9},{25,1},{2,26},{10... | collective-permute-start | bytes 98312 | tf_op jit(solution)/shard_map/ppermute | solution.py:471
  14.5 3.2 %collective-permute-done.3.from_odd = bf16[64,256]{1,0:T(8,128)(2,1)S(1)} collective-permute-done((bf16[64,256]{1,0:T(8,128)(2,1)S(1)}, bf16[64,256]{1,0:T(8,128)(2,1)S(1)}, u32[]{:S(2)}, u32[]{:S(2)}) %collective-permute-start.3) | collective-permute-done | bytes 32800 | tf_op jit(solution)/shard_map/ppermute | solution.py:471
  17.7 3.8 %shard_map.69 = (f32[128,1024]{1,0:T(8,128)S(1)}, f32[11,24,256]{2,1,0:T(8,128)S(1)}, bf16[3,16,256]{2,1,0:T(8,128)(2,1)S(1)}, bf16[3,16,256]{2,1,0:T(8,128)(2,1)S(1)}) custom-call(f32[128,1024]{1,0:T(8,128)S(1)} %get-tuple-element.43.potential, f32[11,24,256]{2,1,0:T(8,128)S(1)} %get-tuple-element.47.joined, ...), custom_call_target="tpu_custom_call" | custom-call | tf_op jit(solution)/shard_map/pallas_call | solution.py:447
  21.5 2.0 %collective-permute-start.5 = (bf16[3,16,256]{2,1,0:T(8,128)(2,1)S(1)}, bf16[3,16,256]{2,1,0:T(8,128)(2,1)S(1)}, u32[]{:S(2)}, u32[]{:S(2)}) collective-permute-start(bf16[3,16,256]{2,1,0:T(8,128)(2,1)S(1)} %get-tuple-element.55), channel_id=1, source_target_pairs={{0,7},{1,2},{2,1},{3,4},{4,3},{5,6},{6,5},{7,0},{8,15},{9,10},{10,... | collective-permute-start | bytes 73736 | tf_op jit(solution)/shard_map/ppermute | solution.py:476
  23.5 2.3 %collective-permute-done.5.from_odd = bf16[3,16,256]{2,1,0:T(8,128)(2,1)S(1)} collective-permute-done((bf16[3,16,256]{2,1,0:T(8,128)(2,1)S(1)}, bf16[3,16,256]{2,1,0:T(8,128)(2,1)S(1)}, u32[]{:S(2)}, u32[]{:S(2)}) %collective-permute-start.5) | collective-permute-done | bytes 24608 | tf_op jit(solution)/shard_map/ppermute | solution.py:476
  25.9 2.5 %collective-permute-start.7 = (bf16[64,256]{1,0:T(8,128)(2,1)S(1)}, bf16[64,256]{1,0:T(8,128)(2,1)S(1)}, u32[]{:S(2)}, u32[]{:S(2)}) collective-permute-start(bf16[64,256]{1,0:T(8,128)(2,1)S(1)} %get-tuple-element.58), channel_id=1, source_target_pairs={{0,24},{8,16},{16,8},{24,0},{1,25},{9,17},{17,9},{25,1},{2,26},{10... | collective-permute-start | bytes 98312 | tf_op jit(solution)/shard_map/ppermute | solution.py:471
  28.5 1.4 %collective-permute-done.6.from_even = bf16[64,256]{1,0:T(8,128)(2,1)S(1)} collective-permute-done((bf16[64,256]{1,0:T(8,128)(2,1)S(1)}, bf16[64,256]{1,0:T(8,128)(2,1)S(1)}, u32[]{:S(2)}, u32[]{:S(2)}) %collective-permute-start.6) | collective-permute-done | bytes 32800 | tf_op jit(solution)/shard_map/ppermute | solution.py:471
  29.8 1.9 %collective-permute-done.7.from_odd = bf16[64,256]{1,0:T(8,128)(2,1)S(1)} collective-permute-done((bf16[64,256]{1,0:T(8,128)(2,1)S(1)}, bf16[64,256]{1,0:T(8,128)(2,1)S(1)}, u32[]{:S(2)}, u32[]{:S(2)}) %collective-permute-start.7) | collective-permute-done | bytes 32800 | tf_op jit(solution)/shard_map/ppermute | solution.py:471
  31.7 3.8 %shard_map.71 = (f32[128,1024]{1,0:T(8,128)S(1)}, f32[11,24,256]{2,1,0:T(8,128)S(1)}, bf16[3,16,256]{2,1,0:T(8,128)(2,1)S(1)}, bf16[3,16,256]{2,1,0:T(8,128)(2,1)S(1)}, bf16[128,1024]{1,0:T(8,128)(2,1)S(1)}) custom-call(f32[128,1024]{1,0:T(8,128)S(1)} %get-tuple-element.52.potential, f32[11,24,256]{2,1,0:T(8,128)S(1)} %get-tuple-element.56.joined, ...), custom_call_target="tpu_custom_call" | custom-call | tf_op jit(solution)/shard_map/pallas_call | solution.py:447
  35.6 1.2 %collective-permute-done.8._.from_even = bf16[3,16,256]{2,1,0:T(8,128)(2,1)S(1)} collective-permute-done((bf16[3,16,256]{2,1,0:T(8,128)(2,1)S(1)}, bf16[3,16,256]{2,1,0:T(8,128)(2,1)S(1)}, u32[]{:S(2)}, u32[]{:S(2)}) %collective-permute-start.8) | collective-permute-done | bytes 24608 | tf_op jit(solution)/shard_map/ppermute | solution.py:475
  37.2 2.9 %collective-permute-start.10 = (bf16[2,128,128]{2,1,0:T(8,128)(2,1)S(1)}, bf16[2,128,128]{2,1,0:T(8,128)(2,1)S(1)}, u32[]{:S(2)}, u32[]{:S(2)}) collective-permute-start(bf16[2,128,128]{2,1,0:T(8,128)(2,1)S(1)} %get-tuple-element.65), channel_id=1, source_target_pairs={{0,16},{8,24},{16,0},{24,8},{1,17},{9,25},{17,1},{25,9},{2,18},{10... | collective-permute-start | bytes 196616 | tf_op jit(solution)/shard_map/ppermute | solution.py:468
  40.1 1.4 %collective-permute-start.11 = (bf16[2,128,128]{2,1,0:T(8,128)(2,1)S(1)}, bf16[2,128,128]{2,1,0:T(8,128)(2,1)S(1)}, u32[]{:S(2)}, u32[]{:S(2)}) collective-permute-start(bf16[2,128,128]{2,1,0:T(8,128)(2,1)S(1)} %get-tuple-element.66), channel_id=1, source_target_pairs={{0,24},{8,16},{16,8},{24,0},{1,25},{9,17},{17,9},{25,1},{2,26},{10... | collective-permute-start | bytes 196616 | tf_op jit(solution)/shard_map/ppermute | solution.py:468
  41.7 3.9 %collective-permute-done.16.from_odd = bf16[3,16,256]{2,1,0:T(8,128)(2,1)S(1)} collective-permute-done((bf16[3,16,256]{2,1,0:T(8,128)(2,1)S(1)}, bf16[3,16,256]{2,1,0:T(8,128)(2,1)S(1)}, u32[]{:S(2)}, u32[]{:S(2)}) %collective-permute-start.16) | collective-permute-done | bytes 24608 | tf_op jit(solution)/shard_map/ppermute | solution.py:476
  45.9 2.5 %collective-permute-start.19 = (bf16[336,128]{1,0:T(8,128)(2,1)S(1)}, bf16[336,128]{1,0:T(8,128)(2,1)S(1)}, u32[]{:S(2)}, u32[]{:S(2)}) collective-permute-start(bf16[336,128]{1,0:T(8,128)(2,1)S(1)} %shard_map.74.rest_0_), channel_id=1, source_target_pairs={{0,24},{8,16},{16,8},{24,0},{1,25},{9,17},{17,9},{25,1},{2,26},{10... | collective-permute-start | bytes 258056 | tf_op jit(solution)/shard_map/ppermute | solution.py:468
  48.5 1.9 %collective-permute-start.17 = (bf16[336,128]{1,0:T(8,128)(2,1)S(1)}, bf16[336,128]{1,0:T(8,128)(2,1)S(1)}, u32[]{:S(2)}, u32[]{:S(2)}) collective-permute-start(bf16[336,128]{1,0:T(8,128)(2,1)S(1)} %shard_map.74.rest_0_), channel_id=1, source_target_pairs={{0,8},{8,0},{16,24},{24,16},{1,9},{9,1},{17,25},{25,17},{2,10},{10... | collective-permute-start | bytes 258056 | tf_op jit(solution)/shard_map/ppermute | solution.py:468
  50.9 2.1 %collective-permute-done.19.rest_3_ = bf16[336,128]{1,0:T(8,128)(2,1)S(1)} collective-permute-done((bf16[336,128]{1,0:T(8,128)(2,1)S(1)}, bf16[336,128]{1,0:T(8,128)(2,1)S(1)}, u32[]{:S(2)}, u32[]{:S(2)}) %collective-permute-start.19) | collective-permute-done | bytes 86048 | tf_op jit(solution)/shard_map/ppermute | solution.py:468
  53.0 1.8 %collective-permute-done.18.rest_2_ = bf16[336,128]{1,0:T(8,128)(2,1)S(1)} collective-permute-done((bf16[336,128]{1,0:T(8,128)(2,1)S(1)}, bf16[336,128]{1,0:T(8,128)(2,1)S(1)}, u32[]{:S(2)}, u32[]{:S(2)}) %collective-permute-start.18) | collective-permute-done | bytes 86048 | tf_op jit(solution)/shard_map/ppermute | solution.py:468
  55.8 0.9 %collective-permute-done.15.rest_7_ = bf16[2,128,128]{2,1,0:T(8,128)(2,1)S(1)} collective-permute-done((bf16[2,128,128]{2,1,0:T(8,128)(2,1)S(1)}, bf16[2,128,128]{2,1,0:T(8,128)(2,1)S(1)}, u32[]{:S(2)}, u32[]{:S(2)}) %collective-permute-start.15) | collective-permute-done | bytes 65568 | tf_op jit(solution)/shard_map/ppermute | solution.py:468
  57.0 1.9 %shard_map.75 = (bf16[32,1536]{1,0:T(8,128)(2,1)S(1)}, bf16[32,1536]{1,0:T(8,128)(2,1)S(1)}, bf16[32,1536]{1,0:T(8,128)(2,1)S(1)}, bf16[32,1536]{1,0:T(8,128)(2,1)S(1)}, bf16[1408,768]{1,0:T(8,128)(2,1)S(1)}) custom-call(bf16[128,1024]{1,0:T(8,128)(2,1)S(1)} %shard_map.73.across, bf16[336,128]{1,0:T(8,128)(2,1)S(1)} %shard_map.74.rest_0_, ...), custom_call_target="tpu_custom_call" | custom-call | tf_op jit(solution)/shard_map/pallas_call | solution.py:447
  58.9 1.4 %collective-permute-start.24 = (bf16[32,1536]{1,0:T(8,128)(2,1)S(1)}, bf16[32,1536]{1,0:T(8,128)(2,1)S(1)}, u32[]{:S(2)}, u32[]{:S(2)}) collective-permute-start(bf16[32,1536]{1,0:T(8,128)(2,1)S(1)} %get-tuple-element.70), channel_id=1, source_target_pairs={{0,2},{2,0},{4,6},{6,4},{1,3},{3,1},{5,7},{7,5},{8,10},{10,8},{12,... | collective-permute-start | bytes 294920 | tf_op jit(solution)/shard_map/ppermute | solution.py:468
  60.3 1.1 %collective-permute-start.25 = (bf16[32,1536]{1,0:T(8,128)(2,1)S(1)}, bf16[32,1536]{1,0:T(8,128)(2,1)S(1)}, u32[]{:S(2)}, u32[]{:S(2)}) collective-permute-start(bf16[32,1536]{1,0:T(8,128)(2,1)S(1)} %get-tuple-element.71), channel_id=1, source_target_pairs={{0,4},{2,6},{4,0},{6,2},{1,5},{3,7},{5,1},{7,3},{8,12},{10,14},{12... | collective-permute-start | bytes 294920 | tf_op jit(solution)/shard_map/ppermute | solution.py:468
  61.4 1.0 %collective-permute-start.26 = (bf16[32,1536]{1,0:T(8,128)(2,1)S(1)}, bf16[32,1536]{1,0:T(8,128)(2,1)S(1)}, u32[]{:S(2)}, u32[]{:S(2)}) collective-permute-start(bf16[32,1536]{1,0:T(8,128)(2,1)S(1)} %get-tuple-element.72), channel_id=1, source_target_pairs={{0,6},{2,4},{4,2},{6,0},{1,7},{3,5},{5,3},{7,1},{8,14},{10,12},{12... | collective-permute-start | bytes 294920 | tf_op jit(solution)/shard_map/ppermute | solution.py:468
  63.1 1.4 %collective-permute-start.27 = (bf16[32,1536]{1,0:T(8,128)(2,1)S(1)}, bf16[32,1536]{1,0:T(8,128)(2,1)S(1)}, u32[]{:S(2)}, u32[]{:S(2)}) collective-permute-start(bf16[32,1536]{1,0:T(8,128)(2,1)S(1)} %get-tuple-element.78), channel_id=1, source_target_pairs={{0,2},{2,0},{4,6},{6,4},{1,3},{3,1},{5,7},{7,5},{8,10},{10,8},{12,... | collective-permute-start | bytes 294920 | tf_op jit(solution)/shard_map/ppermute | solution.py:468
  64.5 1.1 %collective-permute-start.28 = (bf16[32,1536]{1,0:T(8,128)(2,1)S(1)}, bf16[32,1536]{1,0:T(8,128)(2,1)S(1)}, u32[]{:S(2)}, u32[]{:S(2)}) collective-permute-start(bf16[32,1536]{1,0:T(8,128)(2,1)S(1)} %get-tuple-element.79), channel_id=1, source_target_pairs={{0,4},{2,6},{4,0},{6,2},{1,5},{3,7},{5,1},{7,3},{8,12},{10,14},{12... | collective-permute-start | bytes 294920 | tf_op jit(solution)/shard_map/ppermute | solution.py:468
  65.6 1.0 %collective-permute-start.29 = (bf16[32,1536]{1,0:T(8,128)(2,1)S(1)}, bf16[32,1536]{1,0:T(8,128)(2,1)S(1)}, u32[]{:S(2)}, u32[]{:S(2)}) collective-permute-start(bf16[32,1536]{1,0:T(8,128)(2,1)S(1)} %get-tuple-element.80), channel_id=1, source_target_pairs={{0,6},{2,4},{4,2},{6,0},{1,7},{3,5},{5,3},{7,1},{8,14},{10,12},{12... | collective-permute-start | bytes 294920 | tf_op jit(solution)/shard_map/ppermute | solution.py:468
  68.2 1.2 %collective-permute-done.27.rest_1_ = bf16[32,1536]{1,0:T(8,128)(2,1)S(1)} collective-permute-done((bf16[32,1536]{1,0:T(8,128)(2,1)S(1)}, bf16[32,1536]{1,0:T(8,128)(2,1)S(1)}, u32[]{:S(2)}, u32[]{:S(2)}) %collective-permute-start.27) | collective-permute-done | bytes 98336 | tf_op jit(solution)/shard_map/ppermute | solution.py:468
  69.4 2.1 %collective-permute-done.28.rest_2_ = bf16[32,1536]{1,0:T(8,128)(2,1)S(1)} collective-permute-done((bf16[32,1536]{1,0:T(8,128)(2,1)S(1)}, bf16[32,1536]{1,0:T(8,128)(2,1)S(1)}, u32[]{:S(2)}, u32[]{:S(2)}) %collective-permute-start.28) | collective-permute-done | bytes 98336 | tf_op jit(solution)/shard_map/ppermute | solution.py:468
  71.4 1.0 %shard_map.78 = (f32[32,3072]{1,0:T(8,128)}, f32[32,3072]{1,0:T(8,128)}) custom-call(f32[32,1536]{1,0:T(8,128)S(1)} %get-tuple-element.73.first_updated, f32[32,1536]{1,0:T(8,128)S(1)} %get-tuple-element.74.first_weights, f32[32,128]{1,0:T(8,128)S(1)} %get-tuple-element.75.first_power, f32[32,3072]{1,0:T(8,128)S(1)} %copy-done, ...), custom_call_target="tpu_custom_call" | custom-call | tf_op jit(solution)/shard_map/pallas_call | solution.py:447
  (43 shorter events, 6.0 us)
Async XLA Ops:
  4.5 4.1 %collective-permute-start = (bf16[3,16,256]{2,1,0:T(8,128)(2,1)S(1)}, bf16[3,16,256]{2,1,0:T(8,128)(2,1)S(1)}, u32[]{:S(2)}, u32[]{:S(2)}) collective-permute-start(bf16[3,16,256]{2,1,0:T(8,128)(2,1)S(1)} %get-tuple-element.45), channel_id=1, source_target_pairs={{0,1},{1,0},{2,3},{3,2},{4,5},{5,4},{6,7},{7,6},{8,9},{9,8},{10,11... | collective-permute-start | bytes 73736 | tf_op jit(solution)/shard_map/ppermute | solution.py:475
  5.0 5.1 %collective-permute-start.1 = (bf16[3,16,256]{2,1,0:T(8,128)(2,1)S(1)}, bf16[3,16,256]{2,1,0:T(8,128)(2,1)S(1)}, u32[]{:S(2)}, u32[]{:S(2)}) collective-permute-start(bf16[3,16,256]{2,1,0:T(8,128)(2,1)S(1)} %get-tuple-element.46), channel_id=1, source_target_pairs={{0,7},{1,2},{2,1},{3,4},{4,3},{5,6},{6,5},{7,0},{8,15},{9,10},{10,... | collective-permute-start | bytes 73736 | tf_op jit(solution)/shard_map/ppermute | solution.py:476
  10.2 4.3 %collective-permute-start.2 = (bf16[64,256]{1,0:T(8,128)(2,1)S(1)}, bf16[64,256]{1,0:T(8,128)(2,1)S(1)}, u32[]{:S(2)}, u32[]{:S(2)}) collective-permute-start(bf16[64,256]{1,0:T(8,128)(2,1)S(1)} %get-tuple-element.48), channel_id=1, source_target_pairs={{0,8},{8,0},{16,24},{24,16},{1,9},{9,1},{17,25},{25,17},{2,10},{10... | collective-permute-start | bytes 98312 | tf_op jit(solution)/shard_map/ppermute | solution.py:471
  12.0 5.7 %collective-permute-start.3 = (bf16[64,256]{1,0:T(8,128)(2,1)S(1)}, bf16[64,256]{1,0:T(8,128)(2,1)S(1)}, u32[]{:S(2)}, u32[]{:S(2)}) collective-permute-start(bf16[64,256]{1,0:T(8,128)(2,1)S(1)} %get-tuple-element.49), channel_id=1, source_target_pairs={{0,24},{8,16},{16,8},{24,0},{1,25},{9,17},{17,9},{25,1},{2,26},{10... | collective-permute-start | bytes 98312 | tf_op jit(solution)/shard_map/ppermute | solution.py:471
  21.5 2.0 %collective-permute-start.4 = (bf16[3,16,256]{2,1,0:T(8,128)(2,1)S(1)}, bf16[3,16,256]{2,1,0:T(8,128)(2,1)S(1)}, u32[]{:S(2)}, u32[]{:S(2)}) collective-permute-start(bf16[3,16,256]{2,1,0:T(8,128)(2,1)S(1)} %get-tuple-element.54), channel_id=1, source_target_pairs={{0,1},{1,0},{2,3},{3,2},{4,5},{5,4},{6,7},{7,6},{8,9},{9,8},{10,11... | collective-permute-start | bytes 73736 | tf_op jit(solution)/shard_map/ppermute | solution.py:475
  21.5 4.2 %collective-permute-start.5 = (bf16[3,16,256]{2,1,0:T(8,128)(2,1)S(1)}, bf16[3,16,256]{2,1,0:T(8,128)(2,1)S(1)}, u32[]{:S(2)}, u32[]{:S(2)}) collective-permute-start(bf16[3,16,256]{2,1,0:T(8,128)(2,1)S(1)} %get-tuple-element.55), channel_id=1, source_target_pairs={{0,7},{1,2},{2,1},{3,4},{4,3},{5,6},{6,5},{7,0},{8,15},{9,10},{10,... | collective-permute-start | bytes 73736 | tf_op jit(solution)/shard_map/ppermute | solution.py:476
  25.9 4.0 %collective-permute-start.6 = (bf16[64,256]{1,0:T(8,128)(2,1)S(1)}, bf16[64,256]{1,0:T(8,128)(2,1)S(1)}, u32[]{:S(2)}, u32[]{:S(2)}) collective-permute-start(bf16[64,256]{1,0:T(8,128)(2,1)S(1)} %get-tuple-element.57), channel_id=1, source_target_pairs={{0,8},{8,0},{16,24},{24,16},{1,9},{9,1},{17,25},{25,17},{2,10},{10... | collective-permute-start | bytes 98312 | tf_op jit(solution)/shard_map/ppermute | solution.py:471
  25.9 5.8 %collective-permute-start.7 = (bf16[64,256]{1,0:T(8,128)(2,1)S(1)}, bf16[64,256]{1,0:T(8,128)(2,1)S(1)}, u32[]{:S(2)}, u32[]{:S(2)}) collective-permute-start(bf16[64,256]{1,0:T(8,128)(2,1)S(1)} %get-tuple-element.58), channel_id=1, source_target_pairs={{0,24},{8,16},{16,8},{24,0},{1,25},{9,17},{17,9},{25,1},{2,26},{10... | collective-permute-start | bytes 98312 | tf_op jit(solution)/shard_map/ppermute | solution.py:471
  31.7 36.3 %copy-start = (f32[32,3072]{1,0:T(8,128)S(1)}, f32[32,3072]{1,0:T(8,128)}, u32[]{:S(2)}) copy-start(f32[32,3072]{1,0:T(8,128)} %momentum.3) | copy-start | bytes 1179652
  35.5 1.3 %collective-permute-start.8 = (bf16[3,16,256]{2,1,0:T(8,128)(2,1)S(1)}, bf16[3,16,256]{2,1,0:T(8,128)(2,1)S(1)}, u32[]{:S(2)}, u32[]{:S(2)}) collective-permute-start(bf16[3,16,256]{2,1,0:T(8,128)(2,1)S(1)} %get-tuple-element.62), channel_id=1, source_target_pairs={{0,1},{1,0},{2,3},{3,2},{4,5},{5,4},{6,7},{7,6},{8,9},{9,8},{10,11... | collective-permute-start | bytes 73736 | tf_op jit(solution)/shard_map/ppermute | solution.py:475
  37.0 11.5 %collective-permute-start.9 = (bf16[2,128,128]{2,1,0:T(8,128)(2,1)S(1)}, bf16[2,128,128]{2,1,0:T(8,128)(2,1)S(1)}, u32[]{:S(2)}, u32[]{:S(2)}) collective-permute-start(bf16[2,128,128]{2,1,0:T(8,128)(2,1)S(1)} %get-tuple-element.64), channel_id=1, source_target_pairs={{0,8},{8,0},{16,24},{24,16},{1,9},{9,1},{17,25},{25,17},{2,10},{10... | collective-permute-start | bytes 196616 | tf_op jit(solution)/shard_map/ppermute | solution.py:468
  37.2 11.2 %collective-permute-start.10 = (bf16[2,128,128]{2,1,0:T(8,128)(2,1)S(1)}, bf16[2,128,128]{2,1,0:T(8,128)(2,1)S(1)}, u32[]{:S(2)}, u32[]{:S(2)}) collective-permute-start(bf16[2,128,128]{2,1,0:T(8,128)(2,1)S(1)} %get-tuple-element.65), channel_id=1, source_target_pairs={{0,16},{8,24},{16,0},{24,8},{1,17},{9,25},{17,1},{25,9},{2,18},{10... | collective-permute-start | bytes 196616 | tf_op jit(solution)/shard_map/ppermute | solution.py:468
  40.1 10.3 %collective-permute-start.11 = (bf16[2,128,128]{2,1,0:T(8,128)(2,1)S(1)}, bf16[2,128,128]{2,1,0:T(8,128)(2,1)S(1)}, u32[]{:S(2)}, u32[]{:S(2)}) collective-permute-start(bf16[2,128,128]{2,1,0:T(8,128)(2,1)S(1)} %get-tuple-element.66), channel_id=1, source_target_pairs={{0,24},{8,16},{16,8},{24,0},{1,25},{9,17},{17,9},{25,1},{2,26},{10... | collective-permute-start | bytes 196616 | tf_op jit(solution)/shard_map/ppermute | solution.py:468
  41.4 4.2 %collective-permute-start.16 = (bf16[3,16,256]{2,1,0:T(8,128)(2,1)S(1)}, bf16[3,16,256]{2,1,0:T(8,128)(2,1)S(1)}, u32[]{:S(2)}, u32[]{:S(2)}) collective-permute-start(bf16[3,16,256]{2,1,0:T(8,128)(2,1)S(1)} %get-tuple-element.68), channel_id=1, source_target_pairs={{0,7},{1,2},{2,1},{3,4},{4,3},{5,6},{6,5},{7,0},{8,15},{9,10},{10,... | collective-permute-start | bytes 73736 | tf_op jit(solution)/shard_map/ppermute | solution.py:476
  41.5 8.8 %collective-permute-start.12 = (bf16[2,128,128]{2,1,0:T(8,128)(2,1)S(1)}, bf16[2,128,128]{2,1,0:T(8,128)(2,1)S(1)}, u32[]{:S(2)}, u32[]{:S(2)}) collective-permute-start(bf16[2,128,128]{2,1,0:T(8,128)(2,1)S(1)} %get-tuple-element.63.rest_0_), channel_id=1, source_target_pairs={{0,1},{1,0},{2,3},{3,2},{4,5},{5,4},{6,7},{7,6},{8,9},{9,8},{10,11... | collective-permute-start | bytes 196616 | tf_op jit(solution)/shard_map/ppermute | solution.py:468
  45.9 7.1 %collective-permute-start.19 = (bf16[336,128]{1,0:T(8,128)(2,1)S(1)}, bf16[336,128]{1,0:T(8,128)(2,1)S(1)}, u32[]{:S(2)}, u32[]{:S(2)}) collective-permute-start(bf16[336,128]{1,0:T(8,128)(2,1)S(1)} %shard_map.74.rest_0_), channel_id=1, source_target_pairs={{0,24},{8,16},{16,8},{24,0},{1,25},{9,17},{17,9},{25,1},{2,26},{10... | collective-permute-start | bytes 258056 | tf_op jit(solution)/shard_map/ppermute | solution.py:468
  48.4 6.3 %collective-permute-start.18 = (bf16[336,128]{1,0:T(8,128)(2,1)S(1)}, bf16[336,128]{1,0:T(8,128)(2,1)S(1)}, u32[]{:S(2)}, u32[]{:S(2)}) collective-permute-start(bf16[336,128]{1,0:T(8,128)(2,1)S(1)} %shard_map.74.rest_0_), channel_id=1, source_target_pairs={{0,16},{8,24},{16,0},{24,8},{1,17},{9,25},{17,1},{25,9},{2,18},{10... | collective-permute-start | bytes 258056 | tf_op jit(solution)/shard_map/ppermute | solution.py:468
  48.5 6.3 %collective-permute-start.17 = (bf16[336,128]{1,0:T(8,128)(2,1)S(1)}, bf16[336,128]{1,0:T(8,128)(2,1)S(1)}, u32[]{:S(2)}, u32[]{:S(2)}) collective-permute-start(bf16[336,128]{1,0:T(8,128)(2,1)S(1)} %shard_map.74.rest_0_), channel_id=1, source_target_pairs={{0,8},{8,0},{16,24},{24,16},{1,9},{9,1},{17,25},{25,17},{2,10},{10... | collective-permute-start | bytes 258056 | tf_op jit(solution)/shard_map/ppermute | solution.py:468
  50.4 4.9 %collective-permute-start.13 = (bf16[2,128,128]{2,1,0:T(8,128)(2,1)S(1)}, bf16[2,128,128]{2,1,0:T(8,128)(2,1)S(1)}, u32[]{:S(2)}, u32[]{:S(2)}) collective-permute-start(bf16[2,128,128]{2,1,0:T(8,128)(2,1)S(1)} %collective-permute-done.9.rest_1_), channel_id=1, source_target_pairs={{0,1},{1,0},{2,3},{3,2},{4,5},{5,4},{6,7},{7,6},{8,9},{9,8},{10,11... | collective-permute-start | bytes 196616 | tf_op jit(solution)/shard_map/ppermute | solution.py:468
  50.4 5.0 %collective-permute-start.14 = (bf16[2,128,128]{2,1,0:T(8,128)(2,1)S(1)}, bf16[2,128,128]{2,1,0:T(8,128)(2,1)S(1)}, u32[]{:S(2)}, u32[]{:S(2)}) collective-permute-start(bf16[2,128,128]{2,1,0:T(8,128)(2,1)S(1)} %collective-permute-done.10.rest_2_), channel_id=1, source_target_pairs={{0,1},{1,0},{2,3},{3,2},{4,5},{5,4},{6,7},{7,6},{8,9},{9,8},{10,11... | collective-permute-start | bytes 196616 | tf_op jit(solution)/shard_map/ppermute | solution.py:468
  53.0 3.9 %collective-permute-start.20 = (bf16[336,128]{1,0:T(8,128)(2,1)S(1)}, bf16[336,128]{1,0:T(8,128)(2,1)S(1)}, u32[]{:S(2)}, u32[]{:S(2)}) collective-permute-start(bf16[336,128]{1,0:T(8,128)(2,1)S(1)} %shard_map.74.rest_0_), channel_id=1, source_target_pairs={{0,1},{1,0},{2,3},{3,2},{4,5},{5,4},{6,7},{7,6},{8,9},{9,8},{10,11... | collective-permute-start | bytes 258056 | tf_op jit(solution)/shard_map/ppermute | solution.py:468
  54.8 2.2 %collective-permute-start.23 = (bf16[336,128]{1,0:T(8,128)(2,1)S(1)}, bf16[336,128]{1,0:T(8,128)(2,1)S(1)}, u32[]{:S(2)}, u32[]{:S(2)}) collective-permute-start(bf16[336,128]{1,0:T(8,128)(2,1)S(1)} %collective-permute-done.19.rest_3_), channel_id=1, source_target_pairs={{0,1},{1,0},{2,3},{3,2},{4,5},{5,4},{6,7},{7,6},{8,9},{9,8},{10,11... | collective-permute-start | bytes 258056 | tf_op jit(solution)/shard_map/ppermute | solution.py:468
  54.8 2.2 %collective-permute-start.22 = (bf16[336,128]{1,0:T(8,128)(2,1)S(1)}, bf16[336,128]{1,0:T(8,128)(2,1)S(1)}, u32[]{:S(2)}, u32[]{:S(2)}) collective-permute-start(bf16[336,128]{1,0:T(8,128)(2,1)S(1)} %collective-permute-done.18.rest_2_), channel_id=1, source_target_pairs={{0,1},{1,0},{2,3},{3,2},{4,5},{5,4},{6,7},{7,6},{8,9},{9,8},{10,11... | collective-permute-start | bytes 258056 | tf_op jit(solution)/shard_map/ppermute | solution.py:468
  55.3 1.7 %collective-permute-start.21 = (bf16[336,128]{1,0:T(8,128)(2,1)S(1)}, bf16[336,128]{1,0:T(8,128)(2,1)S(1)}, u32[]{:S(2)}, u32[]{:S(2)}) collective-permute-start(bf16[336,128]{1,0:T(8,128)(2,1)S(1)} %collective-permute-done.17.rest_1_), channel_id=1, source_target_pairs={{0,1},{1,0},{2,3},{3,2},{4,5},{5,4},{6,7},{7,6},{8,9},{9,8},{10,11... | collective-permute-start | bytes 258056 | tf_op jit(solution)/shard_map/ppermute | solution.py:468
  55.4 1.3 %collective-permute-start.15 = (bf16[2,128,128]{2,1,0:T(8,128)(2,1)S(1)}, bf16[2,128,128]{2,1,0:T(8,128)(2,1)S(1)}, u32[]{:S(2)}, u32[]{:S(2)}) collective-permute-start(bf16[2,128,128]{2,1,0:T(8,128)(2,1)S(1)} %collective-permute-done.11.rest_3_), channel_id=1, source_target_pairs={{0,1},{1,0},{2,3},{3,2},{4,5},{5,4},{6,7},{7,6},{8,9},{9,8},{10,11... | collective-permute-start | bytes 196616 | tf_op jit(solution)/shard_map/ppermute | solution.py:468
  58.9 6.7 %collective-permute-start.24 = (bf16[32,1536]{1,0:T(8,128)(2,1)S(1)}, bf16[32,1536]{1,0:T(8,128)(2,1)S(1)}, u32[]{:S(2)}, u32[]{:S(2)}) collective-permute-start(bf16[32,1536]{1,0:T(8,128)(2,1)S(1)} %get-tuple-element.70), channel_id=1, source_target_pairs={{0,2},{2,0},{4,6},{6,4},{1,3},{3,1},{5,7},{7,5},{8,10},{10,8},{12,... | collective-permute-start | bytes 294920 | tf_op jit(solution)/shard_map/ppermute | solution.py:468
  60.3 7.1 %collective-permute-start.25 = (bf16[32,1536]{1,0:T(8,128)(2,1)S(1)}, bf16[32,1536]{1,0:T(8,128)(2,1)S(1)}, u32[]{:S(2)}, u32[]{:S(2)}) collective-permute-start(bf16[32,1536]{1,0:T(8,128)(2,1)S(1)} %get-tuple-element.71), channel_id=1, source_target_pairs={{0,4},{2,6},{4,0},{6,2},{1,5},{3,7},{5,1},{7,3},{8,12},{10,14},{12... | collective-permute-start | bytes 294920 | tf_op jit(solution)/shard_map/ppermute | solution.py:468
  61.4 6.6 %collective-permute-start.26 = (bf16[32,1536]{1,0:T(8,128)(2,1)S(1)}, bf16[32,1536]{1,0:T(8,128)(2,1)S(1)}, u32[]{:S(2)}, u32[]{:S(2)}) collective-permute-start(bf16[32,1536]{1,0:T(8,128)(2,1)S(1)} %get-tuple-element.72), channel_id=1, source_target_pairs={{0,6},{2,4},{4,2},{6,0},{1,7},{3,5},{5,3},{7,1},{8,14},{10,12},{12... | collective-permute-start | bytes 294920 | tf_op jit(solution)/shard_map/ppermute | solution.py:468
  63.1 6.3 %collective-permute-start.27 = (bf16[32,1536]{1,0:T(8,128)(2,1)S(1)}, bf16[32,1536]{1,0:T(8,128)(2,1)S(1)}, u32[]{:S(2)}, u32[]{:S(2)}) collective-permute-start(bf16[32,1536]{1,0:T(8,128)(2,1)S(1)} %get-tuple-element.78), channel_id=1, source_target_pairs={{0,2},{2,0},{4,6},{6,4},{1,3},{3,1},{5,7},{7,5},{8,10},{10,8},{12,... | collective-permute-start | bytes 294920 | tf_op jit(solution)/shard_map/ppermute | solution.py:468
  64.5 6.9 %collective-permute-start.28 = (bf16[32,1536]{1,0:T(8,128)(2,1)S(1)}, bf16[32,1536]{1,0:T(8,128)(2,1)S(1)}, u32[]{:S(2)}, u32[]{:S(2)}) collective-permute-start(bf16[32,1536]{1,0:T(8,128)(2,1)S(1)} %get-tuple-element.79), channel_id=1, source_target_pairs={{0,4},{2,6},{4,0},{6,2},{1,5},{3,7},{5,1},{7,3},{8,12},{10,14},{12... | collective-permute-start | bytes 294920 | tf_op jit(solution)/shard_map/ppermute | solution.py:468
  65.6 5.8 %collective-permute-start.29 = (bf16[32,1536]{1,0:T(8,128)(2,1)S(1)}, bf16[32,1536]{1,0:T(8,128)(2,1)S(1)}, u32[]{:S(2)}, u32[]{:S(2)}) collective-permute-start(bf16[32,1536]{1,0:T(8,128)(2,1)S(1)} %get-tuple-element.80), channel_id=1, source_target_pairs={{0,6},{2,4},{4,2},{6,0},{1,7},{3,5},{5,3},{7,1},{8,14},{10,12},{12... | collective-permute-start | bytes 294920 | tf_op jit(solution)/shard_map/ppermute | solution.py:468

commit v4 on v3

--- a/solution.py
+++ b/solution.py
@@ -85,17 +85,20 @@
 
 def reconstruct(z, place, coding, dic, pixels, tall_sum, own, ready=None):
     tall_sum[z.sites :, :] = jnp.zeros((z.tall * z.cols - z.sites, z.band), F32)
-    for i in range(SPAN):
+    for pair in range(0, SPAN, 2):
         if ready is not None:
-            ready(i)
+            ready(pair)
+            ready(pair + 1)
         placed = jnp.dot(
-            coding, dic[:, i * z.band : (i + 1) * z.band], preferred_element_type=F32
+            coding, dic[:, pair * z.band : (pair + 2) * z.band], preferred_element_type=F32
         )
-        start = i * z.cols
-        if i == 0:
-            tall_sum[0 : z.sites, :] = placed
-        else:
-            tall_sum[start : start + z.sites, :] += placed
+        for i in (pair, pair + 1):
+            part = placed[:, (i - pair) * z.band : (i - pair + 1) * z.band]
+            start = i * z.cols
+            if i == 0:
+                tall_sum[0 : z.sites, :] = part
+            else:
+                tall_sum[start : start + z.sites, :] += part
     own[...] = jnp.zeros((z.tall, z.wide_pad, z.lanes), F32)
     own[0 : z.rows, 0 : z.cols, 0 : z.cell] = pixels[...].reshape(z.rows, z.cols, z.cell)
     for j in range(SPAN):
@@ -136,8 +139,25 @@
     return (a == b).astype(F32).astype(BF16)
 
 
-def cells_of(z, picture, pixels, spread):
+def cells_of(z, picture, pixels, spread, picks, ready):
     channels, height, width = picture.shape
+
+    def iota(shape, dim):
+        return lax.broadcasted_iota(jnp.int32, shape, dim)
+
+    shape = (channels * height, z.cell)
+    line, entry = iota(shape, 0), iota(shape, 1)
+    channel, image_row = lax.div(line, height), lax.rem(line, height)
+    away = (
+        (channel * STRIDE + lax.rem(image_row, STRIDE)) * STRIDE
+        + lax.div(image_row, STRIDE) * z.cell
+        - lax.div(entry, STRIDE) * STRIDE
+    )
+    for i in range(z.rows):
+        picks[i] = is_equal(away, i * z.cell)
+    shape = (width, z.cell)
+    mine = (lax.rem(iota(shape, 0), STRIDE) == lax.rem(iota(shape, 1), STRIDE)).astype(F32)
+    ready()
     turned = picture[...].reshape(channels * height, width).T
     high = turned.astype(BF16)
     rest = turned - high.astype(F32)
@@ -145,23 +165,9 @@
     spread[0:width, :] = high
     spread[width : 2 * width, :] = middle
     spread[2 * width :, :] = (rest - middle.astype(F32)).astype(BF16)
-
-    def iota(shape, dim):
-        return lax.broadcasted_iota(jnp.int32, shape, dim)
-
-    shape = (channels * height, z.cell)
-    line, entry = iota(shape, 0), iota(shape, 1)
-    channel, image_row = lax.div(line, height), lax.rem(line, height)
-    away = (
-        (channel * STRIDE + lax.rem(image_row, STRIDE)) * STRIDE
-        + lax.div(image_row, STRIDE) * z.cell
-        - lax.div(entry, STRIDE) * STRIDE
-    )
-    shape = (width, z.cell)
-    mine = (lax.rem(iota(shape, 0), STRIDE) == lax.rem(iota(shape, 1), STRIDE)).astype(F32)
     for i in range(z.rows):
         moved = jnp.dot(
-            spread[...], is_equal(away, i * z.cell), preferred_element_type=F32
+            spread[...], picks[i], preferred_element_type=F32
         )
         whole = (moved[0:width] + moved[width : 2 * width]) + moved[2 * width :]
         whole = (whole * mine).reshape(z.cols, STRIDE, z.cell)
@@ -171,7 +177,7 @@
 def first_kernel(
     z, grid, membrane, picture, source, own, *rest
 ):
-    (*sends, pixels, dic, potential, atoms, tall_sum, spread, drawing, sems) = rest
+    (*sends, pixels, dic, potential, atoms, tall_sum, spread, picks, drawing, sems) = rest
     place = Place(*grid)
     early = [
         pltpu.make_async_copy(picture, drawing, sems.at[SPAN]),
@@ -187,14 +193,23 @@
     ]
     for copy in early + copies:
         copy.start()
-    early[0].wait()
-    cells_of(z, drawing, pixels, spread)
+    cells_of(z, drawing, pixels, spread, picks, early[0].wait)
     early[1].wait()
     coding = shrink(potential[...]).astype(BF16)
     reconstruct(z, place, coding, dic, pixels, tall_sum, own, lambda i: copies[i].wait())
     send_sides(z, place, own, sends)
     owned = atoms.shape[0]
     atoms[...] = dic[pl.ds(pl.multiple_of(place.owner * owned, owned), owned), :]
+
+
+def flip_kernel(z, dic, turned):
+    size = 256
+    shape = (size, size)
+    same = is_equal(lax.broadcasted_iota(jnp.int32, shape, 0), lax.broadcasted_iota(jnp.int32, shape, 1))
+    for i in range(0, z.patch, size):
+        turned[i : i + size, :] = lax.dot_general(
+            same, dic[:, i : i + size], (((1,), (1,)), ((), ())), preferred_element_type=F32
+        ).astype(BF16)
 
 
 def side_kernel(z, grid, own, from_even, from_odd, joined, even, odd, rim):
@@ -238,7 +253,7 @@
 
 
 def sweep_kernel(
-    z, grid, last, potential, joined, from_even, from_odd, pixels, dic, *rest
+    z, grid, last, potential, joined, from_even, from_odd, pixels, dic, turned, *rest
 ):
     if last:
         new_potential, own, *sends, codes, tall_sum, whole, wide_part, rim = rest
@@ -252,8 +267,8 @@
     for i in range(SPAN):
         term = lax.dot_general(
             wide_part[i * z.cols : i * z.cols + z.sites, :],
-            dic[:, i * z.band : (i + 1) * z.band],
-            (((1,), (1,)), ((), ())),
+            turned[i * z.band : (i + 1) * z.band, :],
+            (((1,), (0,)), ((), ())),
             preferred_element_type=F32,
         )
         drive = term if drive is None else drive + term
@@ -499,6 +514,7 @@
         [
             tall_v,
             pltpu.VMEM((3 * picture.shape[2], z.cell), BF16),
+            pltpu.VMEM((z.rows, picture.shape[0] * picture.shape[1], z.cell), BF16),
             pltpu.VMEM(picture.shape, F32),
             pltpu.SemaphoreType.DMA((SPAN + 2,)),
         ],
@@ -506,11 +522,16 @@
     )
     for repeat in range(SWEEPS):
         last = repeat == SWEEPS - 1
+        sides = sideways(sides)
+        if repeat == 0:
+            (turned,) = call(
+                functools.partial(flip_kernel, z),
+                [pltpu.VMEM((z.patch, atom_count), BF16)],
+                (dic,),
+                [],
+            )
         joined, *ends = call(
-            functools.partial(side_kernel, z, grid),
-            [own_v, end_v, end_v],
-            (own, *sideways(sides)),
-            [rim_v],
+            functools.partial(side_kernel, z, grid), [own_v, end_v, end_v], (own, *sides), [rim_v]
         )
         ends = swapped("row", rows_n, ends)
         final = [
@@ -521,7 +542,7 @@
         potential, own, *rest = call(
             functools.partial(sweep_kernel, z, grid, last),
             final if last else [site_v] + outs,
-            (potential, joined, *ends, pixels, dic),
+            (potential, joined, *ends, pixels, dic, turned),
             [tall_v, own_v, wide_v, rim_v],
         )
         sides = rest[:2]

time: 72.8 us -> 70.7 us (0.971)
  waiting for transfers between devices: 24 us -> 22.1 us
    ppermute x4, waiting for transfers between devices: 6.49 us -> 4.62 us  [swapped(): lax.ppermute(b, axis, route)]
    pallas_call x12 -> x13, Pallas kernels: 16 us -> 15.9 us  [call(): pl.pallas_call(kernel, out_shape=outs, in_specs=specs, out_specs=[leave]...]
  transfers between devices with their start and end apart: 30 -> 30, of which waited for: 13 -> 13; matrix products, arithmetic and copies ran while one was open for 1% -> 1% of each run, Pallas kernels for 2% -> 4%
where the time goes in v4:
time: 70.7 us; the launch traced here: 70.6 us
  starting transfers between devices  30.9 us (44%)
  waiting for transfers between devices  22.1 us (31%)
  Pallas kernels  15.9 us (22%)
  between operations  0.97 us (1%)
  local copies, waits for them, and re-layouts  0.8 us (1%)
    ppermute x20, starting transfers between devices, met(): lax.ppermute(block, axis, [(i, offset(i, step, n)) for i in range(n)])  17.7 us
    pallas_call x13, Pallas kernels, call(): pl.pallas_call(kernel, out_shape=outs, in_specs=specs, out_specs=[leave]...  15.9 us
    ppermute x20, waiting for transfers between devices, met(): lax.ppermute(block, axis, [(i, offset(i, step, n)) for i in range(n)])  8.65 us
    ppermute x3, waiting for transfers between devices, sideways(): far_rim = lax.ppermute(blocks[1], ('yx', 'core'), odd)  7.63 us
    ppermute x4, starting transfers between devices, swapped(): lax.ppermute(b, axis, route)  6.88 us
    ppermute x3, starting transfers between devices, sideways(): far_rim = lax.ppermute(blocks[1], ('yx', 'core'), odd)  5.62 us
    ppermute x4, waiting for transfers between devices, swapped(): lax.ppermute(b, axis, route)  4.62 us
  transfers between devices with their start and end apart: 30, of which 13 were waited for; matrix products, arithmetic and copies ran while one was open for 1% of the time, Pallas kernels for 4%

profile of v4, /device:TPU:0, one launch (start us, length us, event | category | flops | bytes accessed | tf_op | source)
XLA Modules:
  0.0 70.6 jit_solution(16890852195882319730)
XLA Ops:
  0.6 4.1 %shard_map.67 = (f32[11,24,256]{2,1,0:T(8,128)S(1)}, bf16[3,16,256]{2,1,0:T(8,128)(2,1)S(1)}, bf16[3,16,256]{2,1,0:T(8,128)(2,1)S(1)}, f32[128,192]{1,0:T(8,128)...) custom-call(f32[128,1024]{1,0:T(8,128)} %bitcast.3, ...), custom_call_target="tpu_custom_call" | custom-call | tf_op jit(solution)/shard_map/pallas_call | solution.py:462
  5.3 3.5 %collective-permute-start.1 = (bf16[3,16,256]{2,1,0:T(8,128)(2,1)S(1)}, bf16[3,16,256]{2,1,0:T(8,128)(2,1)S(1)}, u32[]{:S(2)}, u32[]{:S(2)}) collective-permute-start(bf16[3,16,256]{2,1,0:T(8,128)(2,1)S(1)} %get-tuple-element.46), channel_id=1, source_target_pairs={{0,7},{1,2},{2,1},{3,4},{4,3},{5,6},{6,5},{7,0},{8,15},{9,10},{10,... | collective-permute-start | bytes 73736 | tf_op jit(solution)/shard_map/ppermute | solution.py:491
  8.8 1.5 %collective-permute-done.1.from_odd = bf16[3,16,256]{2,1,0:T(8,128)(2,1)S(1)} collective-permute-done((bf16[3,16,256]{2,1,0:T(8,128)(2,1)S(1)}, bf16[3,16,256]{2,1,0:T(8,128)(2,1)S(1)}, u32[]{:S(2)}, u32[]{:S(2)}) %collective-permute-start.1) | collective-permute-done | bytes 24608 | tf_op jit(solution)/shard_map/ppermute | solution.py:491
  10.4 1.8 %collective-permute-start.2 = (bf16[64,256]{1,0:T(8,128)(2,1)S(1)}, bf16[64,256]{1,0:T(8,128)(2,1)S(1)}, u32[]{:S(2)}, u32[]{:S(2)}) collective-permute-start(bf16[64,256]{1,0:T(8,128)(2,1)S(1)} %get-tuple-element.48), channel_id=1, source_target_pairs={{0,8},{8,0},{16,24},{24,16},{1,9},{9,1},{17,25},{25,17},{2,10},{10... | collective-permute-start | bytes 98312 | tf_op jit(solution)/shard_map/ppermute | solution.py:486
  12.2 2.5 %collective-permute-start.3 = (bf16[64,256]{1,0:T(8,128)(2,1)S(1)}, bf16[64,256]{1,0:T(8,128)(2,1)S(1)}, u32[]{:S(2)}, u32[]{:S(2)}) collective-permute-start(bf16[64,256]{1,0:T(8,128)(2,1)S(1)} %get-tuple-element.49), channel_id=1, source_target_pairs={{0,24},{8,16},{16,8},{24,0},{1,25},{9,17},{17,9},{25,1},{2,26},{10... | collective-permute-start | bytes 98312 | tf_op jit(solution)/shard_map/ppermute | solution.py:486
  14.7 1.8 %shard_map.69.turned = bf16[3072,1024]{1,0:T(8,128)(2,1)S(1)} custom-call(bf16[1024,3072]{1,0:T(8,128)(2,1)S(1)} %get-tuple-element.51.dic), custom_call_target="tpu_custom_call" | custom-call | tf_op jit(solution)/shard_map/pallas_call | solution.py:462
  16.5 1.4 %collective-permute-done.3.from_odd = bf16[64,256]{1,0:T(8,128)(2,1)S(1)} collective-permute-done((bf16[64,256]{1,0:T(8,128)(2,1)S(1)}, bf16[64,256]{1,0:T(8,128)(2,1)S(1)}, u32[]{:S(2)}, u32[]{:S(2)}) %collective-permute-start.3) | collective-permute-done | bytes 32800 | tf_op jit(solution)/shard_map/ppermute | solution.py:486
  17.9 2.6 %shard_map.70 = (f32[128,1024]{1,0:T(8,128)S(1)}, f32[11,24,256]{2,1,0:T(8,128)S(1)}, bf16[3,16,256]{2,1,0:T(8,128)(2,1)S(1)}, bf16[3,16,256]{2,1,0:T(8,128)(2,1)S(1)}) custom-call(f32[128,1024]{1,0:T(8,128)S(1)} %get-tuple-element.43.potential, f32[11,24,256]{2,1,0:T(8,128)S(1)} %get-tuple-element.47.joined, ...), custom_call_target="tpu_custom_call" | custom-call | tf_op jit(solution)/shard_map/pallas_call | solution.py:462
  20.6 2.0 %collective-permute-start.5 = (bf16[3,16,256]{2,1,0:T(8,128)(2,1)S(1)}, bf16[3,16,256]{2,1,0:T(8,128)(2,1)S(1)}, u32[]{:S(2)}, u32[]{:S(2)}) collective-permute-start(bf16[3,16,256]{2,1,0:T(8,128)(2,1)S(1)} %get-tuple-element.55), channel_id=1, source_target_pairs={{0,7},{1,2},{2,1},{3,4},{4,3},{5,6},{6,5},{7,0},{8,15},{9,10},{10,... | collective-permute-start | bytes 73736 | tf_op jit(solution)/shard_map/ppermute | solution.py:491
  22.6 2.2 %collective-permute-done.5.from_odd = bf16[3,16,256]{2,1,0:T(8,128)(2,1)S(1)} collective-permute-done((bf16[3,16,256]{2,1,0:T(8,128)(2,1)S(1)}, bf16[3,16,256]{2,1,0:T(8,128)(2,1)S(1)}, u32[]{:S(2)}, u32[]{:S(2)}) %collective-permute-start.5) | collective-permute-done | bytes 24608 | tf_op jit(solution)/shard_map/ppermute | solution.py:491
  25.0 2.5 %collective-permute-start.7 = (bf16[64,256]{1,0:T(8,128)(2,1)S(1)}, bf16[64,256]{1,0:T(8,128)(2,1)S(1)}, u32[]{:S(2)}, u32[]{:S(2)}) collective-permute-start(bf16[64,256]{1,0:T(8,128)(2,1)S(1)} %get-tuple-element.58), channel_id=1, source_target_pairs={{0,24},{8,16},{16,8},{24,0},{1,25},{9,17},{17,9},{25,1},{2,26},{10... | collective-permute-start | bytes 98312 | tf_op jit(solution)/shard_map/ppermute | solution.py:486
  27.6 1.4 %collective-permute-done.6.from_even = bf16[64,256]{1,0:T(8,128)(2,1)S(1)} collective-permute-done((bf16[64,256]{1,0:T(8,128)(2,1)S(1)}, bf16[64,256]{1,0:T(8,128)(2,1)S(1)}, u32[]{:S(2)}, u32[]{:S(2)}) %collective-permute-start.6) | collective-permute-done | bytes 32800 | tf_op jit(solution)/shard_map/ppermute | solution.py:486
  28.9 1.9 %collective-permute-done.7.from_odd = bf16[64,256]{1,0:T(8,128)(2,1)S(1)} collective-permute-done((bf16[64,256]{1,0:T(8,128)(2,1)S(1)}, bf16[64,256]{1,0:T(8,128)(2,1)S(1)}, u32[]{:S(2)}, u32[]{:S(2)}) %collective-permute-start.7) | collective-permute-done | bytes 32800 | tf_op jit(solution)/shard_map/ppermute | solution.py:486
  30.8 2.6 %shard_map.72 = (f32[128,1024]{1,0:T(8,128)S(1)}, f32[11,24,256]{2,1,0:T(8,128)S(1)}, bf16[3,16,256]{2,1,0:T(8,128)(2,1)S(1)}, bf16[3,16,256]{2,1,0:T(8,128)(2,1)S(1)}, bf16[128,1024]{1,0:T(8,128)(2,1)S(1)}) custom-call(f32[128,1024]{1,0:T(8,128)S(1)} %get-tuple-element.52.potential, f32[11,24,256]{2,1,0:T(8,128)S(1)} %get-tuple-element.56.joined, ...), custom_call_target="tpu_custom_call" | custom-call | tf_op jit(solution)/shard_map/pallas_call | solution.py:462
  33.5 1.2 %collective-permute-done.8._.from_even = bf16[3,16,256]{2,1,0:T(8,128)(2,1)S(1)} collective-permute-done((bf16[3,16,256]{2,1,0:T(8,128)(2,1)S(1)}, bf16[3,16,256]{2,1,0:T(8,128)(2,1)S(1)}, u32[]{:S(2)}, u32[]{:S(2)}) %collective-permute-start.8) | collective-permute-done | bytes 24608 | tf_op jit(solution)/shard_map/ppermute | solution.py:490
  35.2 2.9 %collective-permute-start.10 = (bf16[2,128,128]{2,1,0:T(8,128)(2,1)S(1)}, bf16[2,128,128]{2,1,0:T(8,128)(2,1)S(1)}, u32[]{:S(2)}, u32[]{:S(2)}) collective-permute-start(bf16[2,128,128]{2,1,0:T(8,128)(2,1)S(1)} %get-tuple-element.65), channel_id=1, source_target_pairs={{0,16},{8,24},{16,0},{24,8},{1,17},{9,25},{17,1},{25,9},{2,18},{10... | collective-permute-start | bytes 196616 | tf_op jit(solution)/shard_map/ppermute | solution.py:483
  38.1 1.4 %collective-permute-start.11 = (bf16[2,128,128]{2,1,0:T(8,128)(2,1)S(1)}, bf16[2,128,128]{2,1,0:T(8,128)(2,1)S(1)}, u32[]{:S(2)}, u32[]{:S(2)}) collective-permute-start(bf16[2,128,128]{2,1,0:T(8,128)(2,1)S(1)} %get-tuple-element.66), channel_id=1, source_target_pairs={{0,24},{8,16},{16,8},{24,0},{1,25},{9,17},{17,9},{25,1},{2,26},{10... | collective-permute-start | bytes 196616 | tf_op jit(solution)/shard_map/ppermute | solution.py:483
  39.7 3.9 %collective-permute-done.16.from_odd = bf16[3,16,256]{2,1,0:T(8,128)(2,1)S(1)} collective-permute-done((bf16[3,16,256]{2,1,0:T(8,128)(2,1)S(1)}, bf16[3,16,256]{2,1,0:T(8,128)(2,1)S(1)}, u32[]{:S(2)}, u32[]{:S(2)}) %collective-permute-start.16) | collective-permute-done | bytes 24608 | tf_op jit(solution)/shard_map/ppermute | solution.py:491
  43.9 2.5 %collective-permute-start.19 = (bf16[336,128]{1,0:T(8,128)(2,1)S(1)}, bf16[336,128]{1,0:T(8,128)(2,1)S(1)}, u32[]{:S(2)}, u32[]{:S(2)}) collective-permute-start(bf16[336,128]{1,0:T(8,128)(2,1)S(1)} %shard_map.75.rest_0_), channel_id=1, source_target_pairs={{0,24},{8,16},{16,8},{24,0},{1,25},{9,17},{17,9},{25,1},{2,26},{10... | collective-permute-start | bytes 258056 | tf_op jit(solution)/shard_map/ppermute | solution.py:483
  46.4 1.9 %collective-permute-start.17 = (bf16[336,128]{1,0:T(8,128)(2,1)S(1)}, bf16[336,128]{1,0:T(8,128)(2,1)S(1)}, u32[]{:S(2)}, u32[]{:S(2)}) collective-permute-start(bf16[336,128]{1,0:T(8,128)(2,1)S(1)} %shard_map.75.rest_0_), channel_id=1, source_target_pairs={{0,8},{8,0},{16,24},{24,16},{1,9},{9,1},{17,25},{25,17},{2,10},{10... | collective-permute-start | bytes 258056 | tf_op jit(solution)/shard_map/ppermute | solution.py:483
  48.9 2.1 %collective-permute-done.19.rest_3_ = bf16[336,128]{1,0:T(8,128)(2,1)S(1)} collective-permute-done((bf16[336,128]{1,0:T(8,128)(2,1)S(1)}, bf16[336,128]{1,0:T(8,128)(2,1)S(1)}, u32[]{:S(2)}, u32[]{:S(2)}) %collective-permute-start.19) | collective-permute-done | bytes 86048 | tf_op jit(solution)/shard_map/ppermute | solution.py:483
  51.0 1.8 %collective-permute-done.18.rest_2_ = bf16[336,128]{1,0:T(8,128)(2,1)S(1)} collective-permute-done((bf16[336,128]{1,0:T(8,128)(2,1)S(1)}, bf16[336,128]{1,0:T(8,128)(2,1)S(1)}, u32[]{:S(2)}, u32[]{:S(2)}) %collective-permute-start.18) | collective-permute-done | bytes 86048 | tf_op jit(solution)/shard_map/ppermute | solution.py:483
  55.0 1.9 %shard_map.76 = (bf16[32,1536]{1,0:T(8,128)(2,1)S(1)}, bf16[32,1536]{1,0:T(8,128)(2,1)S(1)}, bf16[32,1536]{1,0:T(8,128)(2,1)S(1)}, bf16[32,1536]{1,0:T(8,128)(2,1)S(1)}, bf16[1408,768]{1,0:T(8,128)(2,1)S(1)}) custom-call(bf16[128,1024]{1,0:T(8,128)(2,1)S(1)} %shard_map.74.across, bf16[336,128]{1,0:T(8,128)(2,1)S(1)} %shard_map.75.rest_0_, ...), custom_call_target="tpu_custom_call" | custom-call | tf_op jit(solution)/shard_map/pallas_call | solution.py:462
  56.9 1.4 %collective-permute-start.24 = (bf16[32,1536]{1,0:T(8,128)(2,1)S(1)}, bf16[32,1536]{1,0:T(8,128)(2,1)S(1)}, u32[]{:S(2)}, u32[]{:S(2)}) collective-permute-start(bf16[32,1536]{1,0:T(8,128)(2,1)S(1)} %get-tuple-element.70), channel_id=1, source_target_pairs={{0,2},{2,0},{4,6},{6,4},{1,3},{3,1},{5,7},{7,5},{8,10},{10,8},{12,... | collective-permute-start | bytes 294920 | tf_op jit(solution)/shard_map/ppermute | solution.py:483
  58.3 1.1 %collective-permute-start.25 = (bf16[32,1536]{1,0:T(8,128)(2,1)S(1)}, bf16[32,1536]{1,0:T(8,128)(2,1)S(1)}, u32[]{:S(2)}, u32[]{:S(2)}) collective-permute-start(bf16[32,1536]{1,0:T(8,128)(2,1)S(1)} %get-tuple-element.71), channel_id=1, source_target_pairs={{0,4},{2,6},{4,0},{6,2},{1,5},{3,7},{5,1},{7,3},{8,12},{10,14},{12... | collective-permute-start | bytes 294920 | tf_op jit(solution)/shard_map/ppermute | solution.py:483
  59.4 1.0 %collective-permute-start.26 = (bf16[32,1536]{1,0:T(8,128)(2,1)S(1)}, bf16[32,1536]{1,0:T(8,128)(2,1)S(1)}, u32[]{:S(2)}, u32[]{:S(2)}) collective-permute-start(bf16[32,1536]{1,0:T(8,128)(2,1)S(1)} %get-tuple-element.72), channel_id=1, source_target_pairs={{0,6},{2,4},{4,2},{6,0},{1,7},{3,5},{5,3},{7,1},{8,14},{10,12},{12... | collective-permute-start | bytes 294920 | tf_op jit(solution)/shard_map/ppermute | solution.py:483
  61.1 1.4 %collective-permute-start.27 = (bf16[32,1536]{1,0:T(8,128)(2,1)S(1)}, bf16[32,1536]{1,0:T(8,128)(2,1)S(1)}, u32[]{:S(2)}, u32[]{:S(2)}) collective-permute-start(bf16[32,1536]{1,0:T(8,128)(2,1)S(1)} %get-tuple-element.78), channel_id=1, source_target_pairs={{0,2},{2,0},{4,6},{6,4},{1,3},{3,1},{5,7},{7,5},{8,10},{10,8},{12,... | collective-permute-start | bytes 294920 | tf_op jit(solution)/shard_map/ppermute | solution.py:483
  62.5 1.1 %collective-permute-start.28 = (bf16[32,1536]{1,0:T(8,128)(2,1)S(1)}, bf16[32,1536]{1,0:T(8,128)(2,1)S(1)}, u32[]{:S(2)}, u32[]{:S(2)}) collective-permute-start(bf16[32,1536]{1,0:T(8,128)(2,1)S(1)} %get-tuple-element.79), channel_id=1, source_target_pairs={{0,4},{2,6},{4,0},{6,2},{1,5},{3,7},{5,1},{7,3},{8,12},{10,14},{12... | collective-permute-start | bytes 294920 | tf_op jit(solution)/shard_map/ppermute | solution.py:483
  63.6 1.0 %collective-permute-start.29 = (bf16[32,1536]{1,0:T(8,128)(2,1)S(1)}, bf16[32,1536]{1,0:T(8,128)(2,1)S(1)}, u32[]{:S(2)}, u32[]{:S(2)}) collective-permute-start(bf16[32,1536]{1,0:T(8,128)(2,1)S(1)} %get-tuple-element.80), channel_id=1, source_target_pairs={{0,6},{2,4},{4,2},{6,0},{1,7},{3,5},{5,3},{7,1},{8,14},{10,12},{12... | collective-permute-start | bytes 294920 | tf_op jit(solution)/shard_map/ppermute | solution.py:483
  66.2 1.2 %collective-permute-done.27.rest_1_ = bf16[32,1536]{1,0:T(8,128)(2,1)S(1)} collective-permute-done((bf16[32,1536]{1,0:T(8,128)(2,1)S(1)}, bf16[32,1536]{1,0:T(8,128)(2,1)S(1)}, u32[]{:S(2)}, u32[]{:S(2)}) %collective-permute-start.27) | collective-permute-done | bytes 98336 | tf_op jit(solution)/shard_map/ppermute | solution.py:483
  67.3 2.1 %collective-permute-done.28.rest_2_ = bf16[32,1536]{1,0:T(8,128)(2,1)S(1)} collective-permute-done((bf16[32,1536]{1,0:T(8,128)(2,1)S(1)}, bf16[32,1536]{1,0:T(8,128)(2,1)S(1)}, u32[]{:S(2)}, u32[]{:S(2)}) %collective-permute-start.28) | collective-permute-done | bytes 98336 | tf_op jit(solution)/shard_map/ppermute | solution.py:483
  69.4 1.0 %shard_map.79 = (f32[32,3072]{1,0:T(8,128)}, f32[32,3072]{1,0:T(8,128)}) custom-call(f32[32,1536]{1,0:T(8,128)S(1)} %get-tuple-element.73.first_updated, f32[32,1536]{1,0:T(8,128)S(1)} %get-tuple-element.74.first_weights, f32[32,128]{1,0:T(8,128)S(1)} %get-tuple-element.75.first_power, f32[32,3072]{1,0:T(8,128)S(1)} %copy-done, ...), custom_call_target="tpu_custom_call" | custom-call | tf_op jit(solution)/shard_map/pallas_call | solution.py:462
  (44 shorter events, 6.9 us)
Async XLA Ops:
  4.7 4.1 %collective-permute-start = (bf16[3,16,256]{2,1,0:T(8,128)(2,1)S(1)}, bf16[3,16,256]{2,1,0:T(8,128)(2,1)S(1)}, u32[]{:S(2)}, u32[]{:S(2)}) collective-permute-start(bf16[3,16,256]{2,1,0:T(8,128)(2,1)S(1)} %get-tuple-element.45), channel_id=1, source_target_pairs={{0,1},{1,0},{2,3},{3,2},{4,5},{5,4},{6,7},{7,6},{8,9},{9,8},{10,11... | collective-permute-start | bytes 73736 | tf_op jit(solution)/shard_map/ppermute | solution.py:490
  5.3 5.1 %collective-permute-start.1 = (bf16[3,16,256]{2,1,0:T(8,128)(2,1)S(1)}, bf16[3,16,256]{2,1,0:T(8,128)(2,1)S(1)}, u32[]{:S(2)}, u32[]{:S(2)}) collective-permute-start(bf16[3,16,256]{2,1,0:T(8,128)(2,1)S(1)} %get-tuple-element.46), channel_id=1, source_target_pairs={{0,7},{1,2},{2,1},{3,4},{4,3},{5,6},{6,5},{7,0},{8,15},{9,10},{10,... | collective-permute-start | bytes 73736 | tf_op jit(solution)/shard_map/ppermute | solution.py:491
  10.4 6.1 %collective-permute-start.2 = (bf16[64,256]{1,0:T(8,128)(2,1)S(1)}, bf16[64,256]{1,0:T(8,128)(2,1)S(1)}, u32[]{:S(2)}, u32[]{:S(2)}) collective-permute-start(bf16[64,256]{1,0:T(8,128)(2,1)S(1)} %get-tuple-element.48), channel_id=1, source_target_pairs={{0,8},{8,0},{16,24},{24,16},{1,9},{9,1},{17,25},{25,17},{2,10},{10... | collective-permute-start | bytes 98312 | tf_op jit(solution)/shard_map/ppermute | solution.py:486
  12.2 5.7 %collective-permute-start.3 = (bf16[64,256]{1,0:T(8,128)(2,1)S(1)}, bf16[64,256]{1,0:T(8,128)(2,1)S(1)}, u32[]{:S(2)}, u32[]{:S(2)}) collective-permute-start(bf16[64,256]{1,0:T(8,128)(2,1)S(1)} %get-tuple-element.49), channel_id=1, source_target_pairs={{0,24},{8,16},{16,8},{24,0},{1,25},{9,17},{17,9},{25,1},{2,26},{10... | collective-permute-start | bytes 98312 | tf_op jit(solution)/shard_map/ppermute | solution.py:486
  20.6 2.0 %collective-permute-start.4 = (bf16[3,16,256]{2,1,0:T(8,128)(2,1)S(1)}, bf16[3,16,256]{2,1,0:T(8,128)(2,1)S(1)}, u32[]{:S(2)}, u32[]{:S(2)}) collective-permute-start(bf16[3,16,256]{2,1,0:T(8,128)(2,1)S(1)} %get-tuple-element.54), channel_id=1, source_target_pairs={{0,1},{1,0},{2,3},{3,2},{4,5},{5,4},{6,7},{7,6},{8,9},{9,8},{10,11... | collective-permute-start | bytes 73736 | tf_op jit(solution)/shard_map/ppermute | solution.py:490
  20.6 4.2 %collective-permute-start.5 = (bf16[3,16,256]{2,1,0:T(8,128)(2,1)S(1)}, bf16[3,16,256]{2,1,0:T(8,128)(2,1)S(1)}, u32[]{:S(2)}, u32[]{:S(2)}) collective-permute-start(bf16[3,16,256]{2,1,0:T(8,128)(2,1)S(1)} %get-tuple-element.55), channel_id=1, source_target_pairs={{0,7},{1,2},{2,1},{3,4},{4,3},{5,6},{6,5},{7,0},{8,15},{9,10},{10,... | collective-permute-start | bytes 73736 | tf_op jit(solution)/shard_map/ppermute | solution.py:491
  24.9 4.0 %collective-permute-start.6 = (bf16[64,256]{1,0:T(8,128)(2,1)S(1)}, bf16[64,256]{1,0:T(8,128)(2,1)S(1)}, u32[]{:S(2)}, u32[]{:S(2)}) collective-permute-start(bf16[64,256]{1,0:T(8,128)(2,1)S(1)} %get-tuple-element.57), channel_id=1, source_target_pairs={{0,8},{8,0},{16,24},{24,16},{1,9},{9,1},{17,25},{25,17},{2,10},{10... | collective-permute-start | bytes 98312 | tf_op jit(solution)/shard_map/ppermute | solution.py:486
  25.0 5.8 %collective-permute-start.7 = (bf16[64,256]{1,0:T(8,128)(2,1)S(1)}, bf16[64,256]{1,0:T(8,128)(2,1)S(1)}, u32[]{:S(2)}, u32[]{:S(2)}) collective-permute-start(bf16[64,256]{1,0:T(8,128)(2,1)S(1)} %get-tuple-element.58), channel_id=1, source_target_pairs={{0,24},{8,16},{16,8},{24,0},{1,25},{9,17},{17,9},{25,1},{2,26},{10... | collective-permute-start | bytes 98312 | tf_op jit(solution)/shard_map/ppermute | solution.py:486
  30.8 35.2 %copy-start = (f32[32,3072]{1,0:T(8,128)S(1)}, f32[32,3072]{1,0:T(8,128)}, u32[]{:S(2)}) copy-start(f32[32,3072]{1,0:T(8,128)} %momentum.3) | copy-start | bytes 1179652
  33.5 1.3 %collective-permute-start.8 = (bf16[3,16,256]{2,1,0:T(8,128)(2,1)S(1)}, bf16[3,16,256]{2,1,0:T(8,128)(2,1)S(1)}, u32[]{:S(2)}, u32[]{:S(2)}) collective-permute-start(bf16[3,16,256]{2,1,0:T(8,128)(2,1)S(1)} %get-tuple-element.62), channel_id=1, source_target_pairs={{0,1},{1,0},{2,3},{3,2},{4,5},{5,4},{6,7},{7,6},{8,9},{9,8},{10,11... | collective-permute-start | bytes 73736 | tf_op jit(solution)/shard_map/ppermute | solution.py:490
  35.0 11.5 %collective-permute-start.9 = (bf16[2,128,128]{2,1,0:T(8,128)(2,1)S(1)}, bf16[2,128,128]{2,1,0:T(8,128)(2,1)S(1)}, u32[]{:S(2)}, u32[]{:S(2)}) collective-permute-start(bf16[2,128,128]{2,1,0:T(8,128)(2,1)S(1)} %get-tuple-element.64), channel_id=1, source_target_pairs={{0,8},{8,0},{16,24},{24,16},{1,9},{9,1},{17,25},{25,17},{2,10},{10... | collective-permute-start | bytes 196616 | tf_op jit(solution)/shard_map/ppermute | solution.py:483
  35.2 11.3 %collective-permute-start.10 = (bf16[2,128,128]{2,1,0:T(8,128)(2,1)S(1)}, bf16[2,128,128]{2,1,0:T(8,128)(2,1)S(1)}, u32[]{:S(2)}, u32[]{:S(2)}) collective-permute-start(bf16[2,128,128]{2,1,0:T(8,128)(2,1)S(1)} %get-tuple-element.65), channel_id=1, source_target_pairs={{0,16},{8,24},{16,0},{24,8},{1,17},{9,25},{17,1},{25,9},{2,18},{10... | collective-permute-start | bytes 196616 | tf_op jit(solution)/shard_map/ppermute | solution.py:483
  38.1 10.3 %collective-permute-start.11 = (bf16[2,128,128]{2,1,0:T(8,128)(2,1)S(1)}, bf16[2,128,128]{2,1,0:T(8,128)(2,1)S(1)}, u32[]{:S(2)}, u32[]{:S(2)}) collective-permute-start(bf16[2,128,128]{2,1,0:T(8,128)(2,1)S(1)} %get-tuple-element.66), channel_id=1, source_target_pairs={{0,24},{8,16},{16,8},{24,0},{1,25},{9,17},{17,9},{25,1},{2,26},{10... | collective-permute-start | bytes 196616 | tf_op jit(solution)/shard_map/ppermute | solution.py:483
  39.4 4.2 %collective-permute-start.16 = (bf16[3,16,256]{2,1,0:T(8,128)(2,1)S(1)}, bf16[3,16,256]{2,1,0:T(8,128)(2,1)S(1)}, u32[]{:S(2)}, u32[]{:S(2)}) collective-permute-start(bf16[3,16,256]{2,1,0:T(8,128)(2,1)S(1)} %get-tuple-element.68), channel_id=1, source_target_pairs={{0,7},{1,2},{2,1},{3,4},{4,3},{5,6},{6,5},{7,0},{8,15},{9,10},{10,... | collective-permute-start | bytes 73736 | tf_op jit(solution)/shard_map/ppermute | solution.py:491
  39.5 8.8 %collective-permute-start.12 = (bf16[2,128,128]{2,1,0:T(8,128)(2,1)S(1)}, bf16[2,128,128]{2,1,0:T(8,128)(2,1)S(1)}, u32[]{:S(2)}, u32[]{:S(2)}) collective-permute-start(bf16[2,128,128]{2,1,0:T(8,128)(2,1)S(1)} %get-tuple-element.63.rest_0_), channel_id=1, source_target_pairs={{0,1},{1,0},{2,3},{3,2},{4,5},{5,4},{6,7},{7,6},{8,9},{9,8},{10,11... | collective-permute-start | bytes 196616 | tf_op jit(solution)/shard_map/ppermute | solution.py:483
  43.9 7.1 %collective-permute-start.19 = (bf16[336,128]{1,0:T(8,128)(2,1)S(1)}, bf16[336,128]{1,0:T(8,128)(2,1)S(1)}, u32[]{:S(2)}, u32[]{:S(2)}) collective-permute-start(bf16[336,128]{1,0:T(8,128)(2,1)S(1)} %shard_map.75.rest_0_), channel_id=1, source_target_pairs={{0,24},{8,16},{16,8},{24,0},{1,25},{9,17},{17,9},{25,1},{2,26},{10... | collective-permute-start | bytes 258056 | tf_op jit(solution)/shard_map/ppermute | solution.py:483
  46.4 6.3 %collective-permute-start.18 = (bf16[336,128]{1,0:T(8,128)(2,1)S(1)}, bf16[336,128]{1,0:T(8,128)(2,1)S(1)}, u32[]{:S(2)}, u32[]{:S(2)}) collective-permute-start(bf16[336,128]{1,0:T(8,128)(2,1)S(1)} %shard_map.75.rest_0_), channel_id=1, source_target_pairs={{0,16},{8,24},{16,0},{24,8},{1,17},{9,25},{17,1},{25,9},{2,18},{10... | collective-permute-start | bytes 258056 | tf_op jit(solution)/shard_map/ppermute | solution.py:483
  46.4 6.3 %collective-permute-start.17 = (bf16[336,128]{1,0:T(8,128)(2,1)S(1)}, bf16[336,128]{1,0:T(8,128)(2,1)S(1)}, u32[]{:S(2)}, u32[]{:S(2)}) collective-permute-start(bf16[336,128]{1,0:T(8,128)(2,1)S(1)} %shard_map.75.rest_0_), channel_id=1, source_target_pairs={{0,8},{8,0},{16,24},{24,16},{1,9},{9,1},{17,25},{25,17},{2,10},{10... | collective-permute-start | bytes 258056 | tf_op jit(solution)/shard_map/ppermute | solution.py:483
  48.4 4.9 %collective-permute-start.13 = (bf16[2,128,128]{2,1,0:T(8,128)(2,1)S(1)}, bf16[2,128,128]{2,1,0:T(8,128)(2,1)S(1)}, u32[]{:S(2)}, u32[]{:S(2)}) collective-permute-start(bf16[2,128,128]{2,1,0:T(8,128)(2,1)S(1)} %collective-permute-done.9.rest_1_), channel_id=1, source_target_pairs={{0,1},{1,0},{2,3},{3,2},{4,5},{5,4},{6,7},{7,6},{8,9},{9,8},{10,11... | collective-permute-start | bytes 196616 | tf_op jit(solution)/shard_map/ppermute | solution.py:483
  48.4 5.0 %collective-permute-start.14 = (bf16[2,128,128]{2,1,0:T(8,128)(2,1)S(1)}, bf16[2,128,128]{2,1,0:T(8,128)(2,1)S(1)}, u32[]{:S(2)}, u32[]{:S(2)}) collective-permute-start(bf16[2,128,128]{2,1,0:T(8,128)(2,1)S(1)} %collective-permute-done.10.rest_2_), channel_id=1, source_target_pairs={{0,1},{1,0},{2,3},{3,2},{4,5},{5,4},{6,7},{7,6},{8,9},{9,8},{10,11... | collective-permute-start | bytes 196616 | tf_op jit(solution)/shard_map/ppermute | solution.py:483
  51.0 3.9 %collective-permute-start.20 = (bf16[336,128]{1,0:T(8,128)(2,1)S(1)}, bf16[336,128]{1,0:T(8,128)(2,1)S(1)}, u32[]{:S(2)}, u32[]{:S(2)}) collective-permute-start(bf16[336,128]{1,0:T(8,128)(2,1)S(1)} %shard_map.75.rest_0_), channel_id=1, source_target_pairs={{0,1},{1,0},{2,3},{3,2},{4,5},{5,4},{6,7},{7,6},{8,9},{9,8},{10,11... | collective-permute-start | bytes 258056 | tf_op jit(solution)/shard_map/ppermute | solution.py:483
  52.8 2.2 %collective-permute-start.23 = (bf16[336,128]{1,0:T(8,128)(2,1)S(1)}, bf16[336,128]{1,0:T(8,128)(2,1)S(1)}, u32[]{:S(2)}, u32[]{:S(2)}) collective-permute-start(bf16[336,128]{1,0:T(8,128)(2,1)S(1)} %collective-permute-done.19.rest_3_), channel_id=1, source_target_pairs={{0,1},{1,0},{2,3},{3,2},{4,5},{5,4},{6,7},{7,6},{8,9},{9,8},{10,11... | collective-permute-start | bytes 258056 | tf_op jit(solution)/shard_map/ppermute | solution.py:483
  52.8 2.2 %collective-permute-start.22 = (bf16[336,128]{1,0:T(8,128)(2,1)S(1)}, bf16[336,128]{1,0:T(8,128)(2,1)S(1)}, u32[]{:S(2)}, u32[]{:S(2)}) collective-permute-start(bf16[336,128]{1,0:T(8,128)(2,1)S(1)} %collective-permute-done.18.rest_2_), channel_id=1, source_target_pairs={{0,1},{1,0},{2,3},{3,2},{4,5},{5,4},{6,7},{7,6},{8,9},{9,8},{10,11... | collective-permute-start | bytes 258056 | tf_op jit(solution)/shard_map/ppermute | solution.py:483
  53.3 1.7 %collective-permute-start.21 = (bf16[336,128]{1,0:T(8,128)(2,1)S(1)}, bf16[336,128]{1,0:T(8,128)(2,1)S(1)}, u32[]{:S(2)}, u32[]{:S(2)}) collective-permute-start(bf16[336,128]{1,0:T(8,128)(2,1)S(1)} %collective-permute-done.17.rest_1_), channel_id=1, source_target_pairs={{0,1},{1,0},{2,3},{3,2},{4,5},{5,4},{6,7},{7,6},{8,9},{9,8},{10,11... | collective-permute-start | bytes 258056 | tf_op jit(solution)/shard_map/ppermute | solution.py:483
  53.4 1.3 %collective-permute-start.15 = (bf16[2,128,128]{2,1,0:T(8,128)(2,1)S(1)}, bf16[2,128,128]{2,1,0:T(8,128)(2,1)S(1)}, u32[]{:S(2)}, u32[]{:S(2)}) collective-permute-start(bf16[2,128,128]{2,1,0:T(8,128)(2,1)S(1)} %collective-permute-done.11.rest_3_), channel_id=1, source_target_pairs={{0,1},{1,0},{2,3},{3,2},{4,5},{5,4},{6,7},{7,6},{8,9},{9,8},{10,11... | collective-permute-start | bytes 196616 | tf_op jit(solution)/shard_map/ppermute | solution.py:483
  56.9 6.7 %collective-permute-start.24 = (bf16[32,1536]{1,0:T(8,128)(2,1)S(1)}, bf16[32,1536]{1,0:T(8,128)(2,1)S(1)}, u32[]{:S(2)}, u32[]{:S(2)}) collective-permute-start(bf16[32,1536]{1,0:T(8,128)(2,1)S(1)} %get-tuple-element.70), channel_id=1, source_target_pairs={{0,2},{2,0},{4,6},{6,4},{1,3},{3,1},{5,7},{7,5},{8,10},{10,8},{12,... | collective-permute-start | bytes 294920 | tf_op jit(solution)/shard_map/ppermute | solution.py:483
  58.3 7.1 %collective-permute-start.25 = (bf16[32,1536]{1,0:T(8,128)(2,1)S(1)}, bf16[32,1536]{1,0:T(8,128)(2,1)S(1)}, u32[]{:S(2)}, u32[]{:S(2)}) collective-permute-start(bf16[32,1536]{1,0:T(8,128)(2,1)S(1)} %get-tuple-element.71), channel_id=1, source_target_pairs={{0,4},{2,6},{4,0},{6,2},{1,5},{3,7},{5,1},{7,3},{8,12},{10,14},{12... | collective-permute-start | bytes 294920 | tf_op jit(solution)/shard_map/ppermute | solution.py:483
  59.4 6.6 %collective-permute-start.26 = (bf16[32,1536]{1,0:T(8,128)(2,1)S(1)}, bf16[32,1536]{1,0:T(8,128)(2,1)S(1)}, u32[]{:S(2)}, u32[]{:S(2)}) collective-permute-start(bf16[32,1536]{1,0:T(8,128)(2,1)S(1)} %get-tuple-element.72), channel_id=1, source_target_pairs={{0,6},{2,4},{4,2},{6,0},{1,7},{3,5},{5,3},{7,1},{8,14},{10,12},{12... | collective-permute-start | bytes 294920 | tf_op jit(solution)/shard_map/ppermute | solution.py:483
  61.1 6.3 %collective-permute-start.27 = (bf16[32,1536]{1,0:T(8,128)(2,1)S(1)}, bf16[32,1536]{1,0:T(8,128)(2,1)S(1)}, u32[]{:S(2)}, u32[]{:S(2)}) collective-permute-start(bf16[32,1536]{1,0:T(8,128)(2,1)S(1)} %get-tuple-element.78), channel_id=1, source_target_pairs={{0,2},{2,0},{4,6},{6,4},{1,3},{3,1},{5,7},{7,5},{8,10},{10,8},{12,... | collective-permute-start | bytes 294920 | tf_op jit(solution)/shard_map/ppermute | solution.py:483
  62.5 6.9 %collective-permute-start.28 = (bf16[32,1536]{1,0:T(8,128)(2,1)S(1)}, bf16[32,1536]{1,0:T(8,128)(2,1)S(1)}, u32[]{:S(2)}, u32[]{:S(2)}) collective-permute-start(bf16[32,1536]{1,0:T(8,128)(2,1)S(1)} %get-tuple-element.79), channel_id=1, source_target_pairs={{0,4},{2,6},{4,0},{6,2},{1,5},{3,7},{5,1},{7,3},{8,12},{10,14},{12... | collective-permute-start | bytes 294920 | tf_op jit(solution)/shard_map/ppermute | solution.py:483
  63.6 5.8 %collective-permute-start.29 = (bf16[32,1536]{1,0:T(8,128)(2,1)S(1)}, bf16[32,1536]{1,0:T(8,128)(2,1)S(1)}, u32[]{:S(2)}, u32[]{:S(2)}) collective-permute-start(bf16[32,1536]{1,0:T(8,128)(2,1)S(1)} %get-tuple-element.80), channel_id=1, source_target_pairs={{0,6},{2,4},{4,2},{6,0},{1,7},{3,5},{5,3},{7,1},{8,14},{10,12},{12... | collective-permute-start | bytes 294920 | tf_op jit(solution)/shard_map/ppermute | solution.py:483

commit v5 on v4

--- a/solution.py
+++ b/solution.py
@@ -51,6 +51,7 @@
         self.rim = up_to(MARGIN * self.wide, 16)
         self.packed = up_to(self.tall * self.cols + MARGIN * self.tall_pad, 32)
         self.scale = patch_len ** (-0.5)
+        self.block = 512 if patch_len % 512 == 0 else self.band
 
 
 class Place:
@@ -83,22 +84,21 @@
     return [sorted(even.items()), sorted(odd.items())]
 
 
-def reconstruct(z, place, coding, dic, pixels, tall_sum, own, ready=None):
+def reconstruct(z, place, coding, dic, pixels, tall_sum, own, step, ready=None):
     tall_sum[z.sites :, :] = jnp.zeros((z.tall * z.cols - z.sites, z.band), F32)
-    for pair in range(0, SPAN, 2):
+    for n, low in enumerate(range(0, z.patch, step)):
+        high = low + step
         if ready is not None:
-            ready(pair)
-            ready(pair + 1)
-        placed = jnp.dot(
-            coding, dic[:, pair * z.band : (pair + 2) * z.band], preferred_element_type=F32
-        )
-        for i in (pair, pair + 1):
-            part = placed[:, (i - pair) * z.band : (i - pair + 1) * z.band]
-            start = i * z.cols
+            ready(n)
+        placed = jnp.dot(coding, dic[:, low:high], preferred_element_type=F32)
+        for i in range(low // z.band, (high - 1) // z.band + 1):
+            left, right = max(low, i * z.band), min(high, (i + 1) * z.band)
+            part = placed[:, left - low : right - low]
+            lanes = slice(left - i * z.band, right - i * z.band)
             if i == 0:
-                tall_sum[0 : z.sites, :] = part
+                tall_sum[0 : z.sites, lanes] = part
             else:
-                tall_sum[start : start + z.sites, :] += part
+                tall_sum[i * z.cols : i * z.cols + z.sites, lanes] += part
     own[...] = jnp.zeros((z.tall, z.wide_pad, z.lanes), F32)
     own[0 : z.rows, 0 : z.cols, 0 : z.cell] = pixels[...].reshape(z.rows, z.cols, z.cell)
     for j in range(SPAN):
@@ -180,23 +180,22 @@
     (*sends, pixels, dic, potential, atoms, tall_sum, spread, picks, drawing, sems) = rest
     place = Place(*grid)
     early = [
-        pltpu.make_async_copy(picture, drawing, sems.at[SPAN]),
-        pltpu.make_async_copy(membrane, potential, sems.at[SPAN + 1]),
+        pltpu.make_async_copy(picture, drawing, sems.at[0]),
+        pltpu.make_async_copy(membrane, potential, sems.at[1]),
     ]
+    step = z.block
     copies = [
         pltpu.make_async_copy(
-            source.at[:, i * z.band : (i + 1) * z.band],
-            dic.at[:, i * z.band : (i + 1) * z.band],
-            sems.at[i],
+            source.at[:, low : low + step], dic.at[:, low : low + step], sems.at[2 + n]
         )
-        for i in range(SPAN)
+        for n, low in enumerate(range(0, z.patch, step))
     ]
     for copy in early + copies:
         copy.start()
     cells_of(z, drawing, pixels, spread, picks, early[0].wait)
     early[1].wait()
     coding = shrink(potential[...]).astype(BF16)
-    reconstruct(z, place, coding, dic, pixels, tall_sum, own, lambda i: copies[i].wait())
+    reconstruct(z, place, coding, dic, pixels, tall_sum, own, step, lambda i: copies[i].wait())
     send_sides(z, place, own, sends)
     owned = atoms.shape[0]
     atoms[...] = dic[pl.ds(pl.multiple_of(place.owner * owned, owned), owned), :]
@@ -281,7 +280,7 @@
         codes[...] = coding
     else:
         new_potential[...] = updated
-    reconstruct(z, place, coding, dic, pixels, tall_sum, own)
+    reconstruct(z, place, coding, dic, pixels, tall_sum, own, 2 * z.band)
     send_sides(z, place, own, sends)
 
 
@@ -516,7 +515,7 @@
             pltpu.VMEM((3 * picture.shape[2], z.cell), BF16),
             pltpu.VMEM((z.rows, picture.shape[0] * picture.shape[1], z.cell), BF16),
             pltpu.VMEM(picture.shape, F32),
-            pltpu.SemaphoreType.DMA((SPAN + 2,)),
+            pltpu.SemaphoreType.DMA((2 + z.patch // z.block,)),
         ],
         far=3,
     )

time: 70.7 us -> 70.9 us (level)
  no operation moved by 1% of the time
where the time goes in v5:
time: 70.9 us; the launch traced here: 70.8 us
  starting transfers between devices  30.9 us (44%)
  waiting for transfers between devices  22.1 us (31%)
  Pallas kernels  16 us (23%)
  between operations  0.97 us (1%)
  local copies, waits for them, and re-layouts  0.8 us (1%)
    ppermute x20, starting transfers between devices, met(): lax.ppermute(block, axis, [(i, offset(i, step, n)) for i in range(n)])  17.7 us
    pallas_call x13, Pallas kernels, call(): pl.pallas_call(kernel, out_shape=outs, in_specs=specs, out_specs=[leave]...  16 us
    ppermute x20, waiting for transfers between devices, met(): lax.ppermute(block, axis, [(i, offset(i, step, n)) for i in range(n)])  8.65 us
    ppermute x3, waiting for transfers between devices, sideways(): far_rim = lax.ppermute(blocks[1], ('yx', 'core'), odd)  7.62 us
    ppermute x4, starting transfers between devices, swapped(): lax.ppermute(b, axis, route)  6.88 us
    ppermute x3, starting transfers between devices, sideways(): far_rim = lax.ppermute(blocks[1], ('yx', 'core'), odd)  5.63 us
    ppermute x4, waiting for transfers between devices, swapped(): lax.ppermute(b, axis, route)  4.62 us
  transfers between devices with their start and end apart: 30, of which 13 were waited for; matrix products, arithmetic and copies ran while one was open for 1% of the time, Pallas kernels for 4%

profile of v5, /device:TPU:0, one launch (start us, length us, event | category | flops | bytes accessed | tf_op | source)
XLA Modules:
  0.0 70.8 jit_solution(2787759892014106735)
XLA Ops:
  0.6 4.2 %shard_map.67 = (f32[11,24,256]{2,1,0:T(8,128)S(1)}, bf16[3,16,256]{2,1,0:T(8,128)(2,1)S(1)}, bf16[3,16,256]{2,1,0:T(8,128)(2,1)S(1)}, f32[128,192]{1,0:T(8,128)...) custom-call(f32[128,1024]{1,0:T(8,128)} %bitcast.3, ...), custom_call_target="tpu_custom_call" | custom-call | tf_op jit(solution)/shard_map/pallas_call | solution.py:461
  5.4 3.5 %collective-permute-start.1 = (bf16[3,16,256]{2,1,0:T(8,128)(2,1)S(1)}, bf16[3,16,256]{2,1,0:T(8,128)(2,1)S(1)}, u32[]{:S(2)}, u32[]{:S(2)}) collective-permute-start(bf16[3,16,256]{2,1,0:T(8,128)(2,1)S(1)} %get-tuple-element.46), channel_id=1, source_target_pairs={{0,7},{1,2},{2,1},{3,4},{4,3},{5,6},{6,5},{7,0},{8,15},{9,10},{10,... | collective-permute-start | bytes 73736 | tf_op jit(solution)/shard_map/ppermute | solution.py:490
  8.9 1.5 %collective-permute-done.1.from_odd = bf16[3,16,256]{2,1,0:T(8,128)(2,1)S(1)} collective-permute-done((bf16[3,16,256]{2,1,0:T(8,128)(2,1)S(1)}, bf16[3,16,256]{2,1,0:T(8,128)(2,1)S(1)}, u32[]{:S(2)}, u32[]{:S(2)}) %collective-permute-start.1) | collective-permute-done | bytes 24608 | tf_op jit(solution)/shard_map/ppermute | solution.py:490
  10.5 1.8 %collective-permute-start.2 = (bf16[64,256]{1,0:T(8,128)(2,1)S(1)}, bf16[64,256]{1,0:T(8,128)(2,1)S(1)}, u32[]{:S(2)}, u32[]{:S(2)}) collective-permute-start(bf16[64,256]{1,0:T(8,128)(2,1)S(1)} %get-tuple-element.48), channel_id=1, source_target_pairs={{0,8},{8,0},{16,24},{24,16},{1,9},{9,1},{17,25},{25,17},{2,10},{10... | collective-permute-start | bytes 98312 | tf_op jit(solution)/shard_map/ppermute | solution.py:485
  12.3 2.5 %collective-permute-start.3 = (bf16[64,256]{1,0:T(8,128)(2,1)S(1)}, bf16[64,256]{1,0:T(8,128)(2,1)S(1)}, u32[]{:S(2)}, u32[]{:S(2)}) collective-permute-start(bf16[64,256]{1,0:T(8,128)(2,1)S(1)} %get-tuple-element.49), channel_id=1, source_target_pairs={{0,24},{8,16},{16,8},{24,0},{1,25},{9,17},{17,9},{25,1},{2,26},{10... | collective-permute-start | bytes 98312 | tf_op jit(solution)/shard_map/ppermute | solution.py:485
  14.8 1.8 %shard_map.69.turned = bf16[3072,1024]{1,0:T(8,128)(2,1)S(1)} custom-call(bf16[1024,3072]{1,0:T(8,128)(2,1)S(1)} %get-tuple-element.51.dic), custom_call_target="tpu_custom_call" | custom-call | tf_op jit(solution)/shard_map/pallas_call | solution.py:461
  16.7 1.4 %collective-permute-done.3.from_odd = bf16[64,256]{1,0:T(8,128)(2,1)S(1)} collective-permute-done((bf16[64,256]{1,0:T(8,128)(2,1)S(1)}, bf16[64,256]{1,0:T(8,128)(2,1)S(1)}, u32[]{:S(2)}, u32[]{:S(2)}) %collective-permute-start.3) | collective-permute-done | bytes 32800 | tf_op jit(solution)/shard_map/ppermute | solution.py:485
  18.1 2.6 %shard_map.70 = (f32[128,1024]{1,0:T(8,128)S(1)}, f32[11,24,256]{2,1,0:T(8,128)S(1)}, bf16[3,16,256]{2,1,0:T(8,128)(2,1)S(1)}, bf16[3,16,256]{2,1,0:T(8,128)(2,1)S(1)}) custom-call(f32[128,1024]{1,0:T(8,128)S(1)} %get-tuple-element.43.potential, f32[11,24,256]{2,1,0:T(8,128)S(1)} %get-tuple-element.47.joined, ...), custom_call_target="tpu_custom_call" | custom-call | tf_op jit(solution)/shard_map/pallas_call | solution.py:461
  20.8 2.0 %collective-permute-start.5 = (bf16[3,16,256]{2,1,0:T(8,128)(2,1)S(1)}, bf16[3,16,256]{2,1,0:T(8,128)(2,1)S(1)}, u32[]{:S(2)}, u32[]{:S(2)}) collective-permute-start(bf16[3,16,256]{2,1,0:T(8,128)(2,1)S(1)} %get-tuple-element.55), channel_id=1, source_target_pairs={{0,7},{1,2},{2,1},{3,4},{4,3},{5,6},{6,5},{7,0},{8,15},{9,10},{10,... | collective-permute-start | bytes 73736 | tf_op jit(solution)/shard_map/ppermute | solution.py:490
  22.8 2.2 %collective-permute-done.5.from_odd = bf16[3,16,256]{2,1,0:T(8,128)(2,1)S(1)} collective-permute-done((bf16[3,16,256]{2,1,0:T(8,128)(2,1)S(1)}, bf16[3,16,256]{2,1,0:T(8,128)(2,1)S(1)}, u32[]{:S(2)}, u32[]{:S(2)}) %collective-permute-start.5) | collective-permute-done | bytes 24608 | tf_op jit(solution)/shard_map/ppermute | solution.py:490
  25.2 2.5 %collective-permute-start.7 = (bf16[64,256]{1,0:T(8,128)(2,1)S(1)}, bf16[64,256]{1,0:T(8,128)(2,1)S(1)}, u32[]{:S(2)}, u32[]{:S(2)}) collective-permute-start(bf16[64,256]{1,0:T(8,128)(2,1)S(1)} %get-tuple-element.58), channel_id=1, source_target_pairs={{0,24},{8,16},{16,8},{24,0},{1,25},{9,17},{17,9},{25,1},{2,26},{10... | collective-permute-start | bytes 98312 | tf_op jit(solution)/shard_map/ppermute | solution.py:485
  27.7 1.4 %collective-permute-done.6.from_even = bf16[64,256]{1,0:T(8,128)(2,1)S(1)} collective-permute-done((bf16[64,256]{1,0:T(8,128)(2,1)S(1)}, bf16[64,256]{1,0:T(8,128)(2,1)S(1)}, u32[]{:S(2)}, u32[]{:S(2)}) %collective-permute-start.6) | collective-permute-done | bytes 32800 | tf_op jit(solution)/shard_map/ppermute | solution.py:485
  29.1 1.9 %collective-permute-done.7.from_odd = bf16[64,256]{1,0:T(8,128)(2,1)S(1)} collective-permute-done((bf16[64,256]{1,0:T(8,128)(2,1)S(1)}, bf16[64,256]{1,0:T(8,128)(2,1)S(1)}, u32[]{:S(2)}, u32[]{:S(2)}) %collective-permute-start.7) | collective-permute-done | bytes 32800 | tf_op jit(solution)/shard_map/ppermute | solution.py:485
  30.9 2.6 %shard_map.72 = (f32[128,1024]{1,0:T(8,128)S(1)}, f32[11,24,256]{2,1,0:T(8,128)S(1)}, bf16[3,16,256]{2,1,0:T(8,128)(2,1)S(1)}, bf16[3,16,256]{2,1,0:T(8,128)(2,1)S(1)}, bf16[128,1024]{1,0:T(8,128)(2,1)S(1)}) custom-call(f32[128,1024]{1,0:T(8,128)S(1)} %get-tuple-element.52.potential, f32[11,24,256]{2,1,0:T(8,128)S(1)} %get-tuple-element.56.joined, ...), custom_call_target="tpu_custom_call" | custom-call | tf_op jit(solution)/shard_map/pallas_call | solution.py:461
  33.7 1.2 %collective-permute-done.8._.from_even = bf16[3,16,256]{2,1,0:T(8,128)(2,1)S(1)} collective-permute-done((bf16[3,16,256]{2,1,0:T(8,128)(2,1)S(1)}, bf16[3,16,256]{2,1,0:T(8,128)(2,1)S(1)}, u32[]{:S(2)}, u32[]{:S(2)}) %collective-permute-start.8) | collective-permute-done | bytes 24608 | tf_op jit(solution)/shard_map/ppermute | solution.py:489
  35.3 2.9 %collective-permute-start.10 = (bf16[2,128,128]{2,1,0:T(8,128)(2,1)S(1)}, bf16[2,128,128]{2,1,0:T(8,128)(2,1)S(1)}, u32[]{:S(2)}, u32[]{:S(2)}) collective-permute-start(bf16[2,128,128]{2,1,0:T(8,128)(2,1)S(1)} %get-tuple-element.65), channel_id=1, source_target_pairs={{0,16},{8,24},{16,0},{24,8},{1,17},{9,25},{17,1},{25,9},{2,18},{10... | collective-permute-start | bytes 196616 | tf_op jit(solution)/shard_map/ppermute | solution.py:482
  38.2 1.4 %collective-permute-start.11 = (bf16[2,128,128]{2,1,0:T(8,128)(2,1)S(1)}, bf16[2,128,128]{2,1,0:T(8,128)(2,1)S(1)}, u32[]{:S(2)}, u32[]{:S(2)}) collective-permute-start(bf16[2,128,128]{2,1,0:T(8,128)(2,1)S(1)} %get-tuple-element.66), channel_id=1, source_target_pairs={{0,24},{8,16},{16,8},{24,0},{1,25},{9,17},{17,9},{25,1},{2,26},{10... | collective-permute-start | bytes 196616 | tf_op jit(solution)/shard_map/ppermute | solution.py:482
  39.9 3.9 %collective-permute-done.16.from_odd = bf16[3,16,256]{2,1,0:T(8,128)(2,1)S(1)} collective-permute-done((bf16[3,16,256]{2,1,0:T(8,128)(2,1)S(1)}, bf16[3,16,256]{2,1,0:T(8,128)(2,1)S(1)}, u32[]{:S(2)}, u32[]{:S(2)}) %collective-permute-start.16) | collective-permute-done | bytes 24608 | tf_op jit(solution)/shard_map/ppermute | solution.py:490
  44.0 2.5 %collective-permute-start.19 = (bf16[336,128]{1,0:T(8,128)(2,1)S(1)}, bf16[336,128]{1,0:T(8,128)(2,1)S(1)}, u32[]{:S(2)}, u32[]{:S(2)}) collective-permute-start(bf16[336,128]{1,0:T(8,128)(2,1)S(1)} %shard_map.75.rest_0_), channel_id=1, source_target_pairs={{0,24},{8,16},{16,8},{24,0},{1,25},{9,17},{17,9},{25,1},{2,26},{10... | collective-permute-start | bytes 258056 | tf_op jit(solution)/shard_map/ppermute | solution.py:482
  46.6 1.9 %collective-permute-start.17 = (bf16[336,128]{1,0:T(8,128)(2,1)S(1)}, bf16[336,128]{1,0:T(8,128)(2,1)S(1)}, u32[]{:S(2)}, u32[]{:S(2)}) collective-permute-start(bf16[336,128]{1,0:T(8,128)(2,1)S(1)} %shard_map.75.rest_0_), channel_id=1, source_target_pairs={{0,8},{8,0},{16,24},{24,16},{1,9},{9,1},{17,25},{25,17},{2,10},{10... | collective-permute-start | bytes 258056 | tf_op jit(solution)/shard_map/ppermute | solution.py:482
  49.0 2.1 %collective-permute-done.19.rest_3_ = bf16[336,128]{1,0:T(8,128)(2,1)S(1)} collective-permute-done((bf16[336,128]{1,0:T(8,128)(2,1)S(1)}, bf16[336,128]{1,0:T(8,128)(2,1)S(1)}, u32[]{:S(2)}, u32[]{:S(2)}) %collective-permute-start.19) | collective-permute-done | bytes 86048 | tf_op jit(solution)/shard_map/ppermute | solution.py:482
  51.1 1.8 %collective-permute-done.18.rest_2_ = bf16[336,128]{1,0:T(8,128)(2,1)S(1)} collective-permute-done((bf16[336,128]{1,0:T(8,128)(2,1)S(1)}, bf16[336,128]{1,0:T(8,128)(2,1)S(1)}, u32[]{:S(2)}, u32[]{:S(2)}) %collective-permute-start.18) | collective-permute-done | bytes 86048 | tf_op jit(solution)/shard_map/ppermute | solution.py:482
  55.1 1.9 %shard_map.76 = (bf16[32,1536]{1,0:T(8,128)(2,1)S(1)}, bf16[32,1536]{1,0:T(8,128)(2,1)S(1)}, bf16[32,1536]{1,0:T(8,128)(2,1)S(1)}, bf16[32,1536]{1,0:T(8,128)(2,1)S(1)}, bf16[1408,768]{1,0:T(8,128)(2,1)S(1)}) custom-call(bf16[128,1024]{1,0:T(8,128)(2,1)S(1)} %shard_map.74.across, bf16[336,128]{1,0:T(8,128)(2,1)S(1)} %shard_map.75.rest_0_, ...), custom_call_target="tpu_custom_call" | custom-call | tf_op jit(solution)/shard_map/pallas_call | solution.py:461
  57.0 1.4 %collective-permute-start.24 = (bf16[32,1536]{1,0:T(8,128)(2,1)S(1)}, bf16[32,1536]{1,0:T(8,128)(2,1)S(1)}, u32[]{:S(2)}, u32[]{:S(2)}) collective-permute-start(bf16[32,1536]{1,0:T(8,128)(2,1)S(1)} %get-tuple-element.70), channel_id=1, source_target_pairs={{0,2},{2,0},{4,6},{6,4},{1,3},{3,1},{5,7},{7,5},{8,10},{10,8},{12,... | collective-permute-start | bytes 294920 | tf_op jit(solution)/shard_map/ppermute | solution.py:482
  58.5 1.1 %collective-permute-start.25 = (bf16[32,1536]{1,0:T(8,128)(2,1)S(1)}, bf16[32,1536]{1,0:T(8,128)(2,1)S(1)}, u32[]{:S(2)}, u32[]{:S(2)}) collective-permute-start(bf16[32,1536]{1,0:T(8,128)(2,1)S(1)} %get-tuple-element.71), channel_id=1, source_target_pairs={{0,4},{2,6},{4,0},{6,2},{1,5},{3,7},{5,1},{7,3},{8,12},{10,14},{12... | collective-permute-start | bytes 294920 | tf_op jit(solution)/shard_map/ppermute | solution.py:482
  59.6 1.0 %collective-permute-start.26 = (bf16[32,1536]{1,0:T(8,128)(2,1)S(1)}, bf16[32,1536]{1,0:T(8,128)(2,1)S(1)}, u32[]{:S(2)}, u32[]{:S(2)}) collective-permute-start(bf16[32,1536]{1,0:T(8,128)(2,1)S(1)} %get-tuple-element.72), channel_id=1, source_target_pairs={{0,6},{2,4},{4,2},{6,0},{1,7},{3,5},{5,3},{7,1},{8,14},{10,12},{12... | collective-permute-start | bytes 294920 | tf_op jit(solution)/shard_map/ppermute | solution.py:482
  61.2 1.4 %collective-permute-start.27 = (bf16[32,1536]{1,0:T(8,128)(2,1)S(1)}, bf16[32,1536]{1,0:T(8,128)(2,1)S(1)}, u32[]{:S(2)}, u32[]{:S(2)}) collective-permute-start(bf16[32,1536]{1,0:T(8,128)(2,1)S(1)} %get-tuple-element.78), channel_id=1, source_target_pairs={{0,2},{2,0},{4,6},{6,4},{1,3},{3,1},{5,7},{7,5},{8,10},{10,8},{12,... | collective-permute-start | bytes 294920 | tf_op jit(solution)/shard_map/ppermute | solution.py:482
  62.6 1.1 %collective-permute-start.28 = (bf16[32,1536]{1,0:T(8,128)(2,1)S(1)}, bf16[32,1536]{1,0:T(8,128)(2,1)S(1)}, u32[]{:S(2)}, u32[]{:S(2)}) collective-permute-start(bf16[32,1536]{1,0:T(8,128)(2,1)S(1)} %get-tuple-element.79), channel_id=1, source_target_pairs={{0,4},{2,6},{4,0},{6,2},{1,5},{3,7},{5,1},{7,3},{8,12},{10,14},{12... | collective-permute-start | bytes 294920 | tf_op jit(solution)/shard_map/ppermute | solution.py:482
  63.8 1.0 %collective-permute-start.29 = (bf16[32,1536]{1,0:T(8,128)(2,1)S(1)}, bf16[32,1536]{1,0:T(8,128)(2,1)S(1)}, u32[]{:S(2)}, u32[]{:S(2)}) collective-permute-start(bf16[32,1536]{1,0:T(8,128)(2,1)S(1)} %get-tuple-element.80), channel_id=1, source_target_pairs={{0,6},{2,4},{4,2},{6,0},{1,7},{3,5},{5,3},{7,1},{8,14},{10,12},{12... | collective-permute-start | bytes 294920 | tf_op jit(solution)/shard_map/ppermute | solution.py:482
  66.3 1.2 %collective-permute-done.27.rest_1_ = bf16[32,1536]{1,0:T(8,128)(2,1)S(1)} collective-permute-done((bf16[32,1536]{1,0:T(8,128)(2,1)S(1)}, bf16[32,1536]{1,0:T(8,128)(2,1)S(1)}, u32[]{:S(2)}, u32[]{:S(2)}) %collective-permute-start.27) | collective-permute-done | bytes 98336 | tf_op jit(solution)/shard_map/ppermute | solution.py:482
  67.5 2.0 %collective-permute-done.28.rest_2_ = bf16[32,1536]{1,0:T(8,128)(2,1)S(1)} collective-permute-done((bf16[32,1536]{1,0:T(8,128)(2,1)S(1)}, bf16[32,1536]{1,0:T(8,128)(2,1)S(1)}, u32[]{:S(2)}, u32[]{:S(2)}) %collective-permute-start.28) | collective-permute-done | bytes 98336 | tf_op jit(solution)/shard_map/ppermute | solution.py:482
  69.6 1.0 %shard_map.79 = (f32[32,3072]{1,0:T(8,128)}, f32[32,3072]{1,0:T(8,128)}) custom-call(f32[32,1536]{1,0:T(8,128)S(1)} %get-tuple-element.73.first_updated, f32[32,1536]{1,0:T(8,128)S(1)} %get-tuple-element.74.first_weights, f32[32,128]{1,0:T(8,128)S(1)} %get-tuple-element.75.first_power, f32[32,3072]{1,0:T(8,128)S(1)} %copy-done, ...), custom_call_target="tpu_custom_call" | custom-call | tf_op jit(solution)/shard_map/pallas_call | solution.py:461
  (44 shorter events, 6.9 us)
Async XLA Ops:
  4.8 4.1 %collective-permute-start = (bf16[3,16,256]{2,1,0:T(8,128)(2,1)S(1)}, bf16[3,16,256]{2,1,0:T(8,128)(2,1)S(1)}, u32[]{:S(2)}, u32[]{:S(2)}) collective-permute-start(bf16[3,16,256]{2,1,0:T(8,128)(2,1)S(1)} %get-tuple-element.45), channel_id=1, source_target_pairs={{0,1},{1,0},{2,3},{3,2},{4,5},{5,4},{6,7},{7,6},{8,9},{9,8},{10,11... | collective-permute-start | bytes 73736 | tf_op jit(solution)/shard_map/ppermute | solution.py:489
  5.4 5.1 %collective-permute-start.1 = (bf16[3,16,256]{2,1,0:T(8,128)(2,1)S(1)}, bf16[3,16,256]{2,1,0:T(8,128)(2,1)S(1)}, u32[]{:S(2)}, u32[]{:S(2)}) collective-permute-start(bf16[3,16,256]{2,1,0:T(8,128)(2,1)S(1)} %get-tuple-element.46), channel_id=1, source_target_pairs={{0,7},{1,2},{2,1},{3,4},{4,3},{5,6},{6,5},{7,0},{8,15},{9,10},{10,... | collective-permute-start | bytes 73736 | tf_op jit(solution)/shard_map/ppermute | solution.py:490
  10.5 6.1 %collective-permute-start.2 = (bf16[64,256]{1,0:T(8,128)(2,1)S(1)}, bf16[64,256]{1,0:T(8,128)(2,1)S(1)}, u32[]{:S(2)}, u32[]{:S(2)}) collective-permute-start(bf16[64,256]{1,0:T(8,128)(2,1)S(1)} %get-tuple-element.48), channel_id=1, source_target_pairs={{0,8},{8,0},{16,24},{24,16},{1,9},{9,1},{17,25},{25,17},{2,10},{10... | collective-permute-start | bytes 98312 | tf_op jit(solution)/shard_map/ppermute | solution.py:485
  12.3 5.7 %collective-permute-start.3 = (bf16[64,256]{1,0:T(8,128)(2,1)S(1)}, bf16[64,256]{1,0:T(8,128)(2,1)S(1)}, u32[]{:S(2)}, u32[]{:S(2)}) collective-permute-start(bf16[64,256]{1,0:T(8,128)(2,1)S(1)} %get-tuple-element.49), channel_id=1, source_target_pairs={{0,24},{8,16},{16,8},{24,0},{1,25},{9,17},{17,9},{25,1},{2,26},{10... | collective-permute-start | bytes 98312 | tf_op jit(solution)/shard_map/ppermute | solution.py:485
  20.7 2.0 %collective-permute-start.4 = (bf16[3,16,256]{2,1,0:T(8,128)(2,1)S(1)}, bf16[3,16,256]{2,1,0:T(8,128)(2,1)S(1)}, u32[]{:S(2)}, u32[]{:S(2)}) collective-permute-start(bf16[3,16,256]{2,1,0:T(8,128)(2,1)S(1)} %get-tuple-element.54), channel_id=1, source_target_pairs={{0,1},{1,0},{2,3},{3,2},{4,5},{5,4},{6,7},{7,6},{8,9},{9,8},{10,11... | collective-permute-start | bytes 73736 | tf_op jit(solution)/shard_map/ppermute | solution.py:489
  20.8 4.2 %collective-permute-start.5 = (bf16[3,16,256]{2,1,0:T(8,128)(2,1)S(1)}, bf16[3,16,256]{2,1,0:T(8,128)(2,1)S(1)}, u32[]{:S(2)}, u32[]{:S(2)}) collective-permute-start(bf16[3,16,256]{2,1,0:T(8,128)(2,1)S(1)} %get-tuple-element.55), channel_id=1, source_target_pairs={{0,7},{1,2},{2,1},{3,4},{4,3},{5,6},{6,5},{7,0},{8,15},{9,10},{10,... | collective-permute-start | bytes 73736 | tf_op jit(solution)/shard_map/ppermute | solution.py:490
  25.1 4.0 %collective-permute-start.6 = (bf16[64,256]{1,0:T(8,128)(2,1)S(1)}, bf16[64,256]{1,0:T(8,128)(2,1)S(1)}, u32[]{:S(2)}, u32[]{:S(2)}) collective-permute-start(bf16[64,256]{1,0:T(8,128)(2,1)S(1)} %get-tuple-element.57), channel_id=1, source_target_pairs={{0,8},{8,0},{16,24},{24,16},{1,9},{9,1},{17,25},{25,17},{2,10},{10... | collective-permute-start | bytes 98312 | tf_op jit(solution)/shard_map/ppermute | solution.py:485
  25.2 5.8 %collective-permute-start.7 = (bf16[64,256]{1,0:T(8,128)(2,1)S(1)}, bf16[64,256]{1,0:T(8,128)(2,1)S(1)}, u32[]{:S(2)}, u32[]{:S(2)}) collective-permute-start(bf16[64,256]{1,0:T(8,128)(2,1)S(1)} %get-tuple-element.58), channel_id=1, source_target_pairs={{0,24},{8,16},{16,8},{24,0},{1,25},{9,17},{17,9},{25,1},{2,26},{10... | collective-permute-start | bytes 98312 | tf_op jit(solution)/shard_map/ppermute | solution.py:485
  30.9 35.2 %copy-start = (f32[32,3072]{1,0:T(8,128)S(1)}, f32[32,3072]{1,0:T(8,128)}, u32[]{:S(2)}) copy-start(f32[32,3072]{1,0:T(8,128)} %momentum.3) | copy-start | bytes 1179652
  33.6 1.3 %collective-permute-start.8 = (bf16[3,16,256]{2,1,0:T(8,128)(2,1)S(1)}, bf16[3,16,256]{2,1,0:T(8,128)(2,1)S(1)}, u32[]{:S(2)}, u32[]{:S(2)}) collective-permute-start(bf16[3,16,256]{2,1,0:T(8,128)(2,1)S(1)} %get-tuple-element.62), channel_id=1, source_target_pairs={{0,1},{1,0},{2,3},{3,2},{4,5},{5,4},{6,7},{7,6},{8,9},{9,8},{10,11... | collective-permute-start | bytes 73736 | tf_op jit(solution)/shard_map/ppermute | solution.py:489
  35.1 11.5 %collective-permute-start.9 = (bf16[2,128,128]{2,1,0:T(8,128)(2,1)S(1)}, bf16[2,128,128]{2,1,0:T(8,128)(2,1)S(1)}, u32[]{:S(2)}, u32[]{:S(2)}) collective-permute-start(bf16[2,128,128]{2,1,0:T(8,128)(2,1)S(1)} %get-tuple-element.64), channel_id=1, source_target_pairs={{0,8},{8,0},{16,24},{24,16},{1,9},{9,1},{17,25},{25,17},{2,10},{10... | collective-permute-start | bytes 196616 | tf_op jit(solution)/shard_map/ppermute | solution.py:482
  35.3 11.3 %collective-permute-start.10 = (bf16[2,128,128]{2,1,0:T(8,128)(2,1)S(1)}, bf16[2,128,128]{2,1,0:T(8,128)(2,1)S(1)}, u32[]{:S(2)}, u32[]{:S(2)}) collective-permute-start(bf16[2,128,128]{2,1,0:T(8,128)(2,1)S(1)} %get-tuple-element.65), channel_id=1, source_target_pairs={{0,16},{8,24},{16,0},{24,8},{1,17},{9,25},{17,1},{25,9},{2,18},{10... | collective-permute-start | bytes 196616 | tf_op jit(solution)/shard_map/ppermute | solution.py:482
  38.2 10.3 %collective-permute-start.11 = (bf16[2,128,128]{2,1,0:T(8,128)(2,1)S(1)}, bf16[2,128,128]{2,1,0:T(8,128)(2,1)S(1)}, u32[]{:S(2)}, u32[]{:S(2)}) collective-permute-start(bf16[2,128,128]{2,1,0:T(8,128)(2,1)S(1)} %get-tuple-element.66), channel_id=1, source_target_pairs={{0,24},{8,16},{16,8},{24,0},{1,25},{9,17},{17,9},{25,1},{2,26},{10... | collective-permute-start | bytes 196616 | tf_op jit(solution)/shard_map/ppermute | solution.py:482
  39.6 4.2 %collective-permute-start.16 = (bf16[3,16,256]{2,1,0:T(8,128)(2,1)S(1)}, bf16[3,16,256]{2,1,0:T(8,128)(2,1)S(1)}, u32[]{:S(2)}, u32[]{:S(2)}) collective-permute-start(bf16[3,16,256]{2,1,0:T(8,128)(2,1)S(1)} %get-tuple-element.68), channel_id=1, source_target_pairs={{0,7},{1,2},{2,1},{3,4},{4,3},{5,6},{6,5},{7,0},{8,15},{9,10},{10,... | collective-permute-start | bytes 73736 | tf_op jit(solution)/shard_map/ppermute | solution.py:490
  39.7 8.8 %collective-permute-start.12 = (bf16[2,128,128]{2,1,0:T(8,128)(2,1)S(1)}, bf16[2,128,128]{2,1,0:T(8,128)(2,1)S(1)}, u32[]{:S(2)}, u32[]{:S(2)}) collective-permute-start(bf16[2,128,128]{2,1,0:T(8,128)(2,1)S(1)} %get-tuple-element.63.rest_0_), channel_id=1, source_target_pairs={{0,1},{1,0},{2,3},{3,2},{4,5},{5,4},{6,7},{7,6},{8,9},{9,8},{10,11... | collective-permute-start | bytes 196616 | tf_op jit(solution)/shard_map/ppermute | solution.py:482
  44.0 7.1 %collective-permute-start.19 = (bf16[336,128]{1,0:T(8,128)(2,1)S(1)}, bf16[336,128]{1,0:T(8,128)(2,1)S(1)}, u32[]{:S(2)}, u32[]{:S(2)}) collective-permute-start(bf16[336,128]{1,0:T(8,128)(2,1)S(1)} %shard_map.75.rest_0_), channel_id=1, source_target_pairs={{0,24},{8,16},{16,8},{24,0},{1,25},{9,17},{17,9},{25,1},{2,26},{10... | collective-permute-start | bytes 258056 | tf_op jit(solution)/shard_map/ppermute | solution.py:482
  46.6 6.3 %collective-permute-start.18 = (bf16[336,128]{1,0:T(8,128)(2,1)S(1)}, bf16[336,128]{1,0:T(8,128)(2,1)S(1)}, u32[]{:S(2)}, u32[]{:S(2)}) collective-permute-start(bf16[336,128]{1,0:T(8,128)(2,1)S(1)} %shard_map.75.rest_0_), channel_id=1, source_target_pairs={{0,16},{8,24},{16,0},{24,8},{1,17},{9,25},{17,1},{25,9},{2,18},{10... | collective-permute-start | bytes 258056 | tf_op jit(solution)/shard_map/ppermute | solution.py:482
  46.6 6.3 %collective-permute-start.17 = (bf16[336,128]{1,0:T(8,128)(2,1)S(1)}, bf16[336,128]{1,0:T(8,128)(2,1)S(1)}, u32[]{:S(2)}, u32[]{:S(2)}) collective-permute-start(bf16[336,128]{1,0:T(8,128)(2,1)S(1)} %shard_map.75.rest_0_), channel_id=1, source_target_pairs={{0,8},{8,0},{16,24},{24,16},{1,9},{9,1},{17,25},{25,17},{2,10},{10... | collective-permute-start | bytes 258056 | tf_op jit(solution)/shard_map/ppermute | solution.py:482
  48.5 4.9 %collective-permute-start.13 = (bf16[2,128,128]{2,1,0:T(8,128)(2,1)S(1)}, bf16[2,128,128]{2,1,0:T(8,128)(2,1)S(1)}, u32[]{:S(2)}, u32[]{:S(2)}) collective-permute-start(bf16[2,128,128]{2,1,0:T(8,128)(2,1)S(1)} %collective-permute-done.9.rest_1_), channel_id=1, source_target_pairs={{0,1},{1,0},{2,3},{3,2},{4,5},{5,4},{6,7},{7,6},{8,9},{9,8},{10,11... | collective-permute-start | bytes 196616 | tf_op jit(solution)/shard_map/ppermute | solution.py:482
  48.5 5.0 %collective-permute-start.14 = (bf16[2,128,128]{2,1,0:T(8,128)(2,1)S(1)}, bf16[2,128,128]{2,1,0:T(8,128)(2,1)S(1)}, u32[]{:S(2)}, u32[]{:S(2)}) collective-permute-start(bf16[2,128,128]{2,1,0:T(8,128)(2,1)S(1)} %collective-permute-done.10.rest_2_), channel_id=1, source_target_pairs={{0,1},{1,0},{2,3},{3,2},{4,5},{5,4},{6,7},{7,6},{8,9},{9,8},{10,11... | collective-permute-start | bytes 196616 | tf_op jit(solution)/shard_map/ppermute | solution.py:482
  51.1 3.9 %collective-permute-start.20 = (bf16[336,128]{1,0:T(8,128)(2,1)S(1)}, bf16[336,128]{1,0:T(8,128)(2,1)S(1)}, u32[]{:S(2)}, u32[]{:S(2)}) collective-permute-start(bf16[336,128]{1,0:T(8,128)(2,1)S(1)} %shard_map.75.rest_0_), channel_id=1, source_target_pairs={{0,1},{1,0},{2,3},{3,2},{4,5},{5,4},{6,7},{7,6},{8,9},{9,8},{10,11... | collective-permute-start | bytes 258056 | tf_op jit(solution)/shard_map/ppermute | solution.py:482
  52.9 2.2 %collective-permute-start.23 = (bf16[336,128]{1,0:T(8,128)(2,1)S(1)}, bf16[336,128]{1,0:T(8,128)(2,1)S(1)}, u32[]{:S(2)}, u32[]{:S(2)}) collective-permute-start(bf16[336,128]{1,0:T(8,128)(2,1)S(1)} %collective-permute-done.19.rest_3_), channel_id=1, source_target_pairs={{0,1},{1,0},{2,3},{3,2},{4,5},{5,4},{6,7},{7,6},{8,9},{9,8},{10,11... | collective-permute-start | bytes 258056 | tf_op jit(solution)/shard_map/ppermute | solution.py:482
  52.9 2.2 %collective-permute-start.22 = (bf16[336,128]{1,0:T(8,128)(2,1)S(1)}, bf16[336,128]{1,0:T(8,128)(2,1)S(1)}, u32[]{:S(2)}, u32[]{:S(2)}) collective-permute-start(bf16[336,128]{1,0:T(8,128)(2,1)S(1)} %collective-permute-done.18.rest_2_), channel_id=1, source_target_pairs={{0,1},{1,0},{2,3},{3,2},{4,5},{5,4},{6,7},{7,6},{8,9},{9,8},{10,11... | collective-permute-start | bytes 258056 | tf_op jit(solution)/shard_map/ppermute | solution.py:482
  53.4 1.7 %collective-permute-start.21 = (bf16[336,128]{1,0:T(8,128)(2,1)S(1)}, bf16[336,128]{1,0:T(8,128)(2,1)S(1)}, u32[]{:S(2)}, u32[]{:S(2)}) collective-permute-start(bf16[336,128]{1,0:T(8,128)(2,1)S(1)} %collective-permute-done.17.rest_1_), channel_id=1, source_target_pairs={{0,1},{1,0},{2,3},{3,2},{4,5},{5,4},{6,7},{7,6},{8,9},{9,8},{10,11... | collective-permute-start | bytes 258056 | tf_op jit(solution)/shard_map/ppermute | solution.py:482
  53.5 1.3 %collective-permute-start.15 = (bf16[2,128,128]{2,1,0:T(8,128)(2,1)S(1)}, bf16[2,128,128]{2,1,0:T(8,128)(2,1)S(1)}, u32[]{:S(2)}, u32[]{:S(2)}) collective-permute-start(bf16[2,128,128]{2,1,0:T(8,128)(2,1)S(1)} %collective-permute-done.11.rest_3_), channel_id=1, source_target_pairs={{0,1},{1,0},{2,3},{3,2},{4,5},{5,4},{6,7},{7,6},{8,9},{9,8},{10,11... | collective-permute-start | bytes 196616 | tf_op jit(solution)/shard_map/ppermute | solution.py:482
  57.0 6.7 %collective-permute-start.24 = (bf16[32,1536]{1,0:T(8,128)(2,1)S(1)}, bf16[32,1536]{1,0:T(8,128)(2,1)S(1)}, u32[]{:S(2)}, u32[]{:S(2)}) collective-permute-start(bf16[32,1536]{1,0:T(8,128)(2,1)S(1)} %get-tuple-element.70), channel_id=1, source_target_pairs={{0,2},{2,0},{4,6},{6,4},{1,3},{3,1},{5,7},{7,5},{8,10},{10,8},{12,... | collective-permute-start | bytes 294920 | tf_op jit(solution)/shard_map/ppermute | solution.py:482
  58.5 7.1 %collective-permute-start.25 = (bf16[32,1536]{1,0:T(8,128)(2,1)S(1)}, bf16[32,1536]{1,0:T(8,128)(2,1)S(1)}, u32[]{:S(2)}, u32[]{:S(2)}) collective-permute-start(bf16[32,1536]{1,0:T(8,128)(2,1)S(1)} %get-tuple-element.71), channel_id=1, source_target_pairs={{0,4},{2,6},{4,0},{6,2},{1,5},{3,7},{5,1},{7,3},{8,12},{10,14},{12... | collective-permute-start | bytes 294920 | tf_op jit(solution)/shard_map/ppermute | solution.py:482
  59.6 6.6 %collective-permute-start.26 = (bf16[32,1536]{1,0:T(8,128)(2,1)S(1)}, bf16[32,1536]{1,0:T(8,128)(2,1)S(1)}, u32[]{:S(2)}, u32[]{:S(2)}) collective-permute-start(bf16[32,1536]{1,0:T(8,128)(2,1)S(1)} %get-tuple-element.72), channel_id=1, source_target_pairs={{0,6},{2,4},{4,2},{6,0},{1,7},{3,5},{5,3},{7,1},{8,14},{10,12},{12... | collective-permute-start | bytes 294920 | tf_op jit(solution)/shard_map/ppermute | solution.py:482
  61.2 6.3 %collective-permute-start.27 = (bf16[32,1536]{1,0:T(8,128)(2,1)S(1)}, bf16[32,1536]{1,0:T(8,128)(2,1)S(1)}, u32[]{:S(2)}, u32[]{:S(2)}) collective-permute-start(bf16[32,1536]{1,0:T(8,128)(2,1)S(1)} %get-tuple-element.78), channel_id=1, source_target_pairs={{0,2},{2,0},{4,6},{6,4},{1,3},{3,1},{5,7},{7,5},{8,10},{10,8},{12,... | collective-permute-start | bytes 294920 | tf_op jit(solution)/shard_map/ppermute | solution.py:482
  62.6 6.9 %collective-permute-start.28 = (bf16[32,1536]{1,0:T(8,128)(2,1)S(1)}, bf16[32,1536]{1,0:T(8,128)(2,1)S(1)}, u32[]{:S(2)}, u32[]{:S(2)}) collective-permute-start(bf16[32,1536]{1,0:T(8,128)(2,1)S(1)} %get-tuple-element.79), channel_id=1, source_target_pairs={{0,4},{2,6},{4,0},{6,2},{1,5},{3,7},{5,1},{7,3},{8,12},{10,14},{12... | collective-permute-start | bytes 294920 | tf_op jit(solution)/shard_map/ppermute | solution.py:482
  63.8 5.8 %collective-permute-start.29 = (bf16[32,1536]{1,0:T(8,128)(2,1)S(1)}, bf16[32,1536]{1,0:T(8,128)(2,1)S(1)}, u32[]{:S(2)}, u32[]{:S(2)}) collective-permute-start(bf16[32,1536]{1,0:T(8,128)(2,1)S(1)} %get-tuple-element.80), channel_id=1, source_target_pairs={{0,6},{2,4},{4,2},{6,0},{1,7},{3,5},{5,3},{7,1},{8,14},{10,12},{12... | collective-permute-start | bytes 294920 | tf_op jit(solution)/shard_map/ppermute | solution.py:482

commit v6 on v5

--- a/solution.py
+++ b/solution.py
@@ -51,7 +51,7 @@
         self.rim = up_to(MARGIN * self.wide, 16)
         self.packed = up_to(self.tall * self.cols + MARGIN * self.tall_pad, 32)
         self.scale = patch_len ** (-0.5)
-        self.block = 512 if patch_len % 512 == 0 else self.band
+        self.block = self.band
 
 
 class Place:
@@ -139,7 +139,7 @@
     return (a == b).astype(F32).astype(BF16)
 
 
-def cells_of(z, picture, pixels, spread, picks, ready):
+def cells_of(z, picture, pixels, spread, ready):
     channels, height, width = picture.shape
 
     def iota(shape, dim):
@@ -153,8 +153,6 @@
         + lax.div(image_row, STRIDE) * z.cell
         - lax.div(entry, STRIDE) * STRIDE
     )
-    for i in range(z.rows):
-        picks[i] = is_equal(away, i * z.cell)
     shape = (width, z.cell)
     mine = (lax.rem(iota(shape, 0), STRIDE) == lax.rem(iota(shape, 1), STRIDE)).astype(F32)
     ready()
@@ -167,7 +165,7 @@
     spread[2 * width :, :] = (rest - middle.astype(F32)).astype(BF16)
     for i in range(z.rows):
         moved = jnp.dot(
-            spread[...], picks[i], preferred_element_type=F32
+            spread[...], is_equal(away, i * z.cell), preferred_element_type=F32
         )
         whole = (moved[0:width] + moved[width : 2 * width]) + moved[2 * width :]
         whole = (whole * mine).reshape(z.cols, STRIDE, z.cell)
@@ -177,7 +175,7 @@
 def first_kernel(
     z, grid, membrane, picture, source, own, *rest
 ):
-    (*sends, pixels, dic, potential, atoms, tall_sum, spread, picks, drawing, sems) = rest
+    (*sends, pixels, dic, potential, atoms, tall_sum, spread, drawing, sems) = rest
     place = Place(*grid)
     early = [
         pltpu.make_async_copy(picture, drawing, sems.at[0]),
@@ -192,7 +190,7 @@
     ]
     for copy in early + copies:
         copy.start()
-    cells_of(z, drawing, pixels, spread, picks, early[0].wait)
+    cells_of(z, drawing, pixels, spread, early[0].wait)
     early[1].wait()
     coding = shrink(potential[...]).astype(BF16)
     reconstruct(z, place, coding, dic, pixels, tall_sum, own, step, lambda i: copies[i].wait())
@@ -513,7 +511,6 @@
         [
             tall_v,
             pltpu.VMEM((3 * picture.shape[2], z.cell), BF16),
-            pltpu.VMEM((z.rows, picture.shape[0] * picture.shape[1], z.cell), BF16),
             pltpu.VMEM(picture.shape, F32),
             pltpu.SemaphoreType.DMA((2 + z.patch // z.block,)),
         ],
@@ -574,7 +571,13 @@
         [own_v, flat_v],
     )
 
-    near = along_row([packed] * rows_n)
+    near = [packed]
+    for x in range(1, rows_n):
+        low = x & -x
+        if power:
+            near.append(met(near[x - low], "row", rows_n, low))
+        else:
+            near.append(met(packed, "row", rows_n, rows_n - x))
     far = across_chip(near)
     stride = members * z.cols
     group_atoms = atom_count // members

time: 70.9 us -> 69.5 us (0.980)
  starting transfers between devices: 30.9 us -> 29.8 us
    ppermute x20, starting transfers between devices: 17.7 us -> 15.4 us  [met(): lax.ppermute(block, axis, [(i, offset(i, step, n)) for i in range(n)])]
    ppermute x20, waiting for transfers between devices: 8.65 us -> 10.9 us  [met(): lax.ppermute(block, axis, [(i, offset(i, step, n)) for i in range(n)])]
    ppermute x3, starting transfers between devices: 5.63 us -> 6.82 us  [sideways(): far_rim = lax.ppermute(blocks[1], ('yx', 'core'), odd)]
    ppermute x3, waiting for transfers between devices: 1.19 us -> 0.01 us  [sideways(): near_rim = lax.ppermute(blocks[0], ('yx', 'core'), even)]
    ppermute x3, waiting for transfers between devices: 7.62 us -> 6.67 us  [sideways(): far_rim = lax.ppermute(blocks[1], ('yx', 'core'), odd)]
  transfers between devices with their start and end apart: 30 -> 30, of which waited for: 13 -> 15; matrix products, arithmetic and copies ran while one was open for 1% -> 1% of each run, Pallas kernels for 4% -> 4%
where the time goes in v6:
time: 69.5 us; the launch traced here: 69.4 us
  starting transfers between devices  29.8 us (43%)
  waiting for transfers between devices  22.2 us (32%)
  Pallas kernels  15.6 us (22%)
  between operations  0.97 us (1%)
  local copies, waits for them, and re-layouts  0.8 us (1%)
    pallas_call x13, Pallas kernels, call(): pl.pallas_call(kernel, out_shape=outs, in_specs=specs, out_specs=[leave]...  15.6 us
    ppermute x20, starting transfers between devices, met(): lax.ppermute(block, axis, [(i, offset(i, step, n)) for i in range(n)])  15.4 us
    ppermute x20, waiting for transfers between devices, met(): lax.ppermute(block, axis, [(i, offset(i, step, n)) for i in range(n)])  10.9 us
    ppermute x4, starting transfers between devices, swapped(): lax.ppermute(b, axis, route)  6.86 us
    ppermute x3, starting transfers between devices, sideways(): far_rim = lax.ppermute(blocks[1], ('yx', 'core'), odd)  6.82 us
    ppermute x3, waiting for transfers between devices, sideways(): far_rim = lax.ppermute(blocks[1], ('yx', 'core'), odd)  6.67 us
    ppermute x4, waiting for transfers between devices, swapped(): lax.ppermute(b, axis, route)  4.64 us
  transfers between devices with their start and end apart: 30, of which 15 were waited for; matrix products, arithmetic and copies ran while one was open for 1% of the time, Pallas kernels for 4%

profile of v6, /device:TPU:0, one launch (start us, length us, event | category | flops | bytes accessed | tf_op | source)
XLA Modules:
  0.0 69.4 jit_solution(8284633589203568459)
XLA Ops:
  0.6 3.8 %shard_map.67 = (f32[11,24,256]{2,1,0:T(8,128)S(1)}, bf16[3,16,256]{2,1,0:T(8,128)(2,1)S(1)}, bf16[3,16,256]{2,1,0:T(8,128)(2,1)S(1)}, f32[128,192]{1,0:T(8,128)...) custom-call(f32[128,1024]{1,0:T(8,128)} %bitcast.3, ...), custom_call_target="tpu_custom_call" | custom-call | tf_op jit(solution)/shard_map/pallas_call | solution.py:459
  5.0 3.5 %collective-permute-start.1 = (bf16[3,16,256]{2,1,0:T(8,128)(2,1)S(1)}, bf16[3,16,256]{2,1,0:T(8,128)(2,1)S(1)}, u32[]{:S(2)}, u32[]{:S(2)}) collective-permute-start(bf16[3,16,256]{2,1,0:T(8,128)(2,1)S(1)} %get-tuple-element.46), channel_id=1, source_target_pairs={{0,7},{1,2},{2,1},{3,4},{4,3},{5,6},{6,5},{7,0},{8,15},{9,10},{10,... | collective-permute-start | bytes 73736 | tf_op jit(solution)/shard_map/ppermute | solution.py:488
  8.6 1.5 %collective-permute-done.1.from_odd = bf16[3,16,256]{2,1,0:T(8,128)(2,1)S(1)} collective-permute-done((bf16[3,16,256]{2,1,0:T(8,128)(2,1)S(1)}, bf16[3,16,256]{2,1,0:T(8,128)(2,1)S(1)}, u32[]{:S(2)}, u32[]{:S(2)}) %collective-permute-start.1) | collective-permute-done | bytes 24608 | tf_op jit(solution)/shard_map/ppermute | solution.py:488
  10.2 1.8 %collective-permute-start.2 = (bf16[64,256]{1,0:T(8,128)(2,1)S(1)}, bf16[64,256]{1,0:T(8,128)(2,1)S(1)}, u32[]{:S(2)}, u32[]{:S(2)}) collective-permute-start(bf16[64,256]{1,0:T(8,128)(2,1)S(1)} %get-tuple-element.48), channel_id=1, source_target_pairs={{0,8},{8,0},{16,24},{24,16},{1,9},{9,1},{17,25},{25,17},{2,10},{10... | collective-permute-start | bytes 98312 | tf_op jit(solution)/shard_map/ppermute | solution.py:483
  12.0 2.5 %collective-permute-start.3 = (bf16[64,256]{1,0:T(8,128)(2,1)S(1)}, bf16[64,256]{1,0:T(8,128)(2,1)S(1)}, u32[]{:S(2)}, u32[]{:S(2)}) collective-permute-start(bf16[64,256]{1,0:T(8,128)(2,1)S(1)} %get-tuple-element.49), channel_id=1, source_target_pairs={{0,24},{8,16},{16,8},{24,0},{1,25},{9,17},{17,9},{25,1},{2,26},{10... | collective-permute-start | bytes 98312 | tf_op jit(solution)/shard_map/ppermute | solution.py:483
  14.5 1.8 %shard_map.69.turned = bf16[3072,1024]{1,0:T(8,128)(2,1)S(1)} custom-call(bf16[1024,3072]{1,0:T(8,128)(2,1)S(1)} %get-tuple-element.51.dic), custom_call_target="tpu_custom_call" | custom-call | tf_op jit(solution)/shard_map/pallas_call | solution.py:459
  16.3 1.4 %collective-permute-done.3.from_odd = bf16[64,256]{1,0:T(8,128)(2,1)S(1)} collective-permute-done((bf16[64,256]{1,0:T(8,128)(2,1)S(1)}, bf16[64,256]{1,0:T(8,128)(2,1)S(1)}, u32[]{:S(2)}, u32[]{:S(2)}) %collective-permute-start.3) | collective-permute-done | bytes 32800 | tf_op jit(solution)/shard_map/ppermute | solution.py:483
  17.7 2.6 %shard_map.70 = (f32[128,1024]{1,0:T(8,128)S(1)}, f32[11,24,256]{2,1,0:T(8,128)S(1)}, bf16[3,16,256]{2,1,0:T(8,128)(2,1)S(1)}, bf16[3,16,256]{2,1,0:T(8,128)(2,1)S(1)}) custom-call(f32[128,1024]{1,0:T(8,128)S(1)} %get-tuple-element.43.potential, f32[11,24,256]{2,1,0:T(8,128)S(1)} %get-tuple-element.47.joined, ...), custom_call_target="tpu_custom_call" | custom-call | tf_op jit(solution)/shard_map/pallas_call | solution.py:459
  20.4 2.0 %collective-permute-start.5 = (bf16[3,16,256]{2,1,0:T(8,128)(2,1)S(1)}, bf16[3,16,256]{2,1,0:T(8,128)(2,1)S(1)}, u32[]{:S(2)}, u32[]{:S(2)}) collective-permute-start(bf16[3,16,256]{2,1,0:T(8,128)(2,1)S(1)} %get-tuple-element.55), channel_id=1, source_target_pairs={{0,7},{1,2},{2,1},{3,4},{4,3},{5,6},{6,5},{7,0},{8,15},{9,10},{10,... | collective-permute-start | bytes 73736 | tf_op jit(solution)/shard_map/ppermute | solution.py:488
  22.4 2.2 %collective-permute-done.5.from_odd = bf16[3,16,256]{2,1,0:T(8,128)(2,1)S(1)} collective-permute-done((bf16[3,16,256]{2,1,0:T(8,128)(2,1)S(1)}, bf16[3,16,256]{2,1,0:T(8,128)(2,1)S(1)}, u32[]{:S(2)}, u32[]{:S(2)}) %collective-permute-start.5) | collective-permute-done | bytes 24608 | tf_op jit(solution)/shard_map/ppermute | solution.py:488
  24.8 2.5 %collective-permute-start.7 = (bf16[64,256]{1,0:T(8,128)(2,1)S(1)}, bf16[64,256]{1,0:T(8,128)(2,1)S(1)}, u32[]{:S(2)}, u32[]{:S(2)}) collective-permute-start(bf16[64,256]{1,0:T(8,128)(2,1)S(1)} %get-tuple-element.58), channel_id=1, source_target_pairs={{0,24},{8,16},{16,8},{24,0},{1,25},{9,17},{17,9},{25,1},{2,26},{10... | collective-permute-start | bytes 98312 | tf_op jit(solution)/shard_map/ppermute | solution.py:483
  27.3 1.4 %collective-permute-done.6.from_even = bf16[64,256]{1,0:T(8,128)(2,1)S(1)} collective-permute-done((bf16[64,256]{1,0:T(8,128)(2,1)S(1)}, bf16[64,256]{1,0:T(8,128)(2,1)S(1)}, u32[]{:S(2)}, u32[]{:S(2)}) %collective-permute-start.6) | collective-permute-done | bytes 32800 | tf_op jit(solution)/shard_map/ppermute | solution.py:483
  28.7 1.9 %collective-permute-done.7.from_odd = bf16[64,256]{1,0:T(8,128)(2,1)S(1)} collective-permute-done((bf16[64,256]{1,0:T(8,128)(2,1)S(1)}, bf16[64,256]{1,0:T(8,128)(2,1)S(1)}, u32[]{:S(2)}, u32[]{:S(2)}) %collective-permute-start.7) | collective-permute-done | bytes 32800 | tf_op jit(solution)/shard_map/ppermute | solution.py:483
  30.6 2.6 %shard_map.72 = (f32[128,1024]{1,0:T(8,128)S(1)}, f32[11,24,256]{2,1,0:T(8,128)S(1)}, bf16[3,16,256]{2,1,0:T(8,128)(2,1)S(1)}, bf16[3,16,256]{2,1,0:T(8,128)(2,1)S(1)}, bf16[128,1024]{1,0:T(8,128)(2,1)S(1)}) custom-call(f32[128,1024]{1,0:T(8,128)S(1)} %get-tuple-element.52.potential, f32[11,24,256]{2,1,0:T(8,128)S(1)} %get-tuple-element.56.joined, ...), custom_call_target="tpu_custom_call" | custom-call | tf_op jit(solution)/shard_map/pallas_call | solution.py:459
  33.3 1.3 %collective-permute-start.16 = (bf16[3,16,256]{2,1,0:T(8,128)(2,1)S(1)}, bf16[3,16,256]{2,1,0:T(8,128)(2,1)S(1)}, u32[]{:S(2)}, u32[]{:S(2)}) collective-permute-start(bf16[3,16,256]{2,1,0:T(8,128)(2,1)S(1)} %get-tuple-element.68), channel_id=1, source_target_pairs={{0,7},{1,2},{2,1},{3,4},{4,3},{5,6},{6,5},{7,0},{8,15},{9,10},{10,... | collective-permute-start | bytes 73736 | tf_op jit(solution)/shard_map/ppermute | solution.py:488
  34.6 2.9 %collective-permute-done.16.from_odd = bf16[3,16,256]{2,1,0:T(8,128)(2,1)S(1)} collective-permute-done((bf16[3,16,256]{2,1,0:T(8,128)(2,1)S(1)}, bf16[3,16,256]{2,1,0:T(8,128)(2,1)S(1)}, u32[]{:S(2)}, u32[]{:S(2)}) %collective-permute-start.16) | collective-permute-done | bytes 24608 | tf_op jit(solution)/shard_map/ppermute | solution.py:488
  37.9 1.2 %collective-permute-start.18 = (bf16[336,128]{1,0:T(8,128)(2,1)S(1)}, bf16[336,128]{1,0:T(8,128)(2,1)S(1)}, u32[]{:S(2)}, u32[]{:S(2)}) collective-permute-start(bf16[336,128]{1,0:T(8,128)(2,1)S(1)} %shard_map.75.rest_0_), channel_id=1, source_target_pairs={{0,16},{8,24},{16,0},{24,8},{1,17},{9,25},{17,1},{25,9},{2,18},{10... | collective-permute-start | bytes 258056 | tf_op jit(solution)/shard_map/ppermute | solution.py:480
  39.3 1.9 %collective-permute-start.9 = (bf16[2,128,128]{2,1,0:T(8,128)(2,1)S(1)}, bf16[2,128,128]{2,1,0:T(8,128)(2,1)S(1)}, u32[]{:S(2)}, u32[]{:S(2)}) collective-permute-start(bf16[2,128,128]{2,1,0:T(8,128)(2,1)S(1)} %get-tuple-element.64), channel_id=1, source_target_pairs={{0,8},{8,0},{16,24},{24,16},{1,9},{9,1},{17,25},{25,17},{2,10},{10... | collective-permute-start | bytes 196616 | tf_op jit(solution)/shard_map/ppermute | solution.py:480
  41.3 2.5 %collective-permute-start.11 = (bf16[2,128,128]{2,1,0:T(8,128)(2,1)S(1)}, bf16[2,128,128]{2,1,0:T(8,128)(2,1)S(1)}, u32[]{:S(2)}, u32[]{:S(2)}) collective-permute-start(bf16[2,128,128]{2,1,0:T(8,128)(2,1)S(1)} %get-tuple-element.66), channel_id=1, source_target_pairs={{0,24},{8,16},{16,8},{24,0},{1,25},{9,17},{17,9},{25,1},{2,26},{10... | collective-permute-start | bytes 196616 | tf_op jit(solution)/shard_map/ppermute | solution.py:480
  43.8 1.0 %collective-permute-start.17 = (bf16[336,128]{1,0:T(8,128)(2,1)S(1)}, bf16[336,128]{1,0:T(8,128)(2,1)S(1)}, u32[]{:S(2)}, u32[]{:S(2)}) collective-permute-start(bf16[336,128]{1,0:T(8,128)(2,1)S(1)} %shard_map.75.rest_0_), channel_id=1, source_target_pairs={{0,8},{8,0},{16,24},{24,16},{1,9},{9,1},{17,25},{25,17},{2,10},{10... | collective-permute-start | bytes 258056 | tf_op jit(solution)/shard_map/ppermute | solution.py:480
  44.8 2.3 %collective-permute-done.18.rest_2_ = bf16[336,128]{1,0:T(8,128)(2,1)S(1)} collective-permute-done((bf16[336,128]{1,0:T(8,128)(2,1)S(1)}, bf16[336,128]{1,0:T(8,128)(2,1)S(1)}, u32[]{:S(2)}, u32[]{:S(2)}) %collective-permute-start.18) | collective-permute-done | bytes 86048 | tf_op jit(solution)/shard_map/ppermute | solution.py:480
  47.0 2.0 %collective-permute-done.10.rest_2_ = bf16[2,128,128]{2,1,0:T(8,128)(2,1)S(1)} collective-permute-done((bf16[2,128,128]{2,1,0:T(8,128)(2,1)S(1)}, bf16[2,128,128]{2,1,0:T(8,128)(2,1)S(1)}, u32[]{:S(2)}, u32[]{:S(2)}) %collective-permute-start.10) | collective-permute-done | bytes 65568 | tf_op jit(solution)/shard_map/ppermute | solution.py:480
  49.7 1.2 %collective-permute-done.17.rest_1_ = bf16[336,128]{1,0:T(8,128)(2,1)S(1)} collective-permute-done((bf16[336,128]{1,0:T(8,128)(2,1)S(1)}, bf16[336,128]{1,0:T(8,128)(2,1)S(1)}, u32[]{:S(2)}, u32[]{:S(2)}) %collective-permute-start.17) | collective-permute-done | bytes 86048 | tf_op jit(solution)/shard_map/ppermute | solution.py:480
  52.5 0.9 %collective-permute-done.15.rest_7_ = bf16[2,128,128]{2,1,0:T(8,128)(2,1)S(1)} collective-permute-done((bf16[2,128,128]{2,1,0:T(8,128)(2,1)S(1)}, bf16[2,128,128]{2,1,0:T(8,128)(2,1)S(1)}, u32[]{:S(2)}, u32[]{:S(2)}) %collective-permute-start.15) | collective-permute-done | bytes 65568 | tf_op jit(solution)/shard_map/ppermute | solution.py:480
  53.6 1.9 %shard_map.76 = (bf16[32,1536]{1,0:T(8,128)(2,1)S(1)}, bf16[32,1536]{1,0:T(8,128)(2,1)S(1)}, bf16[32,1536]{1,0:T(8,128)(2,1)S(1)}, bf16[32,1536]{1,0:T(8,128)(2,1)S(1)}, bf16[1408,768]{1,0:T(8,128)(2,1)S(1)}) custom-call(bf16[128,1024]{1,0:T(8,128)(2,1)S(1)} %shard_map.74.across, bf16[336,128]{1,0:T(8,128)(2,1)S(1)} %shard_map.75.rest_0_, ...), custom_call_target="tpu_custom_call" | custom-call | tf_op jit(solution)/shard_map/pallas_call | solution.py:459
  55.6 1.3 %collective-permute-start.24 = (bf16[32,1536]{1,0:T(8,128)(2,1)S(1)}, bf16[32,1536]{1,0:T(8,128)(2,1)S(1)}, u32[]{:S(2)}, u32[]{:S(2)}) collective-permute-start(bf16[32,1536]{1,0:T(8,128)(2,1)S(1)} %get-tuple-element.70), channel_id=1, source_target_pairs={{0,2},{2,0},{4,6},{6,4},{1,3},{3,1},{5,7},{7,5},{8,10},{10,8},{12,... | collective-permute-start | bytes 294920 | tf_op jit(solution)/shard_map/ppermute | solution.py:480
  56.9 1.5 %collective-permute-start.25 = (bf16[32,1536]{1,0:T(8,128)(2,1)S(1)}, bf16[32,1536]{1,0:T(8,128)(2,1)S(1)}, u32[]{:S(2)}, u32[]{:S(2)}) collective-permute-start(bf16[32,1536]{1,0:T(8,128)(2,1)S(1)} %get-tuple-element.71), channel_id=1, source_target_pairs={{0,4},{2,6},{4,0},{6,2},{1,5},{3,7},{5,1},{7,3},{8,12},{10,14},{12... | collective-permute-start | bytes 294920 | tf_op jit(solution)/shard_map/ppermute | solution.py:480
  59.7 1.3 %collective-permute-start.27 = (bf16[32,1536]{1,0:T(8,128)(2,1)S(1)}, bf16[32,1536]{1,0:T(8,128)(2,1)S(1)}, u32[]{:S(2)}, u32[]{:S(2)}) collective-permute-start(bf16[32,1536]{1,0:T(8,128)(2,1)S(1)} %get-tuple-element.78), channel_id=1, source_target_pairs={{0,2},{2,0},{4,6},{6,4},{1,3},{3,1},{5,7},{7,5},{8,10},{10,8},{12,... | collective-permute-start | bytes 294920 | tf_op jit(solution)/shard_map/ppermute | solution.py:480
  61.1 1.5 %collective-permute-start.28 = (bf16[32,1536]{1,0:T(8,128)(2,1)S(1)}, bf16[32,1536]{1,0:T(8,128)(2,1)S(1)}, u32[]{:S(2)}, u32[]{:S(2)}) collective-permute-start(bf16[32,1536]{1,0:T(8,128)(2,1)S(1)} %get-tuple-element.79), channel_id=1, source_target_pairs={{0,4},{2,6},{4,0},{6,2},{1,5},{3,7},{5,1},{7,3},{8,12},{10,14},{12... | collective-permute-start | bytes 294920 | tf_op jit(solution)/shard_map/ppermute | solution.py:480
  66.0 1.0 %collective-permute-done.28.rest_2_ = bf16[32,1536]{1,0:T(8,128)(2,1)S(1)} collective-permute-done((bf16[32,1536]{1,0:T(8,128)(2,1)S(1)}, bf16[32,1536]{1,0:T(8,128)(2,1)S(1)}, u32[]{:S(2)}, u32[]{:S(2)}) %collective-permute-start.28) | collective-permute-done | bytes 98336 | tf_op jit(solution)/shard_map/ppermute | solution.py:480
  67.1 1.1 %collective-permute-done.29.rest_3_ = bf16[32,1536]{1,0:T(8,128)(2,1)S(1)} collective-permute-done((bf16[32,1536]{1,0:T(8,128)(2,1)S(1)}, bf16[32,1536]{1,0:T(8,128)(2,1)S(1)}, u32[]{:S(2)}, u32[]{:S(2)}) %collective-permute-start.29) | collective-permute-done | bytes 98336 | tf_op jit(solution)/shard_map/ppermute | solution.py:480
  68.2 1.0 %shard_map.79 = (f32[32,3072]{1,0:T(8,128)}, f32[32,3072]{1,0:T(8,128)}) custom-call(f32[32,1536]{1,0:T(8,128)S(1)} %get-tuple-element.73.first_updated, f32[32,1536]{1,0:T(8,128)S(1)} %get-tuple-element.74.first_weights, f32[32,128]{1,0:T(8,128)S(1)} %get-tuple-element.75.first_power, f32[32,3072]{1,0:T(8,128)S(1)} %copy-done, ...), custom_call_target="tpu_custom_call" | custom-call | tf_op jit(solution)/shard_map/pallas_call | solution.py:459
  (44 shorter events, 8.7 us)
Async XLA Ops:
  4.5 4.1 %collective-permute-start = (bf16[3,16,256]{2,1,0:T(8,128)(2,1)S(1)}, bf16[3,16,256]{2,1,0:T(8,128)(2,1)S(1)}, u32[]{:S(2)}, u32[]{:S(2)}) collective-permute-start(bf16[3,16,256]{2,1,0:T(8,128)(2,1)S(1)} %get-tuple-element.45), channel_id=1, source_target_pairs={{0,1},{1,0},{2,3},{3,2},{4,5},{5,4},{6,7},{7,6},{8,9},{9,8},{10,11... | collective-permute-start | bytes 73736 | tf_op jit(solution)/shard_map/ppermute | solution.py:487
  5.0 5.1 %collective-permute-start.1 = (bf16[3,16,256]{2,1,0:T(8,128)(2,1)S(1)}, bf16[3,16,256]{2,1,0:T(8,128)(2,1)S(1)}, u32[]{:S(2)}, u32[]{:S(2)}) collective-permute-start(bf16[3,16,256]{2,1,0:T(8,128)(2,1)S(1)} %get-tuple-element.46), channel_id=1, source_target_pairs={{0,7},{1,2},{2,1},{3,4},{4,3},{5,6},{6,5},{7,0},{8,15},{9,10},{10,... | collective-permute-start | bytes 73736 | tf_op jit(solution)/shard_map/ppermute | solution.py:488
  10.2 6.1 %collective-permute-start.2 = (bf16[64,256]{1,0:T(8,128)(2,1)S(1)}, bf16[64,256]{1,0:T(8,128)(2,1)S(1)}, u32[]{:S(2)}, u32[]{:S(2)}) collective-permute-start(bf16[64,256]{1,0:T(8,128)(2,1)S(1)} %get-tuple-element.48), channel_id=1, source_target_pairs={{0,8},{8,0},{16,24},{24,16},{1,9},{9,1},{17,25},{25,17},{2,10},{10... | collective-permute-start | bytes 98312 | tf_op jit(solution)/shard_map/ppermute | solution.py:483
  12.0 5.7 %collective-permute-start.3 = (bf16[64,256]{1,0:T(8,128)(2,1)S(1)}, bf16[64,256]{1,0:T(8,128)(2,1)S(1)}, u32[]{:S(2)}, u32[]{:S(2)}) collective-permute-start(bf16[64,256]{1,0:T(8,128)(2,1)S(1)} %get-tuple-element.49), channel_id=1, source_target_pairs={{0,24},{8,16},{16,8},{24,0},{1,25},{9,17},{17,9},{25,1},{2,26},{10... | collective-permute-start | bytes 98312 | tf_op jit(solution)/shard_map/ppermute | solution.py:483
  20.4 2.1 %collective-permute-start.4 = (bf16[3,16,256]{2,1,0:T(8,128)(2,1)S(1)}, bf16[3,16,256]{2,1,0:T(8,128)(2,1)S(1)}, u32[]{:S(2)}, u32[]{:S(2)}) collective-permute-start(bf16[3,16,256]{2,1,0:T(8,128)(2,1)S(1)} %get-tuple-element.54), channel_id=1, source_target_pairs={{0,1},{1,0},{2,3},{3,2},{4,5},{5,4},{6,7},{7,6},{8,9},{9,8},{10,11... | collective-permute-start | bytes 73736 | tf_op jit(solution)/shard_map/ppermute | solution.py:487
  20.4 4.2 %collective-permute-start.5 = (bf16[3,16,256]{2,1,0:T(8,128)(2,1)S(1)}, bf16[3,16,256]{2,1,0:T(8,128)(2,1)S(1)}, u32[]{:S(2)}, u32[]{:S(2)}) collective-permute-start(bf16[3,16,256]{2,1,0:T(8,128)(2,1)S(1)} %get-tuple-element.55), channel_id=1, source_target_pairs={{0,7},{1,2},{2,1},{3,4},{4,3},{5,6},{6,5},{7,0},{8,15},{9,10},{10,... | collective-permute-start | bytes 73736 | tf_op jit(solution)/shard_map/ppermute | solution.py:488
  24.7 4.0 %collective-permute-start.6 = (bf16[64,256]{1,0:T(8,128)(2,1)S(1)}, bf16[64,256]{1,0:T(8,128)(2,1)S(1)}, u32[]{:S(2)}, u32[]{:S(2)}) collective-permute-start(bf16[64,256]{1,0:T(8,128)(2,1)S(1)} %get-tuple-element.57), channel_id=1, source_target_pairs={{0,8},{8,0},{16,24},{24,16},{1,9},{9,1},{17,25},{25,17},{2,10},{10... | collective-permute-start | bytes 98312 | tf_op jit(solution)/shard_map/ppermute | solution.py:483
  24.8 5.8 %collective-permute-start.7 = (bf16[64,256]{1,0:T(8,128)(2,1)S(1)}, bf16[64,256]{1,0:T(8,128)(2,1)S(1)}, u32[]{:S(2)}, u32[]{:S(2)}) collective-permute-start(bf16[64,256]{1,0:T(8,128)(2,1)S(1)} %get-tuple-element.58), channel_id=1, source_target_pairs={{0,24},{8,16},{16,8},{24,0},{1,25},{9,17},{17,9},{25,1},{2,26},{10... | collective-permute-start | bytes 98312 | tf_op jit(solution)/shard_map/ppermute | solution.py:483
  30.6 34.4 %copy-start = (f32[32,3072]{1,0:T(8,128)S(1)}, f32[32,3072]{1,0:T(8,128)}, u32[]{:S(2)}) copy-start(f32[32,3072]{1,0:T(8,128)} %momentum.3) | copy-start | bytes 1179652
  33.2 1.4 %collective-permute-start.8 = (bf16[3,16,256]{2,1,0:T(8,128)(2,1)S(1)}, bf16[3,16,256]{2,1,0:T(8,128)(2,1)S(1)}, u32[]{:S(2)}, u32[]{:S(2)}) collective-permute-start(bf16[3,16,256]{2,1,0:T(8,128)(2,1)S(1)} %get-tuple-element.62), channel_id=1, source_target_pairs={{0,1},{1,0},{2,3},{3,2},{4,5},{5,4},{6,7},{7,6},{8,9},{9,8},{10,11... | collective-permute-start | bytes 73736 | tf_op jit(solution)/shard_map/ppermute | solution.py:487
  33.3 4.2 %collective-permute-start.16 = (bf16[3,16,256]{2,1,0:T(8,128)(2,1)S(1)}, bf16[3,16,256]{2,1,0:T(8,128)(2,1)S(1)}, u32[]{:S(2)}, u32[]{:S(2)}) collective-permute-start(bf16[3,16,256]{2,1,0:T(8,128)(2,1)S(1)} %get-tuple-element.68), channel_id=1, source_target_pairs={{0,7},{1,2},{2,1},{3,4},{4,3},{5,6},{6,5},{7,0},{8,15},{9,10},{10,... | collective-permute-start | bytes 73736 | tf_op jit(solution)/shard_map/ppermute | solution.py:488
  37.9 9.1 %collective-permute-start.18 = (bf16[336,128]{1,0:T(8,128)(2,1)S(1)}, bf16[336,128]{1,0:T(8,128)(2,1)S(1)}, u32[]{:S(2)}, u32[]{:S(2)}) collective-permute-start(bf16[336,128]{1,0:T(8,128)(2,1)S(1)} %shard_map.75.rest_0_), channel_id=1, source_target_pairs={{0,16},{8,24},{16,0},{24,8},{1,17},{9,25},{17,1},{25,9},{2,18},{10... | collective-permute-start | bytes 258056 | tf_op jit(solution)/shard_map/ppermute | solution.py:480
  39.3 7.7 %collective-permute-start.9 = (bf16[2,128,128]{2,1,0:T(8,128)(2,1)S(1)}, bf16[2,128,128]{2,1,0:T(8,128)(2,1)S(1)}, u32[]{:S(2)}, u32[]{:S(2)}) collective-permute-start(bf16[2,128,128]{2,1,0:T(8,128)(2,1)S(1)} %get-tuple-element.64), channel_id=1, source_target_pairs={{0,8},{8,0},{16,24},{24,16},{1,9},{9,1},{17,25},{25,17},{2,10},{10... | collective-permute-start | bytes 196616 | tf_op jit(solution)/shard_map/ppermute | solution.py:480
  41.3 7.8 %collective-permute-start.10 = (bf16[2,128,128]{2,1,0:T(8,128)(2,1)S(1)}, bf16[2,128,128]{2,1,0:T(8,128)(2,1)S(1)}, u32[]{:S(2)}, u32[]{:S(2)}) collective-permute-start(bf16[2,128,128]{2,1,0:T(8,128)(2,1)S(1)} %get-tuple-element.65), channel_id=1, source_target_pairs={{0,16},{8,24},{16,0},{24,8},{1,17},{9,25},{17,1},{25,9},{2,18},{10... | collective-permute-start | bytes 196616 | tf_op jit(solution)/shard_map/ppermute | solution.py:480
  41.3 7.8 %collective-permute-start.11 = (bf16[2,128,128]{2,1,0:T(8,128)(2,1)S(1)}, bf16[2,128,128]{2,1,0:T(8,128)(2,1)S(1)}, u32[]{:S(2)}, u32[]{:S(2)}) collective-permute-start(bf16[2,128,128]{2,1,0:T(8,128)(2,1)S(1)} %get-tuple-element.66), channel_id=1, source_target_pairs={{0,24},{8,16},{16,8},{24,0},{1,25},{9,17},{17,9},{25,1},{2,26},{10... | collective-permute-start | bytes 196616 | tf_op jit(solution)/shard_map/ppermute | solution.py:480
  43.8 7.0 %collective-permute-start.17 = (bf16[336,128]{1,0:T(8,128)(2,1)S(1)}, bf16[336,128]{1,0:T(8,128)(2,1)S(1)}, u32[]{:S(2)}, u32[]{:S(2)}) collective-permute-start(bf16[336,128]{1,0:T(8,128)(2,1)S(1)} %shard_map.75.rest_0_), channel_id=1, source_target_pairs={{0,8},{8,0},{16,24},{24,16},{1,9},{9,1},{17,25},{25,17},{2,10},{10... | collective-permute-start | bytes 258056 | tf_op jit(solution)/shard_map/ppermute | solution.py:480
  47.0 5.0 %collective-permute-start.19 = (bf16[336,128]{1,0:T(8,128)(2,1)S(1)}, bf16[336,128]{1,0:T(8,128)(2,1)S(1)}, u32[]{:S(2)}, u32[]{:S(2)}) collective-permute-start(bf16[336,128]{1,0:T(8,128)(2,1)S(1)} %collective-permute-done.18.rest_2_), channel_id=1, source_target_pairs={{0,8},{8,0},{16,24},{24,16},{1,9},{9,1},{17,25},{25,17},{2,10},{10... | collective-permute-start | bytes 258056 | tf_op jit(solution)/shard_map/ppermute | solution.py:480
  47.0 2.6 %collective-permute-start.12 = (bf16[2,128,128]{2,1,0:T(8,128)(2,1)S(1)}, bf16[2,128,128]{2,1,0:T(8,128)(2,1)S(1)}, u32[]{:S(2)}, u32[]{:S(2)}) collective-permute-start(bf16[2,128,128]{2,1,0:T(8,128)(2,1)S(1)} %get-tuple-element.63.rest_0_), channel_id=1, source_target_pairs={{0,1},{1,0},{2,3},{3,2},{4,5},{5,4},{6,7},{7,6},{8,9},{9,8},{10,11... | collective-permute-start | bytes 196616 | tf_op jit(solution)/shard_map/ppermute | solution.py:480
  49.1 1.8 %collective-permute-start.13 = (bf16[2,128,128]{2,1,0:T(8,128)(2,1)S(1)}, bf16[2,128,128]{2,1,0:T(8,128)(2,1)S(1)}, u32[]{:S(2)}, u32[]{:S(2)}) collective-permute-start(bf16[2,128,128]{2,1,0:T(8,128)(2,1)S(1)} %collective-permute-done.9.rest_1_), channel_id=1, source_target_pairs={{0,1},{1,0},{2,3},{3,2},{4,5},{5,4},{6,7},{7,6},{8,9},{9,8},{10,11... | collective-permute-start | bytes 196616 | tf_op jit(solution)/shard_map/ppermute | solution.py:480
  49.1 2.9 %collective-permute-start.14 = (bf16[2,128,128]{2,1,0:T(8,128)(2,1)S(1)}, bf16[2,128,128]{2,1,0:T(8,128)(2,1)S(1)}, u32[]{:S(2)}, u32[]{:S(2)}) collective-permute-start(bf16[2,128,128]{2,1,0:T(8,128)(2,1)S(1)} %collective-permute-done.10.rest_2_), channel_id=1, source_target_pairs={{0,1},{1,0},{2,3},{3,2},{4,5},{5,4},{6,7},{7,6},{8,9},{9,8},{10,11... | collective-permute-start | bytes 196616 | tf_op jit(solution)/shard_map/ppermute | solution.py:480
  49.6 4.0 %collective-permute-start.20 = (bf16[336,128]{1,0:T(8,128)(2,1)S(1)}, bf16[336,128]{1,0:T(8,128)(2,1)S(1)}, u32[]{:S(2)}, u32[]{:S(2)}) collective-permute-start(bf16[336,128]{1,0:T(8,128)(2,1)S(1)} %shard_map.75.rest_0_), channel_id=1, source_target_pairs={{0,1},{1,0},{2,3},{3,2},{4,5},{5,4},{6,7},{7,6},{8,9},{9,8},{10,11... | collective-permute-start | bytes 258056 | tf_op jit(solution)/shard_map/ppermute | solution.py:480
  50.8 2.8 %collective-permute-start.22 = (bf16[336,128]{1,0:T(8,128)(2,1)S(1)}, bf16[336,128]{1,0:T(8,128)(2,1)S(1)}, u32[]{:S(2)}, u32[]{:S(2)}) collective-permute-start(bf16[336,128]{1,0:T(8,128)(2,1)S(1)} %collective-permute-done.18.rest_2_), channel_id=1, source_target_pairs={{0,1},{1,0},{2,3},{3,2},{4,5},{5,4},{6,7},{7,6},{8,9},{9,8},{10,11... | collective-permute-start | bytes 258056 | tf_op jit(solution)/shard_map/ppermute | solution.py:480
  50.8 2.8 %collective-permute-start.21 = (bf16[336,128]{1,0:T(8,128)(2,1)S(1)}, bf16[336,128]{1,0:T(8,128)(2,1)S(1)}, u32[]{:S(2)}, u32[]{:S(2)}) collective-permute-start(bf16[336,128]{1,0:T(8,128)(2,1)S(1)} %collective-permute-done.17.rest_1_), channel_id=1, source_target_pairs={{0,1},{1,0},{2,3},{3,2},{4,5},{5,4},{6,7},{7,6},{8,9},{9,8},{10,11... | collective-permute-start | bytes 258056 | tf_op jit(solution)/shard_map/ppermute | solution.py:480
  52.0 1.7 %collective-permute-start.23 = (bf16[336,128]{1,0:T(8,128)(2,1)S(1)}, bf16[336,128]{1,0:T(8,128)(2,1)S(1)}, u32[]{:S(2)}, u32[]{:S(2)}) collective-permute-start(bf16[336,128]{1,0:T(8,128)(2,1)S(1)} %collective-permute-done.19.rest_3_), channel_id=1, source_target_pairs={{0,1},{1,0},{2,3},{3,2},{4,5},{5,4},{6,7},{7,6},{8,9},{9,8},{10,11... | collective-permute-start | bytes 258056 | tf_op jit(solution)/shard_map/ppermute | solution.py:480
  52.0 1.4 %collective-permute-start.15 = (bf16[2,128,128]{2,1,0:T(8,128)(2,1)S(1)}, bf16[2,128,128]{2,1,0:T(8,128)(2,1)S(1)}, u32[]{:S(2)}, u32[]{:S(2)}) collective-permute-start(bf16[2,128,128]{2,1,0:T(8,128)(2,1)S(1)} %collective-permute-done.11.rest_3_), channel_id=1, source_target_pairs={{0,1},{1,0},{2,3},{3,2},{4,5},{5,4},{6,7},{7,6},{8,9},{9,8},{10,11... | collective-permute-start | bytes 196616 | tf_op jit(solution)/shard_map/ppermute | solution.py:480
  55.6 7.1 %collective-permute-start.24 = (bf16[32,1536]{1,0:T(8,128)(2,1)S(1)}, bf16[32,1536]{1,0:T(8,128)(2,1)S(1)}, u32[]{:S(2)}, u32[]{:S(2)}) collective-permute-start(bf16[32,1536]{1,0:T(8,128)(2,1)S(1)} %get-tuple-element.70), channel_id=1, source_target_pairs={{0,2},{2,0},{4,6},{6,4},{1,3},{3,1},{5,7},{7,5},{8,10},{10,8},{12,... | collective-permute-start | bytes 294920 | tf_op jit(solution)/shard_map/ppermute | solution.py:480
  56.9 7.2 %collective-permute-start.25 = (bf16[32,1536]{1,0:T(8,128)(2,1)S(1)}, bf16[32,1536]{1,0:T(8,128)(2,1)S(1)}, u32[]{:S(2)}, u32[]{:S(2)}) collective-permute-start(bf16[32,1536]{1,0:T(8,128)(2,1)S(1)} %get-tuple-element.71), channel_id=1, source_target_pairs={{0,4},{2,6},{4,0},{6,2},{1,5},{3,7},{5,1},{7,3},{8,12},{10,14},{12... | collective-permute-start | bytes 294920 | tf_op jit(solution)/shard_map/ppermute | solution.py:480
  58.5 6.6 %collective-permute-start.26 = (bf16[32,1536]{1,0:T(8,128)(2,1)S(1)}, bf16[32,1536]{1,0:T(8,128)(2,1)S(1)}, u32[]{:S(2)}, u32[]{:S(2)}) collective-permute-start(bf16[32,1536]{1,0:T(8,128)(2,1)S(1)} %get-tuple-element.72), channel_id=1, source_target_pairs={{0,6},{2,4},{4,2},{6,0},{1,7},{3,5},{5,3},{7,1},{8,14},{10,12},{12... | collective-permute-start | bytes 294920 | tf_op jit(solution)/shard_map/ppermute | solution.py:480
  59.7 6.3 %collective-permute-start.27 = (bf16[32,1536]{1,0:T(8,128)(2,1)S(1)}, bf16[32,1536]{1,0:T(8,128)(2,1)S(1)}, u32[]{:S(2)}, u32[]{:S(2)}) collective-permute-start(bf16[32,1536]{1,0:T(8,128)(2,1)S(1)} %get-tuple-element.78), channel_id=1, source_target_pairs={{0,2},{2,0},{4,6},{6,4},{1,3},{3,1},{5,7},{7,5},{8,10},{10,8},{12,... | collective-permute-start | bytes 294920 | tf_op jit(solution)/shard_map/ppermute | solution.py:480
  61.1 6.0 %collective-permute-start.28 = (bf16[32,1536]{1,0:T(8,128)(2,1)S(1)}, bf16[32,1536]{1,0:T(8,128)(2,1)S(1)}, u32[]{:S(2)}, u32[]{:S(2)}) collective-permute-start(bf16[32,1536]{1,0:T(8,128)(2,1)S(1)} %get-tuple-element.79), channel_id=1, source_target_pairs={{0,4},{2,6},{4,0},{6,2},{1,5},{3,7},{5,1},{7,3},{8,12},{10,14},{12... | collective-permute-start | bytes 294920 | tf_op jit(solution)/shard_map/ppermute | solution.py:480
  62.6 5.6 %collective-permute-start.29 = (bf16[32,1536]{1,0:T(8,128)(2,1)S(1)}, bf16[32,1536]{1,0:T(8,128)(2,1)S(1)}, u32[]{:S(2)}, u32[]{:S(2)}) collective-permute-start(bf16[32,1536]{1,0:T(8,128)(2,1)S(1)} %get-tuple-element.80), channel_id=1, source_target_pairs={{0,6},{2,4},{4,2},{6,0},{1,7},{3,5},{5,3},{7,1},{8,14},{10,12},{12... | collective-permute-start | bytes 294920 | tf_op jit(solution)/shard_map/ppermute | solution.py:480

commit v7 on v6

--- a/solution.py
+++ b/solution.py
@@ -571,13 +571,7 @@
         [own_v, flat_v],
     )
 
-    near = [packed]
-    for x in range(1, rows_n):
-        low = x & -x
-        if power:
-            near.append(met(near[x - low], "row", rows_n, low))
-        else:
-            near.append(met(packed, "row", rows_n, rows_n - x))
+    near = along_row([packed] * rows_n)
     far = across_chip(near)
     stride = members * z.cols
     group_atoms = atom_count // members

time: 69.5 us -> 70.5 us (1.014)
  starting transfers between devices: 29.8 us -> 30.9 us
    ppermute x20, starting transfers between devices: 15.4 us -> 17.7 us  [met(): lax.ppermute(block, axis, [(i, offset(i, step, n)) for i in range(n)])]
    ppermute x20, waiting for transfers between devices: 10.9 us -> 8.65 us  [met(): lax.ppermute(block, axis, [(i, offset(i, step, n)) for i in range(n)])]
    ppermute x3, waiting for transfers between devices: 0.01 us -> 1.19 us  [sideways(): near_rim = lax.ppermute(blocks[0], ('yx', 'core'), even)]
    ppermute x3, starting transfers between devices: 6.82 us -> 5.65 us  [sideways(): far_rim = lax.ppermute(blocks[1], ('yx', 'core'), odd)]
    ppermute x3, waiting for transfers between devices: 6.67 us -> 7.61 us  [sideways(): far_rim = lax.ppermute(blocks[1], ('yx', 'core'), odd)]
  transfers between devices with their start and end apart: 30 -> 30, of which waited for: 15 -> 13; matrix products, arithmetic and copies ran while one was open for 1% -> 1% of each run, Pallas kernels for 4% -> 4%
where the time goes in v7:
time: 70.5 us; the launch traced here: 70.4 us
  starting transfers between devices  30.9 us (44%)
  waiting for transfers between devices  22.1 us (31%)
  Pallas kernels  15.6 us (22%)
  between operations  0.96 us (1%)
  local copies, waits for them, and re-layouts  0.8 us (1%)
    ppermute x20, starting transfers between devices, met(): lax.ppermute(block, axis, [(i, offset(i, step, n)) for i in range(n)])  17.7 us
    pallas_call x13, Pallas kernels, call(): pl.pallas_call(kernel, out_shape=outs, in_specs=specs, out_specs=[leave]...  15.6 us
    ppermute x20, waiting for transfers between devices, met(): lax.ppermute(block, axis, [(i, offset(i, step, n)) for i in range(n)])  8.65 us
    ppermute x3, waiting for transfers between devices, sideways(): far_rim = lax.ppermute(blocks[1], ('yx', 'core'), odd)  7.61 us
    ppermute x4, starting transfers between devices, swapped(): lax.ppermute(b, axis, route)  6.86 us
    ppermute x3, starting transfers between devices, sideways(): far_rim = lax.ppermute(blocks[1], ('yx', 'core'), odd)  5.65 us
    ppermute x4, waiting for transfers between devices, swapped(): lax.ppermute(b, axis, route)  4.64 us
  transfers between devices with their start and end apart: 30, of which 13 were waited for; matrix products, arithmetic and copies ran while one was open for 1% of the time, Pallas kernels for 4%

profile of v7, /device:TPU:0, one launch (start us, length us, event | category | flops | bytes accessed | tf_op | source)
XLA Modules:
  0.0 70.4 jit_solution(18142559557271487202)
XLA Ops:
  0.6 3.8 %shard_map.67 = (f32[11,24,256]{2,1,0:T(8,128)S(1)}, bf16[3,16,256]{2,1,0:T(8,128)(2,1)S(1)}, bf16[3,16,256]{2,1,0:T(8,128)(2,1)S(1)}, f32[128,192]{1,0:T(8,128)...) custom-call(f32[128,1024]{1,0:T(8,128)} %bitcast.3, ...), custom_call_target="tpu_custom_call" | custom-call | tf_op jit(solution)/shard_map/pallas_call | solution.py:459
  5.0 3.5 %collective-permute-start.1 = (bf16[3,16,256]{2,1,0:T(8,128)(2,1)S(1)}, bf16[3,16,256]{2,1,0:T(8,128)(2,1)S(1)}, u32[]{:S(2)}, u32[]{:S(2)}) collective-permute-start(bf16[3,16,256]{2,1,0:T(8,128)(2,1)S(1)} %get-tuple-element.46), channel_id=1, source_target_pairs={{0,7},{1,2},{2,1},{3,4},{4,3},{5,6},{6,5},{7,0},{8,15},{9,10},{10,... | collective-permute-start | bytes 73736 | tf_op jit(solution)/shard_map/ppermute | solution.py:488
  8.6 1.5 %collective-permute-done.1.from_odd = bf16[3,16,256]{2,1,0:T(8,128)(2,1)S(1)} collective-permute-done((bf16[3,16,256]{2,1,0:T(8,128)(2,1)S(1)}, bf16[3,16,256]{2,1,0:T(8,128)(2,1)S(1)}, u32[]{:S(2)}, u32[]{:S(2)}) %collective-permute-start.1) | collective-permute-done | bytes 24608 | tf_op jit(solution)/shard_map/ppermute | solution.py:488
  10.2 1.8 %collective-permute-start.2 = (bf16[64,256]{1,0:T(8,128)(2,1)S(1)}, bf16[64,256]{1,0:T(8,128)(2,1)S(1)}, u32[]{:S(2)}, u32[]{:S(2)}) collective-permute-start(bf16[64,256]{1,0:T(8,128)(2,1)S(1)} %get-tuple-element.48), channel_id=1, source_target_pairs={{0,8},{8,0},{16,24},{24,16},{1,9},{9,1},{17,25},{25,17},{2,10},{10... | collective-permute-start | bytes 98312 | tf_op jit(solution)/shard_map/ppermute | solution.py:483
  12.0 2.5 %collective-permute-start.3 = (bf16[64,256]{1,0:T(8,128)(2,1)S(1)}, bf16[64,256]{1,0:T(8,128)(2,1)S(1)}, u32[]{:S(2)}, u32[]{:S(2)}) collective-permute-start(bf16[64,256]{1,0:T(8,128)(2,1)S(1)} %get-tuple-element.49), channel_id=1, source_target_pairs={{0,24},{8,16},{16,8},{24,0},{1,25},{9,17},{17,9},{25,1},{2,26},{10... | collective-permute-start | bytes 98312 | tf_op jit(solution)/shard_map/ppermute | solution.py:483
  14.5 1.8 %shard_map.69.turned = bf16[3072,1024]{1,0:T(8,128)(2,1)S(1)} custom-call(bf16[1024,3072]{1,0:T(8,128)(2,1)S(1)} %get-tuple-element.51.dic), custom_call_target="tpu_custom_call" | custom-call | tf_op jit(solution)/shard_map/pallas_call | solution.py:459
  16.3 1.4 %collective-permute-done.3.from_odd = bf16[64,256]{1,0:T(8,128)(2,1)S(1)} collective-permute-done((bf16[64,256]{1,0:T(8,128)(2,1)S(1)}, bf16[64,256]{1,0:T(8,128)(2,1)S(1)}, u32[]{:S(2)}, u32[]{:S(2)}) %collective-permute-start.3) | collective-permute-done | bytes 32800 | tf_op jit(solution)/shard_map/ppermute | solution.py:483
  17.7 2.6 %shard_map.70 = (f32[128,1024]{1,0:T(8,128)S(1)}, f32[11,24,256]{2,1,0:T(8,128)S(1)}, bf16[3,16,256]{2,1,0:T(8,128)(2,1)S(1)}, bf16[3,16,256]{2,1,0:T(8,128)(2,1)S(1)}) custom-call(f32[128,1024]{1,0:T(8,128)S(1)} %get-tuple-element.43.potential, f32[11,24,256]{2,1,0:T(8,128)S(1)} %get-tuple-element.47.joined, ...), custom_call_target="tpu_custom_call" | custom-call | tf_op jit(solution)/shard_map/pallas_call | solution.py:459
  20.4 2.0 %collective-permute-start.5 = (bf16[3,16,256]{2,1,0:T(8,128)(2,1)S(1)}, bf16[3,16,256]{2,1,0:T(8,128)(2,1)S(1)}, u32[]{:S(2)}, u32[]{:S(2)}) collective-permute-start(bf16[3,16,256]{2,1,0:T(8,128)(2,1)S(1)} %get-tuple-element.55), channel_id=1, source_target_pairs={{0,7},{1,2},{2,1},{3,4},{4,3},{5,6},{6,5},{7,0},{8,15},{9,10},{10,... | collective-permute-start | bytes 73736 | tf_op jit(solution)/shard_map/ppermute | solution.py:488
  22.4 2.2 %collective-permute-done.5.from_odd = bf16[3,16,256]{2,1,0:T(8,128)(2,1)S(1)} collective-permute-done((bf16[3,16,256]{2,1,0:T(8,128)(2,1)S(1)}, bf16[3,16,256]{2,1,0:T(8,128)(2,1)S(1)}, u32[]{:S(2)}, u32[]{:S(2)}) %collective-permute-start.5) | collective-permute-done | bytes 24608 | tf_op jit(solution)/shard_map/ppermute | solution.py:488
  24.8 2.5 %collective-permute-start.7 = (bf16[64,256]{1,0:T(8,128)(2,1)S(1)}, bf16[64,256]{1,0:T(8,128)(2,1)S(1)}, u32[]{:S(2)}, u32[]{:S(2)}) collective-permute-start(bf16[64,256]{1,0:T(8,128)(2,1)S(1)} %get-tuple-element.58), channel_id=1, source_target_pairs={{0,24},{8,16},{16,8},{24,0},{1,25},{9,17},{17,9},{25,1},{2,26},{10... | collective-permute-start | bytes 98312 | tf_op jit(solution)/shard_map/ppermute | solution.py:483
  27.3 1.4 %collective-permute-done.6.from_even = bf16[64,256]{1,0:T(8,128)(2,1)S(1)} collective-permute-done((bf16[64,256]{1,0:T(8,128)(2,1)S(1)}, bf16[64,256]{1,0:T(8,128)(2,1)S(1)}, u32[]{:S(2)}, u32[]{:S(2)}) %collective-permute-start.6) | collective-permute-done | bytes 32800 | tf_op jit(solution)/shard_map/ppermute | solution.py:483
  28.7 1.9 %collective-permute-done.7.from_odd = bf16[64,256]{1,0:T(8,128)(2,1)S(1)} collective-permute-done((bf16[64,256]{1,0:T(8,128)(2,1)S(1)}, bf16[64,256]{1,0:T(8,128)(2,1)S(1)}, u32[]{:S(2)}, u32[]{:S(2)}) %collective-permute-start.7) | collective-permute-done | bytes 32800 | tf_op jit(solution)/shard_map/ppermute | solution.py:483
  30.6 2.6 %shard_map.72 = (f32[128,1024]{1,0:T(8,128)S(1)}, f32[11,24,256]{2,1,0:T(8,128)S(1)}, bf16[3,16,256]{2,1,0:T(8,128)(2,1)S(1)}, bf16[3,16,256]{2,1,0:T(8,128)(2,1)S(1)}, bf16[128,1024]{1,0:T(8,128)(2,1)S(1)}) custom-call(f32[128,1024]{1,0:T(8,128)S(1)} %get-tuple-element.52.potential, f32[11,24,256]{2,1,0:T(8,128)S(1)} %get-tuple-element.56.joined, ...), custom_call_target="tpu_custom_call" | custom-call | tf_op jit(solution)/shard_map/pallas_call | solution.py:459
  33.3 1.2 %collective-permute-done.8._.from_even = bf16[3,16,256]{2,1,0:T(8,128)(2,1)S(1)} collective-permute-done((bf16[3,16,256]{2,1,0:T(8,128)(2,1)S(1)}, bf16[3,16,256]{2,1,0:T(8,128)(2,1)S(1)}, u32[]{:S(2)}, u32[]{:S(2)}) %collective-permute-start.8) | collective-permute-done | bytes 24608 | tf_op jit(solution)/shard_map/ppermute | solution.py:487
  35.0 2.9 %collective-permute-start.10 = (bf16[2,128,128]{2,1,0:T(8,128)(2,1)S(1)}, bf16[2,128,128]{2,1,0:T(8,128)(2,1)S(1)}, u32[]{:S(2)}, u32[]{:S(2)}) collective-permute-start(bf16[2,128,128]{2,1,0:T(8,128)(2,1)S(1)} %get-tuple-element.65), channel_id=1, source_target_pairs={{0,16},{8,24},{16,0},{24,8},{1,17},{9,25},{17,1},{25,9},{2,18},{10... | collective-permute-start | bytes 196616 | tf_op jit(solution)/shard_map/ppermute | solution.py:480
  37.8 1.4 %collective-permute-start.11 = (bf16[2,128,128]{2,1,0:T(8,128)(2,1)S(1)}, bf16[2,128,128]{2,1,0:T(8,128)(2,1)S(1)}, u32[]{:S(2)}, u32[]{:S(2)}) collective-permute-start(bf16[2,128,128]{2,1,0:T(8,128)(2,1)S(1)} %get-tuple-element.66), channel_id=1, source_target_pairs={{0,24},{8,16},{16,8},{24,0},{1,25},{9,17},{17,9},{25,1},{2,26},{10... | collective-permute-start | bytes 196616 | tf_op jit(solution)/shard_map/ppermute | solution.py:480
  39.5 3.9 %collective-permute-done.16.from_odd = bf16[3,16,256]{2,1,0:T(8,128)(2,1)S(1)} collective-permute-done((bf16[3,16,256]{2,1,0:T(8,128)(2,1)S(1)}, bf16[3,16,256]{2,1,0:T(8,128)(2,1)S(1)}, u32[]{:S(2)}, u32[]{:S(2)}) %collective-permute-start.16) | collective-permute-done | bytes 24608 | tf_op jit(solution)/shard_map/ppermute | solution.py:488
  43.7 2.5 %collective-permute-start.19 = (bf16[336,128]{1,0:T(8,128)(2,1)S(1)}, bf16[336,128]{1,0:T(8,128)(2,1)S(1)}, u32[]{:S(2)}, u32[]{:S(2)}) collective-permute-start(bf16[336,128]{1,0:T(8,128)(2,1)S(1)} %shard_map.75.rest_0_), channel_id=1, source_target_pairs={{0,24},{8,16},{16,8},{24,0},{1,25},{9,17},{17,9},{25,1},{2,26},{10... | collective-permute-start | bytes 258056 | tf_op jit(solution)/shard_map/ppermute | solution.py:480
  46.2 1.9 %collective-permute-start.17 = (bf16[336,128]{1,0:T(8,128)(2,1)S(1)}, bf16[336,128]{1,0:T(8,128)(2,1)S(1)}, u32[]{:S(2)}, u32[]{:S(2)}) collective-permute-start(bf16[336,128]{1,0:T(8,128)(2,1)S(1)} %shard_map.75.rest_0_), channel_id=1, source_target_pairs={{0,8},{8,0},{16,24},{24,16},{1,9},{9,1},{17,25},{25,17},{2,10},{10... | collective-permute-start | bytes 258056 | tf_op jit(solution)/shard_map/ppermute | solution.py:480
  48.7 2.1 %collective-permute-done.19.rest_3_ = bf16[336,128]{1,0:T(8,128)(2,1)S(1)} collective-permute-done((bf16[336,128]{1,0:T(8,128)(2,1)S(1)}, bf16[336,128]{1,0:T(8,128)(2,1)S(1)}, u32[]{:S(2)}, u32[]{:S(2)}) %collective-permute-start.19) | collective-permute-done | bytes 86048 | tf_op jit(solution)/shard_map/ppermute | solution.py:480
  50.8 1.8 %collective-permute-done.18.rest_2_ = bf16[336,128]{1,0:T(8,128)(2,1)S(1)} collective-permute-done((bf16[336,128]{1,0:T(8,128)(2,1)S(1)}, bf16[336,128]{1,0:T(8,128)(2,1)S(1)}, u32[]{:S(2)}, u32[]{:S(2)}) %collective-permute-start.18) | collective-permute-done | bytes 86048 | tf_op jit(solution)/shard_map/ppermute | solution.py:480
  54.8 1.9 %shard_map.76 = (bf16[32,1536]{1,0:T(8,128)(2,1)S(1)}, bf16[32,1536]{1,0:T(8,128)(2,1)S(1)}, bf16[32,1536]{1,0:T(8,128)(2,1)S(1)}, bf16[32,1536]{1,0:T(8,128)(2,1)S(1)}, bf16[1408,768]{1,0:T(8,128)(2,1)S(1)}) custom-call(bf16[128,1024]{1,0:T(8,128)(2,1)S(1)} %shard_map.74.across, bf16[336,128]{1,0:T(8,128)(2,1)S(1)} %shard_map.75.rest_0_, ...), custom_call_target="tpu_custom_call" | custom-call | tf_op jit(solution)/shard_map/pallas_call | solution.py:459
  56.7 1.4 %collective-permute-start.24 = (bf16[32,1536]{1,0:T(8,128)(2,1)S(1)}, bf16[32,1536]{1,0:T(8,128)(2,1)S(1)}, u32[]{:S(2)}, u32[]{:S(2)}) collective-permute-start(bf16[32,1536]{1,0:T(8,128)(2,1)S(1)} %get-tuple-element.70), channel_id=1, source_target_pairs={{0,2},{2,0},{4,6},{6,4},{1,3},{3,1},{5,7},{7,5},{8,10},{10,8},{12,... | collective-permute-start | bytes 294920 | tf_op jit(solution)/shard_map/ppermute | solution.py:480
  58.1 1.1 %collective-permute-start.25 = (bf16[32,1536]{1,0:T(8,128)(2,1)S(1)}, bf16[32,1536]{1,0:T(8,128)(2,1)S(1)}, u32[]{:S(2)}, u32[]{:S(2)}) collective-permute-start(bf16[32,1536]{1,0:T(8,128)(2,1)S(1)} %get-tuple-element.71), channel_id=1, source_target_pairs={{0,4},{2,6},{4,0},{6,2},{1,5},{3,7},{5,1},{7,3},{8,12},{10,14},{12... | collective-permute-start | bytes 294920 | tf_op jit(solution)/shard_map/ppermute | solution.py:480
  59.2 1.0 %collective-permute-start.26 = (bf16[32,1536]{1,0:T(8,128)(2,1)S(1)}, bf16[32,1536]{1,0:T(8,128)(2,1)S(1)}, u32[]{:S(2)}, u32[]{:S(2)}) collective-permute-start(bf16[32,1536]{1,0:T(8,128)(2,1)S(1)} %get-tuple-element.72), channel_id=1, source_target_pairs={{0,6},{2,4},{4,2},{6,0},{1,7},{3,5},{5,3},{7,1},{8,14},{10,12},{12... | collective-permute-start | bytes 294920 | tf_op jit(solution)/shard_map/ppermute | solution.py:480
  60.9 1.4 %collective-permute-start.27 = (bf16[32,1536]{1,0:T(8,128)(2,1)S(1)}, bf16[32,1536]{1,0:T(8,128)(2,1)S(1)}, u32[]{:S(2)}, u32[]{:S(2)}) collective-permute-start(bf16[32,1536]{1,0:T(8,128)(2,1)S(1)} %get-tuple-element.78), channel_id=1, source_target_pairs={{0,2},{2,0},{4,6},{6,4},{1,3},{3,1},{5,7},{7,5},{8,10},{10,8},{12,... | collective-permute-start | bytes 294920 | tf_op jit(solution)/shard_map/ppermute | solution.py:480
  62.3 1.1 %collective-permute-start.28 = (bf16[32,1536]{1,0:T(8,128)(2,1)S(1)}, bf16[32,1536]{1,0:T(8,128)(2,1)S(1)}, u32[]{:S(2)}, u32[]{:S(2)}) collective-permute-start(bf16[32,1536]{1,0:T(8,128)(2,1)S(1)} %get-tuple-element.79), channel_id=1, source_target_pairs={{0,4},{2,6},{4,0},{6,2},{1,5},{3,7},{5,1},{7,3},{8,12},{10,14},{12... | collective-permute-start | bytes 294920 | tf_op jit(solution)/shard_map/ppermute | solution.py:480
  63.4 1.0 %collective-permute-start.29 = (bf16[32,1536]{1,0:T(8,128)(2,1)S(1)}, bf16[32,1536]{1,0:T(8,128)(2,1)S(1)}, u32[]{:S(2)}, u32[]{:S(2)}) collective-permute-start(bf16[32,1536]{1,0:T(8,128)(2,1)S(1)} %get-tuple-element.80), channel_id=1, source_target_pairs={{0,6},{2,4},{4,2},{6,0},{1,7},{3,5},{5,3},{7,1},{8,14},{10,12},{12... | collective-permute-start | bytes 294920 | tf_op jit(solution)/shard_map/ppermute | solution.py:480
  66.0 1.2 %collective-permute-done.27.rest_1_ = bf16[32,1536]{1,0:T(8,128)(2,1)S(1)} collective-permute-done((bf16[32,1536]{1,0:T(8,128)(2,1)S(1)}, bf16[32,1536]{1,0:T(8,128)(2,1)S(1)}, u32[]{:S(2)}, u32[]{:S(2)}) %collective-permute-start.27) | collective-permute-done | bytes 98336 | tf_op jit(solution)/shard_map/ppermute | solution.py:480
  67.1 2.1 %collective-permute-done.28.rest_2_ = bf16[32,1536]{1,0:T(8,128)(2,1)S(1)} collective-permute-done((bf16[32,1536]{1,0:T(8,128)(2,1)S(1)}, bf16[32,1536]{1,0:T(8,128)(2,1)S(1)}, u32[]{:S(2)}, u32[]{:S(2)}) %collective-permute-start.28) | collective-permute-done | bytes 98336 | tf_op jit(solution)/shard_map/ppermute | solution.py:480
  69.2 1.0 %shard_map.79 = (f32[32,3072]{1,0:T(8,128)}, f32[32,3072]{1,0:T(8,128)}) custom-call(f32[32,1536]{1,0:T(8,128)S(1)} %get-tuple-element.73.first_updated, f32[32,1536]{1,0:T(8,128)S(1)} %get-tuple-element.74.first_weights, f32[32,128]{1,0:T(8,128)S(1)} %get-tuple-element.75.first_power, f32[32,3072]{1,0:T(8,128)S(1)} %copy-done, ...), custom_call_target="tpu_custom_call" | custom-call | tf_op jit(solution)/shard_map/pallas_call | solution.py:459
  (44 shorter events, 6.9 us)
Async XLA Ops:
  4.5 4.1 %collective-permute-start = (bf16[3,16,256]{2,1,0:T(8,128)(2,1)S(1)}, bf16[3,16,256]{2,1,0:T(8,128)(2,1)S(1)}, u32[]{:S(2)}, u32[]{:S(2)}) collective-permute-start(bf16[3,16,256]{2,1,0:T(8,128)(2,1)S(1)} %get-tuple-element.45), channel_id=1, source_target_pairs={{0,1},{1,0},{2,3},{3,2},{4,5},{5,4},{6,7},{7,6},{8,9},{9,8},{10,11... | collective-permute-start | bytes 73736 | tf_op jit(solution)/shard_map/ppermute | solution.py:487
  5.0 5.1 %collective-permute-start.1 = (bf16[3,16,256]{2,1,0:T(8,128)(2,1)S(1)}, bf16[3,16,256]{2,1,0:T(8,128)(2,1)S(1)}, u32[]{:S(2)}, u32[]{:S(2)}) collective-permute-start(bf16[3,16,256]{2,1,0:T(8,128)(2,1)S(1)} %get-tuple-element.46), channel_id=1, source_target_pairs={{0,7},{1,2},{2,1},{3,4},{4,3},{5,6},{6,5},{7,0},{8,15},{9,10},{10,... | collective-permute-start | bytes 73736 | tf_op jit(solution)/shard_map/ppermute | solution.py:488
  10.2 6.1 %collective-permute-start.2 = (bf16[64,256]{1,0:T(8,128)(2,1)S(1)}, bf16[64,256]{1,0:T(8,128)(2,1)S(1)}, u32[]{:S(2)}, u32[]{:S(2)}) collective-permute-start(bf16[64,256]{1,0:T(8,128)(2,1)S(1)} %get-tuple-element.48), channel_id=1, source_target_pairs={{0,8},{8,0},{16,24},{24,16},{1,9},{9,1},{17,25},{25,17},{2,10},{10... | collective-permute-start | bytes 98312 | tf_op jit(solution)/shard_map/ppermute | solution.py:483
  12.0 5.7 %collective-permute-start.3 = (bf16[64,256]{1,0:T(8,128)(2,1)S(1)}, bf16[64,256]{1,0:T(8,128)(2,1)S(1)}, u32[]{:S(2)}, u32[]{:S(2)}) collective-permute-start(bf16[64,256]{1,0:T(8,128)(2,1)S(1)} %get-tuple-element.49), channel_id=1, source_target_pairs={{0,24},{8,16},{16,8},{24,0},{1,25},{9,17},{17,9},{25,1},{2,26},{10... | collective-permute-start | bytes 98312 | tf_op jit(solution)/shard_map/ppermute | solution.py:483
  20.4 2.1 %collective-permute-start.4 = (bf16[3,16,256]{2,1,0:T(8,128)(2,1)S(1)}, bf16[3,16,256]{2,1,0:T(8,128)(2,1)S(1)}, u32[]{:S(2)}, u32[]{:S(2)}) collective-permute-start(bf16[3,16,256]{2,1,0:T(8,128)(2,1)S(1)} %get-tuple-element.54), channel_id=1, source_target_pairs={{0,1},{1,0},{2,3},{3,2},{4,5},{5,4},{6,7},{7,6},{8,9},{9,8},{10,11... | collective-permute-start | bytes 73736 | tf_op jit(solution)/shard_map/ppermute | solution.py:487
  20.4 4.2 %collective-permute-start.5 = (bf16[3,16,256]{2,1,0:T(8,128)(2,1)S(1)}, bf16[3,16,256]{2,1,0:T(8,128)(2,1)S(1)}, u32[]{:S(2)}, u32[]{:S(2)}) collective-permute-start(bf16[3,16,256]{2,1,0:T(8,128)(2,1)S(1)} %get-tuple-element.55), channel_id=1, source_target_pairs={{0,7},{1,2},{2,1},{3,4},{4,3},{5,6},{6,5},{7,0},{8,15},{9,10},{10,... | collective-permute-start | bytes 73736 | tf_op jit(solution)/shard_map/ppermute | solution.py:488
  24.7 4.0 %collective-permute-start.6 = (bf16[64,256]{1,0:T(8,128)(2,1)S(1)}, bf16[64,256]{1,0:T(8,128)(2,1)S(1)}, u32[]{:S(2)}, u32[]{:S(2)}) collective-permute-start(bf16[64,256]{1,0:T(8,128)(2,1)S(1)} %get-tuple-element.57), channel_id=1, source_target_pairs={{0,8},{8,0},{16,24},{24,16},{1,9},{9,1},{17,25},{25,17},{2,10},{10... | collective-permute-start | bytes 98312 | tf_op jit(solution)/shard_map/ppermute | solution.py:483
  24.8 5.8 %collective-permute-start.7 = (bf16[64,256]{1,0:T(8,128)(2,1)S(1)}, bf16[64,256]{1,0:T(8,128)(2,1)S(1)}, u32[]{:S(2)}, u32[]{:S(2)}) collective-permute-start(bf16[64,256]{1,0:T(8,128)(2,1)S(1)} %get-tuple-element.58), channel_id=1, source_target_pairs={{0,24},{8,16},{16,8},{24,0},{1,25},{9,17},{17,9},{25,1},{2,26},{10... | collective-permute-start | bytes 98312 | tf_op jit(solution)/shard_map/ppermute | solution.py:483
  30.6 35.2 %copy-start = (f32[32,3072]{1,0:T(8,128)S(1)}, f32[32,3072]{1,0:T(8,128)}, u32[]{:S(2)}) copy-start(f32[32,3072]{1,0:T(8,128)} %momentum.3) | copy-start | bytes 1179652
  33.3 1.3 %collective-permute-start.8 = (bf16[3,16,256]{2,1,0:T(8,128)(2,1)S(1)}, bf16[3,16,256]{2,1,0:T(8,128)(2,1)S(1)}, u32[]{:S(2)}, u32[]{:S(2)}) collective-permute-start(bf16[3,16,256]{2,1,0:T(8,128)(2,1)S(1)} %get-tuple-element.62), channel_id=1, source_target_pairs={{0,1},{1,0},{2,3},{3,2},{4,5},{5,4},{6,7},{7,6},{8,9},{9,8},{10,11... | collective-permute-start | bytes 73736 | tf_op jit(solution)/shard_map/ppermute | solution.py:487
  34.8 11.5 %collective-permute-start.9 = (bf16[2,128,128]{2,1,0:T(8,128)(2,1)S(1)}, bf16[2,128,128]{2,1,0:T(8,128)(2,1)S(1)}, u32[]{:S(2)}, u32[]{:S(2)}) collective-permute-start(bf16[2,128,128]{2,1,0:T(8,128)(2,1)S(1)} %get-tuple-element.64), channel_id=1, source_target_pairs={{0,8},{8,0},{16,24},{24,16},{1,9},{9,1},{17,25},{25,17},{2,10},{10... | collective-permute-start | bytes 196616 | tf_op jit(solution)/shard_map/ppermute | solution.py:480
  35.0 11.2 %collective-permute-start.10 = (bf16[2,128,128]{2,1,0:T(8,128)(2,1)S(1)}, bf16[2,128,128]{2,1,0:T(8,128)(2,1)S(1)}, u32[]{:S(2)}, u32[]{:S(2)}) collective-permute-start(bf16[2,128,128]{2,1,0:T(8,128)(2,1)S(1)} %get-tuple-element.65), channel_id=1, source_target_pairs={{0,16},{8,24},{16,0},{24,8},{1,17},{9,25},{17,1},{25,9},{2,18},{10... | collective-permute-start | bytes 196616 | tf_op jit(solution)/shard_map/ppermute | solution.py:480
  37.8 10.3 %collective-permute-start.11 = (bf16[2,128,128]{2,1,0:T(8,128)(2,1)S(1)}, bf16[2,128,128]{2,1,0:T(8,128)(2,1)S(1)}, u32[]{:S(2)}, u32[]{:S(2)}) collective-permute-start(bf16[2,128,128]{2,1,0:T(8,128)(2,1)S(1)} %get-tuple-element.66), channel_id=1, source_target_pairs={{0,24},{8,16},{16,8},{24,0},{1,25},{9,17},{17,9},{25,1},{2,26},{10... | collective-permute-start | bytes 196616 | tf_op jit(solution)/shard_map/ppermute | solution.py:480
  39.2 4.2 %collective-permute-start.16 = (bf16[3,16,256]{2,1,0:T(8,128)(2,1)S(1)}, bf16[3,16,256]{2,1,0:T(8,128)(2,1)S(1)}, u32[]{:S(2)}, u32[]{:S(2)}) collective-permute-start(bf16[3,16,256]{2,1,0:T(8,128)(2,1)S(1)} %get-tuple-element.68), channel_id=1, source_target_pairs={{0,7},{1,2},{2,1},{3,4},{4,3},{5,6},{6,5},{7,0},{8,15},{9,10},{10,... | collective-permute-start | bytes 73736 | tf_op jit(solution)/shard_map/ppermute | solution.py:488
  39.3 8.8 %collective-permute-start.12 = (bf16[2,128,128]{2,1,0:T(8,128)(2,1)S(1)}, bf16[2,128,128]{2,1,0:T(8,128)(2,1)S(1)}, u32[]{:S(2)}, u32[]{:S(2)}) collective-permute-start(bf16[2,128,128]{2,1,0:T(8,128)(2,1)S(1)} %get-tuple-element.63.rest_0_), channel_id=1, source_target_pairs={{0,1},{1,0},{2,3},{3,2},{4,5},{5,4},{6,7},{7,6},{8,9},{9,8},{10,11... | collective-permute-start | bytes 196616 | tf_op jit(solution)/shard_map/ppermute | solution.py:480
  43.7 7.1 %collective-permute-start.19 = (bf16[336,128]{1,0:T(8,128)(2,1)S(1)}, bf16[336,128]{1,0:T(8,128)(2,1)S(1)}, u32[]{:S(2)}, u32[]{:S(2)}) collective-permute-start(bf16[336,128]{1,0:T(8,128)(2,1)S(1)} %shard_map.75.rest_0_), channel_id=1, source_target_pairs={{0,24},{8,16},{16,8},{24,0},{1,25},{9,17},{17,9},{25,1},{2,26},{10... | collective-permute-start | bytes 258056 | tf_op jit(solution)/shard_map/ppermute | solution.py:480
  46.2 6.4 %collective-permute-start.18 = (bf16[336,128]{1,0:T(8,128)(2,1)S(1)}, bf16[336,128]{1,0:T(8,128)(2,1)S(1)}, u32[]{:S(2)}, u32[]{:S(2)}) collective-permute-start(bf16[336,128]{1,0:T(8,128)(2,1)S(1)} %shard_map.75.rest_0_), channel_id=1, source_target_pairs={{0,16},{8,24},{16,0},{24,8},{1,17},{9,25},{17,1},{25,9},{2,18},{10... | collective-permute-start | bytes 258056 | tf_op jit(solution)/shard_map/ppermute | solution.py:480
  46.2 6.3 %collective-permute-start.17 = (bf16[336,128]{1,0:T(8,128)(2,1)S(1)}, bf16[336,128]{1,0:T(8,128)(2,1)S(1)}, u32[]{:S(2)}, u32[]{:S(2)}) collective-permute-start(bf16[336,128]{1,0:T(8,128)(2,1)S(1)} %shard_map.75.rest_0_), channel_id=1, source_target_pairs={{0,8},{8,0},{16,24},{24,16},{1,9},{9,1},{17,25},{25,17},{2,10},{10... | collective-permute-start | bytes 258056 | tf_op jit(solution)/shard_map/ppermute | solution.py:480
  48.2 4.9 %collective-permute-start.13 = (bf16[2,128,128]{2,1,0:T(8,128)(2,1)S(1)}, bf16[2,128,128]{2,1,0:T(8,128)(2,1)S(1)}, u32[]{:S(2)}, u32[]{:S(2)}) collective-permute-start(bf16[2,128,128]{2,1,0:T(8,128)(2,1)S(1)} %collective-permute-done.9.rest_1_), channel_id=1, source_target_pairs={{0,1},{1,0},{2,3},{3,2},{4,5},{5,4},{6,7},{7,6},{8,9},{9,8},{10,11... | collective-permute-start | bytes 196616 | tf_op jit(solution)/shard_map/ppermute | solution.py:480
  48.2 5.0 %collective-permute-start.14 = (bf16[2,128,128]{2,1,0:T(8,128)(2,1)S(1)}, bf16[2,128,128]{2,1,0:T(8,128)(2,1)S(1)}, u32[]{:S(2)}, u32[]{:S(2)}) collective-permute-start(bf16[2,128,128]{2,1,0:T(8,128)(2,1)S(1)} %collective-permute-done.10.rest_2_), channel_id=1, source_target_pairs={{0,1},{1,0},{2,3},{3,2},{4,5},{5,4},{6,7},{7,6},{8,9},{9,8},{10,11... | collective-permute-start | bytes 196616 | tf_op jit(solution)/shard_map/ppermute | solution.py:480
  50.8 3.9 %collective-permute-start.20 = (bf16[336,128]{1,0:T(8,128)(2,1)S(1)}, bf16[336,128]{1,0:T(8,128)(2,1)S(1)}, u32[]{:S(2)}, u32[]{:S(2)}) collective-permute-start(bf16[336,128]{1,0:T(8,128)(2,1)S(1)} %shard_map.75.rest_0_), channel_id=1, source_target_pairs={{0,1},{1,0},{2,3},{3,2},{4,5},{5,4},{6,7},{7,6},{8,9},{9,8},{10,11... | collective-permute-start | bytes 258056 | tf_op jit(solution)/shard_map/ppermute | solution.py:480
  52.6 2.2 %collective-permute-start.23 = (bf16[336,128]{1,0:T(8,128)(2,1)S(1)}, bf16[336,128]{1,0:T(8,128)(2,1)S(1)}, u32[]{:S(2)}, u32[]{:S(2)}) collective-permute-start(bf16[336,128]{1,0:T(8,128)(2,1)S(1)} %collective-permute-done.19.rest_3_), channel_id=1, source_target_pairs={{0,1},{1,0},{2,3},{3,2},{4,5},{5,4},{6,7},{7,6},{8,9},{9,8},{10,11... | collective-permute-start | bytes 258056 | tf_op jit(solution)/shard_map/ppermute | solution.py:480
  52.6 2.2 %collective-permute-start.22 = (bf16[336,128]{1,0:T(8,128)(2,1)S(1)}, bf16[336,128]{1,0:T(8,128)(2,1)S(1)}, u32[]{:S(2)}, u32[]{:S(2)}) collective-permute-start(bf16[336,128]{1,0:T(8,128)(2,1)S(1)} %collective-permute-done.18.rest_2_), channel_id=1, source_target_pairs={{0,1},{1,0},{2,3},{3,2},{4,5},{5,4},{6,7},{7,6},{8,9},{9,8},{10,11... | collective-permute-start | bytes 258056 | tf_op jit(solution)/shard_map/ppermute | solution.py:480
  53.1 1.7 %collective-permute-start.21 = (bf16[336,128]{1,0:T(8,128)(2,1)S(1)}, bf16[336,128]{1,0:T(8,128)(2,1)S(1)}, u32[]{:S(2)}, u32[]{:S(2)}) collective-permute-start(bf16[336,128]{1,0:T(8,128)(2,1)S(1)} %collective-permute-done.17.rest_1_), channel_id=1, source_target_pairs={{0,1},{1,0},{2,3},{3,2},{4,5},{5,4},{6,7},{7,6},{8,9},{9,8},{10,11... | collective-permute-start | bytes 258056 | tf_op jit(solution)/shard_map/ppermute | solution.py:480
  53.2 1.3 %collective-permute-start.15 = (bf16[2,128,128]{2,1,0:T(8,128)(2,1)S(1)}, bf16[2,128,128]{2,1,0:T(8,128)(2,1)S(1)}, u32[]{:S(2)}, u32[]{:S(2)}) collective-permute-start(bf16[2,128,128]{2,1,0:T(8,128)(2,1)S(1)} %collective-permute-done.11.rest_3_), channel_id=1, source_target_pairs={{0,1},{1,0},{2,3},{3,2},{4,5},{5,4},{6,7},{7,6},{8,9},{9,8},{10,11... | collective-permute-start | bytes 196616 | tf_op jit(solution)/shard_map/ppermute | solution.py:480
  56.7 6.7 %collective-permute-start.24 = (bf16[32,1536]{1,0:T(8,128)(2,1)S(1)}, bf16[32,1536]{1,0:T(8,128)(2,1)S(1)}, u32[]{:S(2)}, u32[]{:S(2)}) collective-permute-start(bf16[32,1536]{1,0:T(8,128)(2,1)S(1)} %get-tuple-element.70), channel_id=1, source_target_pairs={{0,2},{2,0},{4,6},{6,4},{1,3},{3,1},{5,7},{7,5},{8,10},{10,8},{12,... | collective-permute-start | bytes 294920 | tf_op jit(solution)/shard_map/ppermute | solution.py:480
  58.1 7.1 %collective-permute-start.25 = (bf16[32,1536]{1,0:T(8,128)(2,1)S(1)}, bf16[32,1536]{1,0:T(8,128)(2,1)S(1)}, u32[]{:S(2)}, u32[]{:S(2)}) collective-permute-start(bf16[32,1536]{1,0:T(8,128)(2,1)S(1)} %get-tuple-element.71), channel_id=1, source_target_pairs={{0,4},{2,6},{4,0},{6,2},{1,5},{3,7},{5,1},{7,3},{8,12},{10,14},{12... | collective-permute-start | bytes 294920 | tf_op jit(solution)/shard_map/ppermute | solution.py:480
  59.2 6.6 %collective-permute-start.26 = (bf16[32,1536]{1,0:T(8,128)(2,1)S(1)}, bf16[32,1536]{1,0:T(8,128)(2,1)S(1)}, u32[]{:S(2)}, u32[]{:S(2)}) collective-permute-start(bf16[32,1536]{1,0:T(8,128)(2,1)S(1)} %get-tuple-element.72), channel_id=1, source_target_pairs={{0,6},{2,4},{4,2},{6,0},{1,7},{3,5},{5,3},{7,1},{8,14},{10,12},{12... | collective-permute-start | bytes 294920 | tf_op jit(solution)/shard_map/ppermute | solution.py:480
  60.9 6.3 %collective-permute-start.27 = (bf16[32,1536]{1,0:T(8,128)(2,1)S(1)}, bf16[32,1536]{1,0:T(8,128)(2,1)S(1)}, u32[]{:S(2)}, u32[]{:S(2)}) collective-permute-start(bf16[32,1536]{1,0:T(8,128)(2,1)S(1)} %get-tuple-element.78), channel_id=1, source_target_pairs={{0,2},{2,0},{4,6},{6,4},{1,3},{3,1},{5,7},{7,5},{8,10},{10,8},{12,... | collective-permute-start | bytes 294920 | tf_op jit(solution)/shard_map/ppermute | solution.py:480
  62.3 6.9 %collective-permute-start.28 = (bf16[32,1536]{1,0:T(8,128)(2,1)S(1)}, bf16[32,1536]{1,0:T(8,128)(2,1)S(1)}, u32[]{:S(2)}, u32[]{:S(2)}) collective-permute-start(bf16[32,1536]{1,0:T(8,128)(2,1)S(1)} %get-tuple-element.79), channel_id=1, source_target_pairs={{0,4},{2,6},{4,0},{6,2},{1,5},{3,7},{5,1},{7,3},{8,12},{10,14},{12... | collective-permute-start | bytes 294920 | tf_op jit(solution)/shard_map/ppermute | solution.py:480
  63.4 5.8 %collective-permute-start.29 = (bf16[32,1536]{1,0:T(8,128)(2,1)S(1)}, bf16[32,1536]{1,0:T(8,128)(2,1)S(1)}, u32[]{:S(2)}, u32[]{:S(2)}) collective-permute-start(bf16[32,1536]{1,0:T(8,128)(2,1)S(1)} %get-tuple-element.80), channel_id=1, source_target_pairs={{0,6},{2,4},{4,2},{6,0},{1,7},{3,5},{5,3},{7,1},{8,14},{10,12},{12... | collective-permute-start | bytes 294920 | tf_op jit(solution)/shard_map/ppermute | solution.py:480
